TPU v7x, 128 devices: a whole 4x4x4 slice. The times are simulated.
128 devices in a mesh: leaf: 8 (over y_lo, z), front: 16 (over y_hi, x, core).
Axes of the slice: x: 4, y: 4 (y_hi: 2, y_lo: 2; y = y_hi * 2 + y_lo), z: 4, core: 2. Of those that a mesh axis runs over, the one named last changes fastest.
Arguments:
- child_update: float32 [8, 4096, 4096], P('leaf', 'front'), may hold values from -6 to 6
- assembly: int32 [8, 32], replicated, may hold values from 0 to 127, as said below
- front_matrix: float32 [16384, 16384], P('leaf', 'front'), may hold values from -6 to 6
- block_inv: float32 [2, 128, 128], replicated, as said below
Outputs:
- factored: float32 [16384, 16384], P('leaf', 'front')
Inputs may be any that keep to these rules, and one draw needn't show every extreme that they name: `assembly`: each row lists 32 distinct parent block indices in increasing order. Of one row's entries, at most 4 lie among the parent blocks whose columns one index of the front axis holds; in every row, all such groups that make up the rows of one index of the leaf axis hold exactly 4 each. `block_inv`: each block is lower triangular with a nonzero diagonal.
All inputs are finite; a program needn't handle non-finite values.
Results may differ from a plain program's by a relative error of at most 0.0001.
Values sent between devices are 32-bit elements; how exact they have to be, the bound alone decides.
No kernel may reach another device: no remote copies, remote signals or barrier semaphores. Data moves between devices by JAX's collectives and lax.ppermute only.
A program may use at most 192 MiB of HBM per device.

v0:
```python
import jax
import jax.numpy as jnp
from jax import lax
from jax.sharding import PartitionSpec as P

BLK = 128
NPAN = 2
CAPF = 4


def broadcast(x, axis, root):
    mine = lax.axis_index(axis) == root
    return lax.psum(jnp.where(mine, x, jnp.zeros_like(x)), axis)


def rank_within(owners):
    length = owners.shape[-1]
    earlier = lax.broadcasted_iota(jnp.int32, (length, length), 1) < lax.broadcasted_iota(
        jnp.int32, (length, length), 0
    )
    matches = owners[..., :, None] == owners[..., None, :]
    return jnp.sum(jnp.where(matches & earlier, 1, 0), axis=-1).astype(jnp.int32)


def one_hot(values, classes):
    return (values[..., None] == jnp.arange(classes, dtype=jnp.int32)).astype(jnp.float32)


def per_device(child_update, assembly, front_matrix, block_inv):
    highest = lax.Precision.HIGHEST
    n_front = lax.axis_size("front")
    n_leaf = lax.axis_size("leaf")
    row_count, col_count = front_matrix.shape
    child_blocks = assembly.shape[1]
    col_blocks = col_count // BLK
    row_blocks = row_count // BLK
    leaf_slots = CAPF * n_front // n_leaf
    leaf_index = lax.axis_index("leaf")
    front_index = lax.axis_index("front")
    col_owner = assembly // col_blocks
    row_owner = assembly // row_blocks
    col_rank = rank_within(col_owner)
    row_rank = rank_within(row_owner)
    own_col_slot = lax.dynamic_index_in_dim(
        col_owner * CAPF + col_rank, leaf_index, 0, keepdims=False
    )
    select_cols = one_hot(own_col_slot, n_front * CAPF)
    child_rows = child_update[0]
    local_rows = child_rows.shape[0]
    blocked = child_rows.reshape(local_rows, child_blocks, BLK)
    packed = jnp.einsum("rjb,js->srb", blocked, select_cols, precision=highest)
    packed = packed.reshape(n_front, CAPF, local_rows, BLK)
    received = lax.all_to_all(packed, "front", split_axis=0, concat_axis=2, tiled=True)[0]
    own_row_slot = lax.dynamic_index_in_dim(
        row_owner * leaf_slots + row_rank, leaf_index, 0, keepdims=False
    )
    select_rows = one_hot(own_row_slot, n_leaf * leaf_slots)
    slot_grid = received.reshape(CAPF, child_blocks, BLK, BLK)
    routed = jnp.einsum("cirb,it->trcb", slot_grid, select_rows, precision=highest)
    routed = routed.reshape(n_leaf, leaf_slots * BLK, CAPF * BLK)
    arrived = lax.all_to_all(routed, "leaf", split_axis=0, concat_axis=0, tiled=True)
    arrived = arrived.reshape(n_leaf, leaf_slots, BLK, CAPF, BLK)
    col_mask = (col_owner == front_index).astype(jnp.float32)
    col_source = one_hot(col_rank, CAPF) * col_mask[..., None]
    col_target = one_hot(assembly - front_index * col_blocks, col_blocks)
    col_select = jnp.einsum("giq,giv->gqv", col_source, col_target, precision=highest)
    row_mask = (row_owner == leaf_index).astype(jnp.float32)
    row_source = one_hot(row_rank, leaf_slots) * row_mask[..., None]
    row_target = one_hot(assembly - leaf_index * row_blocks, row_blocks)
    row_select = jnp.einsum("gip,giu->gpu", row_source, row_target, precision=highest)
    widened = jnp.einsum("gpaqb,gqv->gpavb", arrived, col_select, precision=highest)
    placed = jnp.einsum("gpavb,gpu->uavb", widened, row_select, precision=highest)
    local_tile = front_matrix + placed.reshape(row_count, col_count)
    row_global = leaf_index * row_count + lax.iota(jnp.int32, row_count)
    offset = front_index * col_count % row_count
    root_leaf = front_index * col_count // row_count
    panel_width = NPAN * BLK
    pieces = []
    for panel_step in range(NPAN):
        columns = local_tile[:, panel_step * BLK : (panel_step + 1) * BLK]
        factor = jnp.einsum("rk,ck->rc", columns, block_inv[panel_step], precision=highest)
        factor = jnp.where((row_global >= panel_step * BLK)[:, None], factor, 0.0)
        factor = broadcast(factor, "front", 0)
        column_part = broadcast(
            lax.dynamic_slice_in_dim(factor, offset, col_count, 0), "leaf", root_leaf
        )
        local_tile = local_tile - jnp.einsum("rk,ck->rc", factor, column_part, precision=highest)
        pieces.append(factor)
    factors = jnp.concatenate(pieces, axis=1)
    replaced = jnp.concatenate([factors, local_tile[:, panel_width:]], axis=1)
    return jnp.where(front_index == 0, replaced, local_tile)


def solution(mesh):
    placed = (P("leaf", "front", None), P(), P("leaf", "front"), P())
    return jax.shard_map(
        per_device, mesh=mesh, in_specs=placed, out_specs=P("leaf", "front"), check_vma=False
    )
```

profile of v0, /device:TPU:0, one launch (start us, length us, event | category | flops | bytes accessed | tf_op | source)
XLA Modules:
  0.0 1033.7 jit_solution(4206115243931974999)
XLA Ops:
  7.3 5.0 copy.52
  12.8 5.4 fusion.16
  18.2 6.0 copy.31
  24.2 7.7 all-to-all-start
  31.9 113.0 %all-to-all-done = f32[16,4,256,128]{3,2,1,0:T(8,128)} async-done(((f32[16,4,256,128]{3,2,1,0:T(8,128)}), f32[16,4,256,128]{3,2,1,0:T(8,128)}, u32[]{:S(2)}, u32[]{:S(2)}) %all-to-all-start) | async-done | bytes 8388640 | tf_op jit(solution)/shard_map/all_to_all | solution.py:53
  144.9 3.9 copy.32
  148.8 17.1 %convolution_bitcast_fusion.1 = f32[64,128,4,128]{3,0,1,2:T(8,128)} fusion(f32[4,32,128,128]{3,2,1,0:T(8,128)S(1)} %bitcast.70, s32[32]{0:T(128)S(1)} %fusion.38), kind=kOutput, calls=%fused_computation.3 | convolution fusion | flops 1610614784 | bytes 25165952 | tf_op jit(solution)/shard_map/cirb,it->trcb/dot_general | solution.py:59
  165.9 16.6 %copy.34 = f32[64,128,4,128]{1,0,3,2:T(8,128)} copy(f32[64,128,4,128]{3,0,1,2:T(8,128)} %convolution_bitcast_fusion.1) | data formatting | bytes 33554432 | tf_op jit(solution)/shard_map/cirb,it->trcb/transpose | solution.py:59
  182.5 18.0 %reshape.58 = f32[8,1024,512]{1,0,2:T(8,128)} reshape(f32[64,128,4,128]{1,0,3,2:T(8,128)} %copy.34) | data formatting | bytes 33554432 | tf_op jit(solution)/shard_map/reshape | solution.py:60
  200.5 17.7 %copy.35 = f32[8,1024,512]{1,2,0:T(8,128)} copy(f32[8,1024,512]{1,0,2:T(8,128)} %reshape.58) | data formatting | bytes 33554432 | tf_op jit(solution)/shard_map/reshape | solution.py:60
  218.1 5.8 all-to-all-start.1
  224.1 9.1 copy.39
  233.6 174.9 %all-to-all-done.1 = f32[8,1024,512]{1,2,0:T(8,128)} async-done(((f32[8,1024,512]{1,2,0:T(8,128)}), f32[8,1024,512]{1,2,0:T(8,128)}, u32[]{:S(2)}, u32[]{:S(2)}) %all-to-all-start.1) | async-done | bytes 16777248 | tf_op jit(solution)/shard_map/all_to_all | solution.py:61
  408.5 14.1 %copy.53 = f32[512,8,8,128]{3,2,1,0:T(8,128)} copy(f32[512,8,8,128]{3,1,2,0:T(8,128)} %bitcast.34) | data formatting | bytes 33554432
  422.6 15.3 %copy.49 = f32[8,8,128,4,128]{4,3,2,1,0:T(4,128)} copy(f32[8,8,128,4,128]{2,1,4,3,0:T(8,128)} %bitcast.69) | data formatting | bytes 33554432 | tf_op jit(solution)/shard_map/reshape | solution.py:62
  437.9 39.0 %convolution_bitcast_fusion = f32[8,8,128,8,128]{4,3,2,1,0:T(8,128)} fusion(f32[8,4,8,1,1]{2,1,4,3,0:T(4,128)S(1)} %convolution_bitcast_fusion.3, f32[8,8,128,4,128]{4,3,2,1,0:T(4,128)} %copy.49), kind=kOutput, calls=%fused_computation.2 | convolution fusion | flops 402653184 | bytes 50332672 | tf_op jit(solution)/shard_map/gpaqb,gqv->gpavb/dot_general | solution.py:71
  476.9 45.1 %fusion.3 = f32[16,128,8,128]{3,0,2,1:T(8,128)} fusion(f32[8,8,16,1,1]{2,1,0,4,3:T(8,128)S(1)} %convolution_bitcast_fusion.2, f32[8,8,128,8,128]{4,3,2,1,0:T(8,128)} %convolution_bitcast_fusion), kind=kOutput, calls=%fused_computation.9 | convolution fusion | flops 1610612736 | bytes 41947136 | tf_op jit(solution)/shard_map/gpavb,gpu->uavb/dot_general | solution.py:72
  522.0 9.7 copy.50
  531.7 13.9 %bitcast_add_fusion = f32[2048,1024]{0,1:T(8,128)} fusion(f32[2048,1024]{0,1:T(8,128)} %copy.39, f32[128,8,16,128]{3,2,1,0:T(8,128)} %bitcast.71), kind=kLoop, calls=%fused_computation.4 | loop fusion | flops 2097152 | bytes 25165824 | tf_op jit(solution)/shard_map/add | solution.py:73
  545.6 4.2 fusion.7
  549.9 139.2 %all-reduce.5.cloned.1.call-done = f32[2048,128]{1,0:T(8,128)} async-done(((f32[2048,128]{1,0:T(8,128)}), f32[2048,128]{1,0:T(8,128)}) %all-reduce.5.cloned.1.call-update) | async-done | bytes 1048592 | tf_op jit(solution)/shard_map/psum | solution.py:13
  689.1 1.9 dynamic-slice_select_fusion.1
  691.1 76.8 %all-reduce.7.cloned.1.call-done = f32[1024,128]{1,0:T(8,128)} async-done(((f32[1024,128]{1,0:T(8,128)}), f32[1024,128]{1,0:T(8,128)}) %all-reduce.7.cloned.1.call-update) | async-done | bytes 524304 | tf_op jit(solution)/shard_map/psum | solution.py:13
  767.9 9.7 convolution_subtract_fusion.1
  777.6 3.4 copy-done
  781.0 2.9 fusion.6
  784.2 139.8 %all-reduce.9.cloned.1.call-done = f32[2048,128]{1,0:T(8,128)} async-done(((f32[2048,128]{1,0:T(8,128)}), f32[2048,128]{1,0:T(8,128)}) %all-reduce.9.cloned.1.call-update) | async-done | bytes 1048592 | tf_op jit(solution)/shard_map/psum | solution.py:13
  924.0 1.9 dynamic-slice_select_fusion
  927.8 74.8 %all-reduce.11.cloned.1.call-done = f32[1024,128]{1,0:T(8,128)} async-done(((f32[1024,128]{1,0:T(8,128)}), f32[1024,128]{1,0:T(8,128)}) %all-reduce.11.cloned.1.call-update) | async-done | bytes 524304 | tf_op jit(solution)/shard_map/psum | solution.py:13
  1002.6 9.9 convolution_subtract_fusion
  1013.4 4.4 maximum_select_fusion
  1017.7 9.2 copy.43
  (30 shorter events, 4.9 us)
Async XLA Ops:
  6.5 6.2 copy-start.3
  24.2 120.7 %all-to-all-start = ((f32[16,4,256,128]{3,2,1,0:T(8,128)}), f32[16,4,256,128]{3,2,1,0:T(8,128)}, u32[]{:S(2)}, u32[]{:S(2)}) async-start(f32[16,4,256,128]{3,2,1,0:T(8,128)} %copy.31), calls=%async_computation | async-start | bytes 16777216 | tf_op jit(solution)/shard_map/all_to_all | solution.py:53
  218.1 190.3 %all-to-all-start.1 = ((f32[8,1024,512]{1,2,0:T(8,128)}), f32[8,1024,512]{1,2,0:T(8,128)}, u32[]{:S(2)}, u32[]{:S(2)}) async-start(f32[8,1024,512]{1,2,0:T(8,128)} %copy.35), calls=%async_computation.1 | async-start | bytes 33554432 | tf_op jit(solution)/shard_map/all_to_all | solution.py:61
  223.9 465.2 %all-reduce.5.cloned.1.call-start = ((), (), s32[]{:S(2)}) async-start(), calls=%async_computation.2 | async-start | bytes 2097152 | tf_op jit(solution)/shard_map/psum | solution.py:13
  531.7 13.9 %copy-start.2 = (f32[2,128,128]{2,1,0:T(8,128)S(1)}, f32[2,128,128]{2,1,0:T(8,128)}, u32[]{:S(2)}) copy-start(f32[2,128,128]{2,1,0:T(8,128)} %param.7) | copy-start | bytes 393220
  549.9 218.1 %all-reduce.7.cloned.1.call-start = ((), (), s32[]{:S(2)}) async-start(), calls=%async_computation.3 | async-start | bytes 1048576 | tf_op jit(solution)/shard_map/psum | solution.py:13
  691.1 233.0 %all-reduce.9.cloned.1.call-start = ((), (), s32[]{:S(2)}) async-start(), calls=%async_computation.4 | async-start | bytes 2097152 | tf_op jit(solution)/shard_map/psum | solution.py:13
  691.1 234.8 %copy-start.1 = (f32[2048,128]{1,0:T(8,128)S(1)}, f32[2048,128]{1,0:T(8,128)}, u32[]{:S(2)}) copy-start(f32[2048,128]{1,0:T(8,128)} %all-reduce.5.cloned.1.call-done) | copy-start | bytes 3145732
  777.6 3.4 copy-start
  784.0 218.7 %all-reduce.11.cloned.1.call-start = ((), (), s32[]{:S(2)}) async-start(), calls=%async_computation.5 | async-start | bytes 1048576 | tf_op jit(solution)/shard_map/psum | solution.py:13
Sparse Core Ops, SparseCore 0:
  550.0 139.1 all-reduce.4
  691.8 76.1 all-reduce.6
  784.1 139.8 all-reduce.8
  926.5 76.0 all-reduce.10
where the time goes:
time: 1040 us; the launch traced here: 1030 us
  waiting for transfers between devices  719 us (69%)
  matrix products  134 us (13%)
  local copies, waits for them, and re-layouts  131 us (13%)
  other arithmetic  23.3 us (2%)
  starting transfers between devices  14 us (1%)
  between operations  13.5 us (1%)
    psum x4, waiting for transfers between devices, broadcast(): return lax.psum(jnp.where(mine, x, jnp.zeros_like(x)), axis)  431 us
    all_to_all x1, waiting for transfers between devices, per_device(): lax.all_to_all(routed, 'leaf', split_axis=0, concat_axis=0, tiled=True)  175 us
    all_to_all x1, waiting for transfers between devices, per_device(): lax.all_to_all(packed, 'front', split_axis=0, concat_axis=2, tiled=True)[0]  113 us
    dot_general x1, matrix products, per_device(): jnp.einsum('gpavb,gpu->uavb', widened, row_select, precision=highest)  45.1 us
    dot_general x1, matrix products, per_device(): jnp.einsum('gpaqb,gqv->gpavb', arrived, col_select, precision=highest)  39 us
    reshape x2, local copies, waits for them, and re-layouts, per_device(): routed = routed.reshape(n_leaf, leaf_slots * BLK, CAPF * BLK)  35.7 us
    unnamed x11, local copies, waits for them, and re-layouts  31.6 us
  transfers between devices with their start and end apart: 6, of which 6 were waited for; matrix products, arithmetic and copies ran while one was open for 1% of the time, Pallas kernels for 0%

commit v1 on v0

v1 whole, which is shorter than its diff:
```python
import functools

import jax
import jax.numpy as jnp
from jax import lax
from jax.experimental import pallas as pl
from jax.experimental.pallas import tpu as pltpu
from jax.sharding import PartitionSpec as P

BLK = 128
CAPF = 4
UB = 32
CHUNKS = tuple((c, 0, 128) for c in range(CAPF))

T_R, T_RANK, T_M, T_ROWU, T_PROW, T_VCOL, T_ALL = 128, 384, 640, 768, 832, 960, 1024

HBM = pl.BlockSpec(memory_space=pltpu.HBM)
SMEM = pl.BlockSpec(memory_space=pltpu.SMEM)
COST = pl.CostEstimate(flops=1000, bytes_accessed=1 << 20, transcendentals=0)


def leaf_at(y_lo, z):
    return y_lo % 2 * 4 + z % 4


def front_at(y_hi, x, core):
    return y_hi % 2 * 8 + x % 4 * 2 + core % 2


def device_at(leaf, front):
    return leaf * 16 + front


def copy(src, dst, sem):
    return pltpu.make_async_copy(src, dst, sem)


def call(body, operands, outs, name):
    n = len(outs)

    def kernel(*refs):
        ins, results, held, sem = refs[:-n - 2], refs[-n - 2:-2], refs[-2], refs[-1]
        body(ins, held, sem)
        writes = [copy(held.at[k], results[k], sem) for k in range(n)]
        for w in writes:
            w.start()
        for w in writes:
            w.wait()

    return pl.pallas_call(
        kernel,
        out_shape=[jax.ShapeDtypeStruct(s, jnp.float32) for s in outs],
        in_specs=[SMEM] + [HBM] * (len(operands) - 1),
        out_specs=[HBM] * n,
        scratch_shapes=[pltpu.VMEM((n,) + outs[0], jnp.float32), pltpu.SemaphoreType.DMA(())],
        compiler_params=pltpu.CompilerParams(vmem_limit_bytes=12 << 20),
        cost_estimate=COST,
        name=name,
    )(*operands)


def own_columns(meta, act):
    def column(j, carry):
        before, rank = carry
        owner = meta[j] >> 3
        rank = jnp.where(owner == before, rank + 1, 0)
        act(j, owner, rank)
        return owner, rank

    lax.fori_loop(0, UB, column, (jnp.int32(-1), jnp.int32(0)))


def pack_core(c, meta, child, after):
    def body(ins, held, sem):
        meta, child = ins[:2]
        core = meta[UB + 1] & 1
        for wait in (False, True):
            def act(j, owner, rank, wait=wait):
                @pl.when((rank == c) & ((owner & 1) != core))
                def _():
                    columns = pl.ds(pl.multiple_of(j * BLK, BLK), BLK)
                    one = copy(child.at[:, :, columns], held.at[0, owner >> 1], sem)
                    one.wait() if wait else one.start()

            own_columns(meta, act)

    return call(body, [meta, child] + after, [(8, 2, BLK, BLK)], "pack_core")


def pack_x(chunk, meta, child, crossed, after):
    c, off, rows = chunk

    def body(ins, held, sem):
        meta, child, crossed = ins[:3]
        front = meta[UB + 1]
        x, core = (front >> 1) & 3, front & 1
        part = pl.ds(off, rows)
        for wait in (False, True):
            def act(j, owner, rank, wait=wait):
                @pl.when((rank == c) & ((owner & 1) == core))
                def _():
                    target = ((owner >> 1) - x) & 3
                    columns = pl.ds(pl.multiple_of(j * BLK, BLK), BLK)
                    one = copy(child.at[:, part, columns], held.at[target, owner >> 3, 0], sem)
                    two = copy(crossed.at[owner >> 1, :, part], held.at[target, owner >> 3, 1], sem)
                    for d in (one, two):
                        d.wait() if wait else d.start()

            own_columns(meta, act)

    return call(body, [meta, child, crossed] + after, [(2, 2, 2, rows, BLK)] * 4, "pack_x")


def pack_y(chunk, tab, arrays, after):
    c, _, rows = chunk

    def body(ins, held, sem):
        tab, arrays = ins[0], ins[1:5]
        leaf, front = tab[0], tab[1]
        y_hi, x, core = front >> 3, (front >> 1) & 3, front & 1
        y = y_hi * 2 + (leaf >> 2)
        for wait in (False, True):
            for to_hi in range(2):
                @pl.when(tab[T_M + leaf * 16 + to_hi * 8 + (front & 7)] > c)
                def _():
                    for k in range(4):
                        def one(n, carry):
                            other, r = n >> 1, n & 1
                            slot = (((x - k) & 3) * 2 + (core ^ other)) * 2 + r
                            owner = tab[T_R + leaf * UB + y_hi * 16 + slot]
                            target = (to_hi * 2 + (owner >> 2) - y) & 3
                            d = copy(arrays[k].at[to_hi, other, r], held.at[target, slot], sem)
                            d.wait() if wait else d.start()
                            return carry

                        lax.fori_loop(0, 4, one, 0)

    return call(body, [tab] + arrays + after, [(16, rows, BLK)] * 4, "pack_y")


def pack_z(chunk, tab, arrays, after):
    c, _, rows = chunk

    def body(ins, held, sem):
        tab, arrays = ins[0], ins[1:5]
        leaf, front = tab[0], tab[1]
        z, y_lo = leaf & 3, leaf >> 2
        y = (front >> 3) * 2 + y_lo
        for wait in (False, True):
            for k in range(4):
                source = (y - k) & 3
                from_lo = source & 1
                group = from_lo * 4 + z

                @pl.when(tab[T_M + group * 16 + front] > c)
                def _():
                    def one(s, carry):
                        i = group * UB + (source >> 1) * 16 + s
                        owner = tab[T_R + i]

                        @pl.when((owner >> 2) == y_lo)
                        def _():
                            d = copy(arrays[k].at[s], held.at[(owner - z) & 3, from_lo, tab[T_RANK + i]], sem)
                            d.wait() if wait else d.start()

                        return carry

                    lax.fori_loop(0, 16, one, 0)

    return call(body, [tab] + arrays + after, [(2, 8, rows, BLK)] * 4, "pack_z")


def panel_sum(chunks, tab, front_tile, arrays):
    n_arrays = 4 * len(chunks)

    def kernel(tab, tile, *refs):
        arrays, outs, (total, held, sem) = refs[:n_arrays], refs[n_arrays:-3], refs[-3:]
        z = tab[0] & 3

        def each(act):
            for n, (c, off, rows) in enumerate(chunks):
                for k in range(4):
                    for lo in range(2):
                        group = lo * 4 + ((z - k) & 3)
                        v = tab[T_VCOL + group * 4 + c]

                        @pl.when((v >= 0) & (v < 2))
                        def _():
                            def one(p, carry):
                                u = tab[T_ROWU + group * 8 + p]

                                @pl.when(u >= 0)
                                def _():
                                    act(arrays[n * 4 + k].at[lo, p], held.at[c, k * 2 + lo, p, pl.ds(off, rows)], u, v, off, rows)

                                return carry

                            lax.fori_loop(0, 8, one, 0)

        @pl.when(tab[1] == 0)
        def _():
            whole = copy(tile.at[:, pl.ds(0, 2 * BLK)], total, sem)
            whole.start()
            each(lambda src, dst, *_: copy(src, dst, sem).start())
            whole.wait()
            each(lambda src, dst, *_: copy(src, dst, sem).wait())

            def add(src, dst, u, v, off, rows):
                at = (pl.ds(pl.multiple_of(u * BLK + off, 64), rows), pl.ds(pl.multiple_of(v * BLK, BLK), BLK))
                total[at] += dst[...]

            each(add)
            out = [copy(total.at[pl.ds(q * 512, 512)], outs[q], sem) for q in range(4)]
            out.append(copy(total.at[pl.ds(BLK, BLK), pl.ds(0, BLK)], outs[4], sem))
            for o in out:
                o.start()
            for o in out:
                o.wait()

    return pl.pallas_call(
        kernel,
        out_shape=[jax.ShapeDtypeStruct((512, 2 * BLK), jnp.float32)] * 4 + [jax.ShapeDtypeStruct((BLK, BLK), jnp.float32)],
        in_specs=[SMEM] + [HBM] * (n_arrays + 1),
        out_specs=[HBM] * 5,
        scratch_shapes=[
            pltpu.VMEM((2048, 2 * BLK), jnp.float32),
            pltpu.VMEM((2, 8, 8, BLK, BLK), jnp.float32),
            pltpu.SemaphoreType.DMA(()),
        ],
        compiler_params=pltpu.CompilerParams(vmem_limit_bytes=24 << 20),
        cost_estimate=COST,
        name="panel_sum",
    )(tab, front_tile, *arrays)


def column_rows(tab, quarters):
    def body(ins, held, sem):
        tab, quarters = ins[0], ins[1:5]
        front = tab[1]
        x, core = (front >> 1) & 3, front & 1
        for wait in (False, True):
            for n in range(4):
                at = (x - core * 2 - n // 2) & 3
                for k in range(4):
                    @pl.when(at == k)
                    def _():
                        d = copy(quarters[k].at[pl.ds(n % 2 * 256, 256)], held.at[n], sem)
                        d.wait() if wait else d.start()

    return call(body, [tab] + quarters, [(256, 2 * BLK)] * 4, "column_rows")


def product(a, b, precision=lax.Precision.HIGHEST):
    return lax.dot_general(a, b, (((1,), (1,)), ((), ())), precision=precision, preferred_element_type=jnp.float32)


def final(tab, front_tile, block_inv, corner, arrays, quarters, pieces):
    n_arrays = 4 * len(CHUNKS)
    steps = front_tile.shape[0] // BLK
    width = front_tile.shape[1]

    def kernel(tab, tile, inv, corner, *refs):
        arrays, quarters, pieces = refs[:n_arrays], refs[n_arrays:n_arrays + 4], refs[n_arrays + 4:n_arrays + 8]
        out, held, rows_in, columns_in, right, sems, column_sem = refs[n_arrays + 8:]
        u = pl.program_id(0)
        leaf, front = tab[0], tab[1]
        z, x = leaf & 3, (front >> 1) & 3

        def each(step, act):
            for k in range(4):
                for lo in range(2):
                    group = lo * 4 + ((z - k) & 3)
                    p = tab[T_PROW + group * 16 + step]

                    @pl.when(p >= 0)
                    def _():
                        for c in range(CAPF):
                            v = tab[T_VCOL + group * 4 + c]

                            @pl.when(v >= 0)
                            def _():
                                act(k, lo, p, c, v)

        def fetch(step, wait):
            slot = step & 1
            sem = sems.at[slot]

            def act(k, lo, p, c, v):
                for n, (cc, off, rows) in enumerate(CHUNKS):
                    if cc == c:
                        one = copy(arrays[n * 4 + k].at[lo, p], held.at[slot, k * 2 + lo, c, pl.ds(off, rows)], sem)
                        one.wait() if wait else one.start()

            each(step, act)
            at = (x - (step >> 2)) & 3
            for k in range(4):
                @pl.when(at == k)
                def _():
                    one = copy(
                        quarters[k].at[pl.ds(pl.multiple_of((step & 3) * BLK, BLK), BLK)], rows_in.at[slot], sem
                    )
                    one.wait() if wait else one.start()

        def panels(raw, first):
            left = product(raw[:, :BLK], inv[0])
            below = product(corner[...], inv[0])
            second = product(raw[:, BLK:] - product(left, below), inv[1])
            return left, jnp.where(first, 0.0, second)

        @pl.when(u == 0)
        def _():
            fetch(0, False)
            for wait in (False, True):
                for k in range(4):
                    n = (z - k - (front >> 1)) & 3
                    one = copy(pieces[k], columns_in.at[pl.ds(pl.multiple_of(n * 256, 256), 256)], column_sem)
                    one.wait() if wait else one.start()
            for n in range(width // BLK):
                rows = pl.ds(n * BLK, BLK)
                left, second = panels(columns_in[rows], (front == 0) & (n == 0))
                for h, part in enumerate((left, second)):
                    high = part.astype(jnp.bfloat16)
                    low = (part - high.astype(jnp.float32)).astype(jnp.bfloat16)
                    for m, value in enumerate((high, high, low)):
                        right[rows, pl.ds((m * 2 + h) * BLK, BLK)] = value

        @pl.when(u + 1 < steps)
        def _():
            fetch(u + 1, False)

        fetch(u, True)
        slot = u & 1
        left, second = panels(rows_in[slot], (leaf == 0) & (u == 0))
        high, low = [], []
        for part in (left, second):
            high.append(part.astype(jnp.bfloat16))
            low.append((part - high[-1].astype(jnp.float32)).astype(jnp.bfloat16))
        split = jnp.concatenate(high + low + high, axis=1)
        out[...] = tile[...] - product(split, right[...], None)

        def add(k, lo, p, c, v):
            columns = pl.ds(pl.multiple_of(v * BLK, BLK), BLK)
            out[:, columns] += held[slot, k * 2 + lo, c]

        each(u, add)

        @pl.when(front == 0)
        def _():
            out[:, pl.ds(0, BLK)] = left
            out[:, pl.ds(BLK, BLK)] = second

    return pl.pallas_call(
        kernel,
        out_shape=jax.ShapeDtypeStruct(front_tile.shape, jnp.float32),
        grid=(steps,),
        in_specs=[
            SMEM,
            pl.BlockSpec((BLK, width), lambda u: (u, 0)),
            pl.BlockSpec((2, BLK, BLK), lambda u: (0, 0, 0)),
            pl.BlockSpec((BLK, BLK), lambda u: (0, 0)),
        ] + [HBM] * (n_arrays + 8),
        out_specs=pl.BlockSpec((BLK, width), lambda u: (u, 0)),
        scratch_shapes=[
            pltpu.VMEM((2, 8, CAPF, BLK, BLK), jnp.float32),
            pltpu.VMEM((2, BLK, 2 * BLK), jnp.float32),
            pltpu.VMEM((width, 2 * BLK), jnp.float32),
            pltpu.VMEM((width, 6 * BLK), jnp.bfloat16),
            pltpu.SemaphoreType.DMA((2,)),
            pltpu.SemaphoreType.DMA(()),
        ],
        compiler_params=pltpu.CompilerParams(vmem_limit_bytes=32 << 20),
        cost_estimate=COST,
        name="final",
    )(tab, front_tile, block_inv, corner, *arrays, *quarters, *pieces)


def shift_x(a, dx, dc):
    pairs = [
        (front_at(h, x, c), front_at(h, x + dx, c + dc)) for h in range(2) for x in range(4) for c in range(2)
    ]
    return lax.ppermute(a, "front", pairs)


def shift_y(a, dy):
    pairs = []
    for y in range(4):
        to = (y + dy) % 4
        for z in range(4):
            for x in range(4):
                for c in range(2):
                    pairs.append((
                        device_at(leaf_at(y, z), front_at(y // 2, x, c)),
                        device_at(leaf_at(to, z), front_at(to // 2, x, c)),
                    ))
    return lax.ppermute(a, ("leaf", "front"), pairs)


def shift_z(a, dz):
    return lax.ppermute(a, "leaf", [(leaf_at(l, z), leaf_at(l, z + dz)) for l in range(2) for z in range(4)])


def spread(a, steps, axis):
    for step in steps:
        a = functools.reduce(jnp.add, [lax.ppermute(a, axis, pairs) for pairs in step], a)
    return a


def tables(assembly, leaf, front):
    col_owner, row_owner = assembly >> 3, assembly >> 4
    earlier = jnp.arange(UB)[:, None] > jnp.arange(UB)[None, :]

    def rank(owner):
        same = (owner[:, :, None] == owner[:, None, :]) & earlier[None]
        return jnp.sum(same.astype(jnp.int32), axis=2)

    def pick(match, value):
        return jnp.sum(jnp.where(match, value + 1, 0), axis=1).astype(jnp.int32) - 1

    row_rank, col_rank = rank(row_owner), rank(col_owner)
    count = jnp.sum((col_owner[:, :, None] == jnp.arange(16)).astype(jnp.int32), axis=1)
    mine = row_owner == leaf
    row_u = pick(
        mine[:, :, None] & (row_rank[:, :, None] == jnp.arange(8)), (assembly & 15)[:, :, None]
    )
    row_p = pick(assembly[:, :, None] == leaf * 16 + jnp.arange(16), row_rank[:, :, None])
    col_v = pick(
        (col_owner == front)[:, :, None] & (col_rank[:, :, None] == jnp.arange(CAPF)), (assembly & 7)[:, :, None]
    )
    head = jnp.concatenate([leaf[None], front[None], jnp.zeros((T_R - 2,), jnp.int32)])
    parts = [head] + [t.reshape(-1) for t in (row_owner, row_rank, count, row_u, row_p, col_v)]
    size = sum(t.shape[0] for t in parts)
    return jnp.concatenate(parts + [jnp.zeros((T_ALL - size,), jnp.int32)])


def per_device(child_update, assembly, front_matrix, block_inv):
    leaf, front = lax.axis_index("leaf"), lax.axis_index("front")
    child = child_update.reshape(2, BLK, child_update.shape[2])
    own = lax.dynamic_index_in_dim(assembly, leaf, 0, keepdims=False)
    meta = jnp.concatenate([own, leaf[None], front[None], jnp.zeros((94,), jnp.int32)])
    tab = tables(assembly, leaf, front)

    n = len(CHUNKS)
    panel_chunks = [s for s in range(n) if CHUNKS[s][0] < 2]
    x_in, y_in, z_in = [None] * n, [None] * n, [None] * n
    after_x, after_y, after_z = [], [], []

    crossed = [None] * CAPF

    def do_x(s):
        c = CHUNKS[s][0]
        if crossed[c] is None:
            mine = pack_core(c, meta, child, after_x)[0]
            crossed[c] = shift_x(mine, 0, 1)
        outs = pack_x(CHUNKS[s], meta, child, crossed[c], after_x)
        x_in[s] = [outs[0]] + [shift_x(outs[k], k, 0) for k in range(1, 4)]
        return outs

    def do_y(s, after):
        outs = pack_y(CHUNKS[s], tab, x_in[s], after)
        y_in[s] = [outs[0]] + [shift_y(outs[k], k) for k in range(1, 4)]
        return outs

    def do_z(s, after):
        outs = pack_z(CHUNKS[s], tab, y_in[s], after)
        z_in[s] = [outs[0]] + [shift_z(outs[k], k) for k in range(1, 4)]
        return outs

    do_x(0)
    last_z = []
    for s in range(n + 1):
        if s < n:
            y_out = do_y(s, list(last_z[:1]))
            after_x = [y_out[0]]
            if s + 1 < n:
                do_x(s + 1)
        if s >= 1:
            last_z = do_z(s - 1, [y_out[0]])

    sums = panel_sum(
        [CHUNKS[s] for s in panel_chunks], tab, front_matrix, [a for s in panel_chunks for a in z_in[s]]
    )
    sums = [jnp.where(front == 0, a, 0.0) for a in sums]
    both = ("leaf", "front")
    root = front_at(0, 0, 0)
    quarter = sums[0]
    for x in range(1, 4):
        quarter = quarter + lax.ppermute(sums[x], "front", [(root, front_at(0, x, 0))])
    quarter = spread(
        quarter,
        [[[(front_at(0, x, 0), front_at(h, x, c)) for x in range(4)] for h, c in ((0, 1), (1, 0), (1, 1))]],
        "front",
    )
    quarters = [quarter] + [shift_x(quarter, dx, 0) for dx in range(1, 4)]
    roots = [(f // 2, f) for f in range(16)]
    pieces = column_rows(tab, quarters)
    at_root = leaf == front >> 1
    piece = jnp.where(at_root, pieces[0], 0.0)
    for dz in range(1, 4):
        pairs = [(device_at(l, f), device_at(leaf_at(l // 4, l + dz), f)) for l, f in roots]
        piece = piece + lax.ppermute(pieces[dz], both, pairs)
    piece = spread(
        piece,
        [[[
            (device_at(leaf_at(l // 4, z), f), device_at(leaf_at(1 - l // 4, z), f)) for l, f in roots for z in range(4)
        ]]],
        both,
    )
    pieces = [piece] + [shift_z(piece, dz) for dz in range(1, 4)]
    corner = jnp.where(leaf == 0, sums[4], 0.0)
    corner = spread(
        corner,
        [
            [[(device_at(0, root), device_at(leaf_at(0, z), root))] for z in range(1, 4)],
            [[(device_at(leaf_at(0, z), root), device_at(leaf_at(1, z), root)) for z in range(4)]],
            [[(device_at(l, root), device_at(l, front_at(0, x, 0))) for l in range(8)] for x in range(1, 4)],
            [[
                (device_at(l, front_at(0, x, 0)), device_at(l, front_at(h, x, c))) for l in range(8) for x in range(4)
            ] for h, c in ((0, 1), (1, 0), (1, 1))],
        ],
        both,
    )
    arrays = [a for s in range(n) for a in z_in[s]]
    return final(tab, front_matrix, block_inv, corner, arrays, quarters, pieces)


def solution(mesh):
    placed = (P("leaf", "front", None), P(), P("leaf", "front"), P())
    return jax.shard_map(
        per_device, mesh=mesh, in_specs=placed, out_specs=P("leaf", "front"), check_vma=False
    )
```

time: 1040 us -> 592 us (0.57)
  waiting for transfers between devices: 719 us -> 272 us
  starting transfers between devices: 14 us -> 189 us
  matrix products: 134 us -> 0 us
  local copies, waits for them, and re-layouts: 131 us -> 29.3 us
  Pallas kernels: 0 us -> 97.2 us
  other arithmetic: 23.3 us -> 6.09 us
  between operations: 13.5 us -> 1.09 us
    psum x4 -> x0, waiting for transfers between devices: 431 us -> none  [broadcast(): return lax.psum(jnp.where(mine, x, jnp.zeros_like(x)), axis)]
    all_to_all x2 -> x0, waiting for transfers between devices: 288 us -> none  [the longest x1 175 us: per_device(): lax.all_to_all(routed, 'leaf', split_axis=0, concat_axis=0, tiled=True)]
    ppermute x0 -> x66, waiting for transfers between devices: none -> 272 us  [the longest x15 118 us: shift_z(): lax.ppermute(a, 'leaf', [(leaf_at(l, z), leaf_at(l, z + dz)) for l in ran...]
    ppermute x0 -> x66, starting transfers between devices: none -> 189 us  [the longest x12 76 us: shift_y(): return lax.ppermute(a, ('leaf', 'front'), pairs)]
    dot_general x10 -> x0, matrix products: 134 us -> none  [the longest x1 45.1 us: per_device(): jnp.einsum('gpavb,gpu->uavb', widened, row_select, precision=highest)]
    pallas_call x0 -> x19, Pallas kernels: none -> 97.2 us  [the longest x1 49.5 us: final(): pl.pallas_call(kernel, out_shape=jax.ShapeDtypeStruct(front_tile.shape, j...]
    reshape x4 -> x3, local copies, waits for them, and re-layouts: 60.7 us -> 0.24 us  [tables(): t.reshape(-1)]
    transpose x1 -> x0, local copies, waits for them, and re-layouts: 16.6 us -> none  [per_device(): jnp.einsum('cirb,it->trcb', slot_grid, select_rows, precision=highest)]
  transfers between devices with their start and end apart: 6 -> 66, of which waited for: 6 -> 22; matrix products, arithmetic and copies ran while one was open for 1% -> 1% of each run, Pallas kernels for 0% -> 5%
where the time goes in v1:
time: 592 us; the launch traced here: 595 us
  waiting for transfers between devices  272 us (46%)
  starting transfers between devices  189 us (32%)
  Pallas kernels  97.2 us (16%)
  local copies, waits for them, and re-layouts  29.3 us (5%)
  other arithmetic  6.09 us (1%)
    ppermute x15, waiting for transfers between devices, shift_z(): lax.ppermute(a, 'leaf', [(leaf_at(l, z), leaf_at(l, z + dz)) for l in ran...  118 us
    ppermute x12, starting transfers between devices, shift_y(): return lax.ppermute(a, ('leaf', 'front'), pairs)  76 us
    ppermute x19, waiting for transfers between devices, shift_x(): return lax.ppermute(a, 'front', pairs)  65.9 us
    pallas_call x1, Pallas kernels, final(): pl.pallas_call(kernel, out_shape=jax.ShapeDtypeStruct(front_tile.shape, j...  49.5 us
    pallas_call x17, Pallas kernels, call(): pl.pallas_call(kernel, out_shape=[jax.ShapeDtypeStruct(s, jnp.float32) fo...  43 us
    ppermute x14, starting transfers between devices, spread(): lax.ppermute(a, axis, pairs)  40.5 us
    ppermute x12, waiting for transfers between devices, shift_y(): return lax.ppermute(a, ('leaf', 'front'), pairs)  36.8 us
    ppermute x3, waiting for transfers between devices, per_device(): piece = piece + lax.ppermute(pieces[dz], both, pairs)  35.8 us
  transfers between devices with their start and end apart: 66, of which 22 were waited for; matrix products, arithmetic and copies ran while one was open for 1% of the time, Pallas kernels for 5%

profile of v1, /device:TPU:0, one launch (start us, length us, event | category | flops | bytes accessed | tf_op | source)
XLA Modules:
  0.0 594.6 jit_solution(17435085204228193216)
XLA Ops:
  20.7 9.3 %collective-permute-done.1.refs_2_ = f32[2,2,2,128,128]{4,3,2,1,0:T(8,128)S(1)} collective-permute-done((f32[2,2,2,128,128]{4,3,2,1,0:T(8,128)S(1)}, f32[2,2,2,128,128]{4,3,2,1,0:T(8,128)S(1)}, u32[]{:S(2)}, u32[]{:S(2)}) %collective-permute-start.1) | collective-permute-done | bytes 524320 | tf_op jit(solution)/shard_map/ppermute | solution.py:381
  30.0 12.3 %collective-permute-done.2.refs_3_ = f32[2,2,2,128,128]{4,3,2,1,0:T(8,128)S(1)} collective-permute-done((f32[2,2,2,128,128]{4,3,2,1,0:T(8,128)}, f32[2,2,2,128,128]{4,3,2,1,0:T(8,128)S(1)}, u32[]{:S(2)}, u32[]{:S(2)}) %collective-permute-start.2) | collective-permute-done | bytes 524320 | tf_op jit(solution)/shard_map/ppermute | solution.py:381
  42.3 4.3 pack_y.4
  60.4 10.8 %collective-permute-done.8.refs_2_ = f32[2,2,2,128,128]{4,3,2,1,0:T(8,128)S(1)} collective-permute-done((f32[2,2,2,128,128]{4,3,2,1,0:T(8,128)S(1)}, f32[2,2,2,128,128]{4,3,2,1,0:T(8,128)S(1)}, u32[]{:S(2)}, u32[]{:S(2)}) %collective-permute-start.8) | collective-permute-done | bytes 524320 | tf_op jit(solution)/shard_map/ppermute | solution.py:381
  71.2 11.7 %collective-permute-done.9.refs_3_ = f32[2,2,2,128,128]{4,3,2,1,0:T(8,128)S(1)} collective-permute-done((f32[2,2,2,128,128]{4,3,2,1,0:T(8,128)S(1)}, f32[2,2,2,128,128]{4,3,2,1,0:T(8,128)S(1)}, u32[]{:S(2)}, u32[]{:S(2)}) %collective-permute-start.9) | collective-permute-done | bytes 524320 | tf_op jit(solution)/shard_map/ppermute | solution.py:381
  98.3 17.0 %collective-permute-done.4.refs_2_ = f32[16,128,128]{2,1,0:T(8,128)S(1)} collective-permute-done((f32[16,128,128]{2,1,0:T(8,128)S(1)}, f32[16,128,128]{2,1,0:T(8,128)S(1)}, u32[]{:S(2)}, u32[]{:S(2)}) %collective-permute-start.4) | collective-permute-done | bytes 1048608 | tf_op jit(solution)/shard_map/ppermute | solution.py:395
  115.3 23.8 %collective-permute-start.15 = (f32[16,128,128]{2,1,0:T(8,128)S(1)}, f32[16,128,128]{2,1,0:T(8,128)S(1)}, u32[]{:S(2)}, u32[]{:S(2)}) collective-permute-start(f32[16,128,128]{2,1,0:T(8,128)S(1)} %get-tuple-element.80), channel_id=1, source_target_pairs={{0,8},{1,9},{2,10},{3,11},{4,12},{5,13},{6,14},{7,15},{16,24},{17,... | collective-permute-start | bytes 3145736 | tf_op jit(solution)/shard_map/ppermute | solution.py:395
  139.1 5.5 pack_z.4
  147.4 11.8 %collective-permute-done.14.refs_2_ = f32[16,128,128]{2,1,0:T(8,128)S(1)} collective-permute-done((f32[16,128,128]{2,1,0:T(8,128)S(1)}, f32[16,128,128]{2,1,0:T(8,128)S(1)}, u32[]{:S(2)}, u32[]{:S(2)}) %collective-permute-start.14) | collective-permute-done | bytes 1048608 | tf_op jit(solution)/shard_map/ppermute | solution.py:395
  159.2 4.5 collective-permute-start.19
  164.3 11.4 %collective-permute-done.19.refs_3_ = f32[2,2,2,128,128]{4,3,2,1,0:T(8,128)S(1)} collective-permute-done((f32[2,2,2,128,128]{4,3,2,1,0:T(8,128)S(1)}, f32[2,2,2,128,128]{4,3,2,1,0:T(8,128)S(1)}, u32[]{:S(2)}, u32[]{:S(2)}) %collective-permute-start.19) | collective-permute-done | bytes 524320 | tf_op jit(solution)/shard_map/ppermute | solution.py:381
  179.1 7.7 %collective-permute-done.20.refs_4_ = f32[2,2,2,128,128]{4,3,2,1,0:T(8,128)S(1)} collective-permute-done((f32[2,2,2,128,128]{4,3,2,1,0:T(8,128)S(1)}, f32[2,2,2,128,128]{4,3,2,1,0:T(8,128)S(1)}, u32[]{:S(2)}, u32[]{:S(2)}) %collective-permute-start.20) | collective-permute-done | bytes 524320 | tf_op jit(solution)/shard_map/ppermute | solution.py:381
  186.9 4.5 collective-permute-start.13
  206.0 21.1 %collective-permute-done.13.refs_3_ = f32[2,8,128,128]{3,2,1,0:T(8,128)S(1)} collective-permute-done((f32[2,8,128,128]{3,2,1,0:T(8,128)S(1)}, f32[2,8,128,128]{3,2,1,0:T(8,128)S(1)}, u32[]{:S(2)}, u32[]{:S(2)}) %collective-permute-start.13) | collective-permute-done | bytes 1048608 | tf_op jit(solution)/shard_map/ppermute | solution.py:399
  228.0 20.6 %collective-permute-start.34 = (f32[16,128,128]{2,1,0:T(8,128)}, f32[16,128,128]{2,1,0:T(8,128)}, u32[]{:S(2)}, u32[]{:S(2)}) collective-permute-start(f32[16,128,128]{2,1,0:T(8,128)} %get-tuple-element.92), channel_id=1, source_target_pairs={{0,64},{1,65},{2,66},{3,67},{4,68},{5,69},{6,70},{7,71},{16,80},{1... | collective-permute-start | bytes 3145736 | tf_op jit(solution)/shard_map/ppermute | solution.py:395
  248.6 21.6 %collective-permute-done.23.refs_7_ = f32[2,8,128,128]{3,2,1,0:T(8,128)} collective-permute-done((f32[2,8,128,128]{3,2,1,0:T(8,128)}, f32[2,8,128,128]{3,2,1,0:T(8,128)}, u32[]{:S(2)}, u32[]{:S(2)}) %collective-permute-start.23) | collective-permute-done | bytes 1048608 | tf_op jit(solution)/shard_map/ppermute | solution.py:399
  277.3 4.7 panel_sum.1
  294.7 12.8 %collective-permute-start.35 = (f32[16,128,128]{2,1,0:T(8,128)S(1)}, f32[16,128,128]{2,1,0:T(8,128)S(1)}, u32[]{:S(2)}, u32[]{:S(2)}) collective-permute-start(f32[16,128,128]{2,1,0:T(8,128)S(1)} %copy-done.33), channel_id=1, source_target_pairs={{0,8},{1,9},{2,10},{3,11},{4,12},{5,13},{6,14},{7,15},{16,24},{17,... | collective-permute-start | bytes 3145736 | tf_op jit(solution)/shard_map/ppermute | solution.py:395
  310.9 18.3 %collective-permute-start.27 = (f32[128,128]{1,0:T(8,128)S(1)}, f32[128,128]{1,0:T(8,128)S(1)}, u32[]{:S(2)}, u32[]{:S(2)}) collective-permute-start(f32[128,128]{1,0:T(8,128)S(1)} %add_add_fusion.5), channel_id=1, source_target_pairs={{0,64},{16,80},{32,96},{48,112}} | collective-permute-start | bytes 196616 | tf_op jit(solution)/shard_map/ppermute | solution.py:404
  341.8 5.7 collective-permute-done.54
  348.8 8.7 %collective-permute-start.44 = (f32[16,128,128]{2,1,0:T(8,128)S(1)}, f32[16,128,128]{2,1,0:T(8,128)S(1)}, u32[]{:S(2)}, u32[]{:S(2)}) collective-permute-start(f32[16,128,128]{2,1,0:T(8,128)S(1)} %get-tuple-element.104), channel_id=1, source_target_pairs={{0,64},{1,65},{2,66},{3,67},{4,68},{5,69},{6,70},{7,71},{16,80},{1... | collective-permute-start | bytes 3145736 | tf_op jit(solution)/shard_map/ppermute | solution.py:395
  359.9 7.9 %collective-permute-done.36.refs_4_ = f32[16,128,128]{2,1,0:T(8,128)S(1)} collective-permute-done((f32[16,128,128]{2,1,0:T(8,128)S(1)}, f32[16,128,128]{2,1,0:T(8,128)S(1)}, u32[]{:S(2)}, u32[]{:S(2)}) %collective-permute-start.36) | collective-permute-done | bytes 1048608 | tf_op jit(solution)/shard_map/ppermute | solution.py:395
  379.6 5.7 collective-permute-start.41
  386.9 6.2 %collective-permute-done.32 = f32[128,128]{1,0:T(8,128)S(1)} collective-permute-done((f32[128,128]{1,0:T(8,128)S(1)}, f32[128,128]{1,0:T(8,128)S(1)}, u32[]{:S(2)}, u32[]{:S(2)}) %collective-permute-start.32) | collective-permute-done | bytes 65568 | tf_op jit(solution)/shard_map/ppermute | solution.py:404
  393.1 6.2 %collective-permute-start.59 = (f32[256,256]{1,0:T(8,128)S(1)}, f32[256,256]{1,0:T(8,128)}, u32[]{:S(2)}, u32[]{:S(2)}) collective-permute-start(f32[256,256]{1,0:T(8,128)S(1)} %get-tuple-element.116), channel_id=1, source_target_pairs={{0,16},{1,17},{18,34},{19,35},{36,52},{37,53},{54,6},{55,7},{72,88... | collective-permute-start | bytes 786440 | tf_op jit(solution)/shard_map/ppermute | solution.py:500
  402.4 11.7 %collective-permute-done.59 = f32[256,256]{1,0:T(8,128)} collective-permute-done((f32[256,256]{1,0:T(8,128)S(1)}, f32[256,256]{1,0:T(8,128)}, u32[]{:S(2)}, u32[]{:S(2)}) %collective-permute-start.59) | collective-permute-done | bytes 262176 | tf_op jit(solution)/shard_map/ppermute | solution.py:500
  419.7 4.1 collective-permute-start.42
  423.8 20.5 %collective-permute-done.61 = f32[256,256]{1,0:T(8,128)} collective-permute-done((f32[256,256]{1,0:T(8,128)}, f32[256,256]{1,0:T(8,128)}, u32[]{:S(2)}, u32[]{:S(2)}) %collective-permute-start.61) | collective-permute-done | bytes 262176 | tf_op jit(solution)/shard_map/ppermute | solution.py:500
  460.4 33.9 %collective-permute-done.43.refs_11_ = f32[2,8,128,128]{3,2,1,0:T(8,128)S(1)} collective-permute-done((f32[2,8,128,128]{3,2,1,0:T(8,128)}, f32[2,8,128,128]{3,2,1,0:T(8,128)S(1)}, u32[]{:S(2)}, u32[]{:S(2)}) %collective-permute-start.43) | collective-permute-done | bytes 1048608 | tf_op jit(solution)/shard_map/ppermute | solution.py:399
  494.3 33.0 %collective-permute-done.65.refs_23_ = f32[256,256]{1,0:T(8,128)S(1)} collective-permute-done((f32[256,256]{1,0:T(8,128)S(1)}, f32[256,256]{1,0:T(8,128)S(1)}, u32[]{:S(2)}, u32[]{:S(2)}) %collective-permute-start.65) | collective-permute-done | bytes 262176 | tf_op jit(solution)/shard_map/ppermute | solution.py:399
  528.3 8.8 %collective-permute-done.63.refs_21_ = f32[256,256]{1,0:T(8,128)S(1)} collective-permute-done((f32[256,256]{1,0:T(8,128)S(1)}, f32[256,256]{1,0:T(8,128)S(1)}, u32[]{:S(2)}, u32[]{:S(2)}) %collective-permute-start.63) | collective-permute-done | bytes 262176 | tf_op jit(solution)/shard_map/ppermute | solution.py:399
  544.9 49.5 %final.1 = f32[2048,1024]{1,0:T(8,128)} custom-call(s32[1024]{0:T(1024)S(1)} %concatenate.6.refs_0_.tab, f32[2048,1024]{1,0:T(8,128)} %tile.3, f32[2,128,128]{2,1,0:T(8,128)S(1)} %copy-done.29, f32[128,128]{1,0:T(8,128)S(1)} %add_add_fusion.3.corner, f32[2,8,128,128]{3,2,1,0:T(8,128)S(1)} %get-tuple-element.75.refs_5_.refs_0_, ...), custom_call_target="tpu_custom_call" | custom-call | flops 1000 | bytes 1048576 | tf_op jit(solution)/shard_map/final/pallas_call | solution.py:352
  (233 shorter events, 158.0 us)
Async XLA Ops:
  16.1 26.3 %collective-permute-start.2 = (f32[2,2,2,128,128]{4,3,2,1,0:T(8,128)}, f32[2,2,2,128,128]{4,3,2,1,0:T(8,128)S(1)}, u32[]{:S(2)}, u32[]{:S(2)}) collective-permute-start(f32[2,2,2,128,128]{4,3,2,1,0:T(8,128)} %get-tuple-element.64), channel_id=1, source_target_pairs={{0,4},{1,5},{2,6},{3,7},{4,0},{5,1},{6,2},{7,3},{8,12},{9,13},{10,... | collective-permute-start | bytes 1572872 | tf_op jit(solution)/shard_map/ppermute | solution.py:381
  87.3 28.0 %collective-permute-start.4 = (f32[16,128,128]{2,1,0:T(8,128)S(1)}, f32[16,128,128]{2,1,0:T(8,128)S(1)}, u32[]{:S(2)}, u32[]{:S(2)}) collective-permute-start(f32[16,128,128]{2,1,0:T(8,128)S(1)} %get-tuple-element.67), channel_id=1, source_target_pairs={{0,64},{1,65},{2,66},{3,67},{4,68},{5,69},{6,70},{7,71},{16,80},{1... | collective-permute-start | bytes 3145736 | tf_op jit(solution)/shard_map/ppermute | solution.py:395
  88.6 50.5 %collective-permute-start.5 = (f32[16,128,128]{2,1,0:T(8,128)S(1)}, f32[16,128,128]{2,1,0:T(8,128)S(1)}, u32[]{:S(2)}, u32[]{:S(2)}) collective-permute-start(f32[16,128,128]{2,1,0:T(8,128)S(1)} %get-tuple-element.68), channel_id=1, source_target_pairs={{0,8},{1,9},{2,10},{3,11},{4,12},{5,13},{6,14},{7,15},{16,24},{17,... | collective-permute-start | bytes 3145736 | tf_op jit(solution)/shard_map/ppermute | solution.py:395
  91.5 47.6 %collective-permute-start.6 = (f32[16,128,128]{2,1,0:T(8,128)S(1)}, f32[16,128,128]{2,1,0:T(8,128)S(1)}, u32[]{:S(2)}, u32[]{:S(2)}) collective-permute-start(f32[16,128,128]{2,1,0:T(8,128)S(1)} %get-tuple-element.69), channel_id=1, source_target_pairs={{0,72},{1,73},{2,74},{3,75},{4,76},{5,77},{6,78},{7,79},{16,88},{1... | collective-permute-start | bytes 3145736 | tf_op jit(solution)/shard_map/ppermute | solution.py:395
  93.2 66.0 %collective-permute-start.14 = (f32[16,128,128]{2,1,0:T(8,128)S(1)}, f32[16,128,128]{2,1,0:T(8,128)S(1)}, u32[]{:S(2)}, u32[]{:S(2)}) collective-permute-start(f32[16,128,128]{2,1,0:T(8,128)S(1)} %get-tuple-element.79), channel_id=1, source_target_pairs={{0,64},{1,65},{2,66},{3,67},{4,68},{5,69},{6,70},{7,71},{16,80},{1... | collective-permute-start | bytes 3145736 | tf_op jit(solution)/shard_map/ppermute | solution.py:395
  95.5 68.2 %collective-permute-start.18 = (f32[2,2,2,128,128]{4,3,2,1,0:T(8,128)S(1)}, f32[2,2,2,128,128]{4,3,2,1,0:T(8,128)S(1)}, u32[]{:S(2)}, u32[]{:S(2)}) collective-permute-start(f32[2,2,2,128,128]{4,3,2,1,0:T(8,128)S(1)} %get-tuple-element.83), channel_id=1, source_target_pairs={{0,2},{1,3},{2,4},{3,5},{4,6},{5,7},{6,0},{7,1},{8,10},{9,11},{10,... | collective-permute-start | bytes 1572872 | tf_op jit(solution)/shard_map/ppermute | solution.py:381
  115.3 79.5 %collective-permute-start.15 = (f32[16,128,128]{2,1,0:T(8,128)S(1)}, f32[16,128,128]{2,1,0:T(8,128)S(1)}, u32[]{:S(2)}, u32[]{:S(2)}) collective-permute-start(f32[16,128,128]{2,1,0:T(8,128)S(1)} %get-tuple-element.80), channel_id=1, source_target_pairs={{0,8},{1,9},{2,10},{3,11},{4,12},{5,13},{6,14},{7,15},{16,24},{17,... | collective-permute-start | bytes 3145736 | tf_op jit(solution)/shard_map/ppermute | solution.py:395
  139.0 55.7 %collective-permute-start.16 = (f32[16,128,128]{2,1,0:T(8,128)S(1)}, f32[16,128,128]{2,1,0:T(8,128)S(1)}, u32[]{:S(2)}, u32[]{:S(2)}) collective-permute-start(f32[16,128,128]{2,1,0:T(8,128)S(1)} %get-tuple-element.81), channel_id=1, source_target_pairs={{0,72},{1,73},{2,74},{3,75},{4,76},{5,77},{6,78},{7,79},{16,88},{1... | collective-permute-start | bytes 3145736 | tf_op jit(solution)/shard_map/ppermute | solution.py:395
  144.6 55.3 %collective-permute-start.11 = (f32[2,8,128,128]{3,2,1,0:T(8,128)S(1)}, f32[2,8,128,128]{3,2,1,0:T(8,128)S(1)}, u32[]{:S(2)}, u32[]{:S(2)}) collective-permute-start(f32[2,8,128,128]{3,2,1,0:T(8,128)S(1)} %get-tuple-element.76), channel_id=1, source_target_pairs={{0,16},{16,32},{32,48},{48,0},{64,80},{80,96},{96,112},{112,64},{1... | collective-permute-start | bytes 3145736 | tf_op jit(solution)/shard_map/ppermute | solution.py:399
  175.7 29.3 %collective-permute-start.12 = (f32[2,8,128,128]{3,2,1,0:T(8,128)S(1)}, f32[2,8,128,128]{3,2,1,0:T(8,128)S(1)}, u32[]{:S(2)}, u32[]{:S(2)}) collective-permute-start(f32[2,8,128,128]{3,2,1,0:T(8,128)S(1)} %get-tuple-element.77), channel_id=1, source_target_pairs={{0,32},{16,48},{32,0},{48,16},{64,96},{80,112},{96,64},{112,80},{1... | collective-permute-start | bytes 3145736 | tf_op jit(solution)/shard_map/ppermute | solution.py:399
  186.9 40.2 %collective-permute-start.13 = (f32[2,8,128,128]{3,2,1,0:T(8,128)S(1)}, f32[2,8,128,128]{3,2,1,0:T(8,128)S(1)}, u32[]{:S(2)}, u32[]{:S(2)}) collective-permute-start(f32[2,8,128,128]{3,2,1,0:T(8,128)S(1)} %get-tuple-element.78), channel_id=1, source_target_pairs={{0,48},{16,0},{32,16},{48,32},{64,112},{80,64},{96,80},{112,96},{1... | collective-permute-start | bytes 3145736 | tf_op jit(solution)/shard_map/ppermute | solution.py:399
  197.3 51.3 %collective-permute-start.21 = (f32[2,8,128,128]{3,2,1,0:T(8,128)}, f32[2,8,128,128]{3,2,1,0:T(8,128)}, u32[]{:S(2)}, u32[]{:S(2)}) collective-permute-start(f32[2,8,128,128]{3,2,1,0:T(8,128)} %get-tuple-element.88), channel_id=1, source_target_pairs={{0,16},{16,32},{32,48},{48,0},{64,80},{80,96},{96,112},{112,64},{1... | collective-permute-start | bytes 3145736 | tf_op jit(solution)/shard_map/ppermute | solution.py:399
  197.4 51.2 %collective-permute-start.22 = (f32[2,8,128,128]{3,2,1,0:T(8,128)}, f32[2,8,128,128]{3,2,1,0:T(8,128)}, u32[]{:S(2)}, u32[]{:S(2)}) collective-permute-start(f32[2,8,128,128]{3,2,1,0:T(8,128)} %get-tuple-element.89), channel_id=1, source_target_pairs={{0,32},{16,48},{32,0},{48,16},{64,96},{80,112},{96,64},{112,80},{1... | collective-permute-start | bytes 3145736 | tf_op jit(solution)/shard_map/ppermute | solution.py:399
  199.9 70.3 %collective-permute-start.23 = (f32[2,8,128,128]{3,2,1,0:T(8,128)}, f32[2,8,128,128]{3,2,1,0:T(8,128)}, u32[]{:S(2)}, u32[]{:S(2)}) collective-permute-start(f32[2,8,128,128]{3,2,1,0:T(8,128)} %get-tuple-element.90), channel_id=1, source_target_pairs={{0,48},{16,0},{32,16},{48,32},{64,112},{80,64},{96,80},{112,96},{1... | collective-permute-start | bytes 3145736 | tf_op jit(solution)/shard_map/ppermute | solution.py:399
  206.0 80.3 %collective-permute-start.37 = (f32[8,2,128,128]{3,2,1,0:T(8,128)}, f32[8,2,128,128]{3,2,1,0:T(8,128)}, u32[]{:S(2)}, u32[]{:S(2)}) collective-permute-start(f32[8,2,128,128]{3,2,1,0:T(8,128)} %pack_core.7), channel_id=1, source_target_pairs={{0,1},{1,0},{2,3},{3,2},{4,5},{5,4},{6,7},{7,6},{8,9},{9,8},{10,11... | collective-permute-start | bytes 3145736 | tf_op jit(solution)/shard_map/ppermute | solution.py:381
  228.0 61.3 %collective-permute-start.34 = (f32[16,128,128]{2,1,0:T(8,128)}, f32[16,128,128]{2,1,0:T(8,128)}, u32[]{:S(2)}, u32[]{:S(2)}) collective-permute-start(f32[16,128,128]{2,1,0:T(8,128)} %get-tuple-element.92), channel_id=1, source_target_pairs={{0,64},{1,65},{2,66},{3,67},{4,68},{5,69},{6,70},{7,71},{16,80},{1... | collective-permute-start | bytes 3145736 | tf_op jit(solution)/shard_map/ppermute | solution.py:395
  282.0 26.1 %collective-permute-start.52 = (f32[512,256]{1,0:T(8,128)S(1)}, f32[512,256]{1,0:T(8,128)S(1)}, u32[]{:S(2)}, u32[]{:S(2)}) collective-permute-start(f32[512,256]{1,0:T(8,128)S(1)} %broadcast_select_fusion), channel_id=1, source_target_pairs={{0,6},{16,22},{32,38},{48,54},{64,70},{80,86},{96,102},{112,118}} | collective-permute-start | bytes 1572872 | tf_op jit(solution)/shard_map/ppermute | solution.py:487
  283.5 27.0 %collective-permute-start.51 = (f32[512,256]{1,0:T(8,128)S(1)}, f32[512,256]{1,0:T(8,128)S(1)}, u32[]{:S(2)}, u32[]{:S(2)}) collective-permute-start(f32[512,256]{1,0:T(8,128)S(1)} %broadcast_select_fusion.1), channel_id=1, source_target_pairs={{0,4},{16,20},{32,36},{48,52},{64,68},{80,84},{96,100},{112,116}} | collective-permute-start | bytes 1572872 | tf_op jit(solution)/shard_map/ppermute | solution.py:487
  294.7 44.3 %collective-permute-start.35 = (f32[16,128,128]{2,1,0:T(8,128)S(1)}, f32[16,128,128]{2,1,0:T(8,128)S(1)}, u32[]{:S(2)}, u32[]{:S(2)}) collective-permute-start(f32[16,128,128]{2,1,0:T(8,128)S(1)} %copy-done.33), channel_id=1, source_target_pairs={{0,8},{1,9},{2,10},{3,11},{4,12},{5,13},{6,14},{7,15},{16,24},{17,... | collective-permute-start | bytes 3145736 | tf_op jit(solution)/shard_map/ppermute | solution.py:395
  335.1 32.7 %collective-permute-start.36 = (f32[16,128,128]{2,1,0:T(8,128)S(1)}, f32[16,128,128]{2,1,0:T(8,128)S(1)}, u32[]{:S(2)}, u32[]{:S(2)}) collective-permute-start(f32[16,128,128]{2,1,0:T(8,128)S(1)} %copy-done.31), channel_id=1, source_target_pairs={{0,72},{1,73},{2,74},{3,75},{4,76},{5,77},{6,78},{7,79},{16,88},{1... | collective-permute-start | bytes 3145736 | tf_op jit(solution)/shard_map/ppermute | solution.py:395
  348.8 50.5 %collective-permute-start.44 = (f32[16,128,128]{2,1,0:T(8,128)S(1)}, f32[16,128,128]{2,1,0:T(8,128)S(1)}, u32[]{:S(2)}, u32[]{:S(2)}) collective-permute-start(f32[16,128,128]{2,1,0:T(8,128)S(1)} %get-tuple-element.104), channel_id=1, source_target_pairs={{0,64},{1,65},{2,66},{3,67},{4,68},{5,69},{6,70},{7,71},{16,80},{1... | collective-permute-start | bytes 3145736 | tf_op jit(solution)/shard_map/ppermute | solution.py:395
  371.0 78.2 %collective-permute-start.45 = (f32[16,128,128]{2,1,0:T(8,128)}, f32[16,128,128]{2,1,0:T(8,128)}, u32[]{:S(2)}, u32[]{:S(2)}) collective-permute-start(f32[16,128,128]{2,1,0:T(8,128)} %get-tuple-element.105), channel_id=1, source_target_pairs={{0,8},{1,9},{2,10},{3,11},{4,12},{5,13},{6,14},{7,15},{16,24},{17,... | collective-permute-start | bytes 3145736 | tf_op jit(solution)/shard_map/ppermute | solution.py:395
  371.0 79.5 %collective-permute-start.46 = (f32[16,128,128]{2,1,0:T(8,128)}, f32[16,128,128]{2,1,0:T(8,128)}, u32[]{:S(2)}, u32[]{:S(2)}) collective-permute-start(f32[16,128,128]{2,1,0:T(8,128)} %get-tuple-element.106), channel_id=1, source_target_pairs={{0,72},{1,73},{2,74},{3,75},{4,76},{5,77},{6,78},{7,79},{16,88},{1... | collective-permute-start | bytes 3145736 | tf_op jit(solution)/shard_map/ppermute | solution.py:395
  379.6 76.5 %collective-permute-start.41 = (f32[2,8,128,128]{3,2,1,0:T(8,128)}, f32[2,8,128,128]{3,2,1,0:T(8,128)}, u32[]{:S(2)}, u32[]{:S(2)}) collective-permute-start(f32[2,8,128,128]{3,2,1,0:T(8,128)} %get-tuple-element.101), channel_id=1, source_target_pairs={{0,16},{16,32},{32,48},{48,0},{64,80},{80,96},{96,112},{112,64},{1... | collective-permute-start | bytes 3145736 | tf_op jit(solution)/shard_map/ppermute | solution.py:399
  414.1 30.2 %collective-permute-start.61 = (f32[256,256]{1,0:T(8,128)}, f32[256,256]{1,0:T(8,128)}, u32[]{:S(2)}, u32[]{:S(2)}) collective-permute-start(f32[256,256]{1,0:T(8,128)} %get-tuple-element.118), channel_id=1, source_target_pairs={{0,48},{1,49},{18,2},{19,3},{36,20},{37,21},{54,38},{55,39},{72,12... | collective-permute-start | bytes 786440 | tf_op jit(solution)/shard_map/ppermute | solution.py:500
  419.7 39.7 %collective-permute-start.42 = (f32[2,8,128,128]{3,2,1,0:T(8,128)}, f32[2,8,128,128]{3,2,1,0:T(8,128)}, u32[]{:S(2)}, u32[]{:S(2)}) collective-permute-start(f32[2,8,128,128]{3,2,1,0:T(8,128)} %get-tuple-element.102), channel_id=1, source_target_pairs={{0,32},{16,48},{32,0},{48,16},{64,96},{80,112},{96,64},{112,80},{1... | collective-permute-start | bytes 3145736 | tf_op jit(solution)/shard_map/ppermute | solution.py:399
  444.3 50.0 %collective-permute-start.43 = (f32[2,8,128,128]{3,2,1,0:T(8,128)}, f32[2,8,128,128]{3,2,1,0:T(8,128)S(1)}, u32[]{:S(2)}, u32[]{:S(2)}) collective-permute-start(f32[2,8,128,128]{3,2,1,0:T(8,128)} %copy-done.34), channel_id=1, source_target_pairs={{0,48},{16,0},{32,16},{48,32},{64,112},{80,64},{96,80},{112,96},{1... | collective-permute-start | bytes 3145736 | tf_op jit(solution)/shard_map/ppermute | solution.py:399
  456.0 81.1 %collective-permute-start.47 = (f32[2,8,128,128]{3,2,1,0:T(8,128)S(1)}, f32[2,8,128,128]{3,2,1,0:T(8,128)S(1)}, u32[]{:S(2)}, u32[]{:S(2)}) collective-permute-start(f32[2,8,128,128]{3,2,1,0:T(8,128)S(1)} %get-tuple-element.108), channel_id=1, source_target_pairs={{0,16},{16,32},{32,48},{48,0},{64,80},{80,96},{96,112},{112,64},{1... | collective-permute-start | bytes 3145736 | tf_op jit(solution)/shard_map/ppermute | solution.py:399
  456.1 81.0 %collective-permute-start.48 = (f32[2,8,128,128]{3,2,1,0:T(8,128)S(1)}, f32[2,8,128,128]{3,2,1,0:T(8,128)S(1)}, u32[]{:S(2)}, u32[]{:S(2)}) collective-permute-start(f32[2,8,128,128]{3,2,1,0:T(8,128)S(1)} %get-tuple-element.109), channel_id=1, source_target_pairs={{0,32},{16,48},{32,0},{48,16},{64,96},{80,112},{96,64},{112,80},{1... | collective-permute-start | bytes 3145736 | tf_op jit(solution)/shard_map/ppermute | solution.py:399
  457.8 79.3 %collective-permute-start.49 = (f32[2,8,128,128]{3,2,1,0:T(8,128)S(1)}, f32[2,8,128,128]{3,2,1,0:T(8,128)S(1)}, u32[]{:S(2)}, u32[]{:S(2)}) collective-permute-start(f32[2,8,128,128]{3,2,1,0:T(8,128)S(1)} %get-tuple-element.110), channel_id=1, source_target_pairs={{0,48},{16,0},{32,16},{48,32},{64,112},{80,64},{96,80},{112,96},{1... | collective-permute-start | bytes 3145736 | tf_op jit(solution)/shard_map/ppermute | solution.py:399
  459.4 67.9 %collective-permute-start.65 = (f32[256,256]{1,0:T(8,128)S(1)}, f32[256,256]{1,0:T(8,128)S(1)}, u32[]{:S(2)}, u32[]{:S(2)}) collective-permute-start(f32[256,256]{1,0:T(8,128)S(1)} %add.124.refs_20_), channel_id=1, source_target_pairs={{0,48},{16,0},{32,16},{48,32},{64,112},{80,64},{96,80},{112,96},{1... | collective-permute-start | bytes 786440 | tf_op jit(solution)/shard_map/ppermute | solution.py:399
  494.3 34.0 %collective-permute-start.64 = (f32[256,256]{1,0:T(8,128)S(1)}, f32[256,256]{1,0:T(8,128)S(1)}, u32[]{:S(2)}, u32[]{:S(2)}) collective-permute-start(f32[256,256]{1,0:T(8,128)S(1)} %add.124.refs_20_), channel_id=1, source_target_pairs={{0,32},{16,48},{32,0},{48,16},{64,96},{80,112},{96,64},{112,80},{1... | collective-permute-start | bytes 786440 | tf_op jit(solution)/shard_map/ppermute | solution.py:399
  (72 other events, 1296.9 us)

commit v2 on v0

v2 whole, which is shorter than its diff:
```python
import functools

import jax
import jax.numpy as jnp
from jax import lax
from jax.experimental import pallas as pl
from jax.experimental.pallas import tpu as pltpu
from jax.sharding import PartitionSpec as P

BLK = 128
CAPF = 4
NPAN = 2
UB = 32
WHOLE = [(c, 0, 128) for c in range(CAPF)]
COUNT = 48

T_R, T_RANK, T_M, T_ROWU, T_PROW, T_VCOL, T_ALL = 128, 384, 640, 768, 832, 960, 1024

HBM = pl.BlockSpec(memory_space=pltpu.HBM)
SMEM = pl.BlockSpec(memory_space=pltpu.SMEM)
COST = pl.CostEstimate(flops=1000, bytes_accessed=1 << 16, transcendentals=0)
VMEM = 60 << 20
STEP = 2


def leaf_at(y_lo, z):
    return y_lo % 2 * 4 + z % 4


def front_at(y_hi, x, core):
    return y_hi % 2 * 8 + x % 4 * 2 + core % 2


def device_at(leaf, front):
    return leaf * 16 + front


def copy(src, dst, sem):
    return pltpu.make_async_copy(src, dst, sem)


def call(body, operands, outs, name):
    n = len(outs)

    def kernel(*refs):
        ins, results, held, sem = refs[:-n - 2], refs[-n - 2:-2], refs[-2], refs[-1]
        body(ins, held, sem)
        writes = [copy(held.at[k], results[k], sem) for k in range(n)]
        for w in writes:
            w.start()
        for w in writes:
            w.wait()

    return pl.pallas_call(
        kernel,
        out_shape=[jax.ShapeDtypeStruct(s, jnp.float32) for s in outs],
        in_specs=[SMEM] + [HBM] * (len(operands) - 1),
        out_specs=[HBM] * n,
        scratch_shapes=[pltpu.VMEM((n,) + outs[0], jnp.float32), pltpu.SemaphoreType.DMA(())],
        compiler_params=pltpu.CompilerParams(vmem_limit_bytes=VMEM),
        cost_estimate=COST,
        name=name,
    )(*operands)


def own_columns(meta, act):
    def column(j, carry):
        before, rank = carry
        owner = meta[j] >> 3
        rank = jnp.where(owner == before, rank + 1, 0)
        act(j, owner, rank)
        return owner, rank

    lax.fori_loop(0, UB, column, (jnp.int32(-1), jnp.int32(0)))


def pack_core(first, last, meta, child):
    def body(ins, held, sem):
        meta, child = ins[:2]
        core = meta[UB + 1] & 1
        for wait in (False, True):
            def act(j, owner, rank, wait=wait):
                @pl.when((rank >= first) & (rank < last) & ((owner & 1) != core))
                def _():
                    columns = pl.ds(pl.multiple_of(j * BLK, BLK), BLK)
                    one = copy(child.at[:, :, columns], held.at[0, rank - first, owner >> 1], sem)
                    one.wait() if wait else one.start()

            own_columns(meta, act)

    return call(body, [meta, child], [(last - first, 8, 2, BLK, BLK)], "pack_core")


def pack_x(first, last, meta, child, crossed, base, after):
    def body(ins, held, sem):
        meta, child, crossed = ins[:3]
        front = meta[UB + 1]
        x, core = (front >> 1) & 3, front & 1
        for wait in (False, True):
            def act(j, owner, rank, wait=wait):
                @pl.when((rank >= first) & (rank < last) & ((owner & 1) == core))
                def _():
                    source = child.at[:, :, pl.ds(pl.multiple_of(j * BLK, BLK), BLK)]
                    d = copy(source, held.at[((owner >> 1) - x) & 3, rank - first, owner >> 3, 0], sem)
                    d.wait() if wait else d.start()

            def other(f, carry, wait=wait):
                for rank in range(first, last):
                    @pl.when(meta[COUNT + f * 2 + core] > rank)
                    def _():
                        d = copy(crossed.at[rank - base, f], held.at[(f - x) & 3, rank - first, f >> 2, 1], sem)
                        d.wait() if wait else d.start()

                return carry

            own_columns(meta, act)
            lax.fori_loop(0, 8, other, 0)

    return call(body, [meta, child, crossed] + after, [(last - first, 2, 2, 2, BLK, BLK)] * 4, "pack_x")


def pack_y(c, tab, arrays, base, extra=None):
    def body(ins, held, sem):
        tab, arrays = ins[0], ins[1:]
        leaf, front = tab[0], tab[1]
        y_hi, x, core = front >> 3, (front >> 1) & 3, front & 1
        for wait in (False, True):
            for to_hi in range(2):
                @pl.when(tab[T_M + leaf * 16 + to_hi * 8 + (front & 7)] > c)
                def _():
                    for k in range(4):
                        def one(n, carry):
                            other, r = n >> 1, n & 1
                            slot = (((x - k) & 3) * 2 + (core ^ other)) * 2 + r
                            owner = tab[T_R + leaf * UB + y_hi * 16 + slot]
                            d = copy(arrays[k].at[c - base, to_hi, other, r], held.at[0, to_hi * 2 + (owner >> 2), slot], sem)
                            d.wait() if wait else d.start()
                            return carry

                        lax.fori_loop(0, 4, one, 0)

            if extra is not None:
                to = held.at[0, (1 - y_hi) * 2 + (leaf >> 2)]
                for h in range(2):
                    columns = pl.ds(h * BLK, BLK)
                    for source, target in (
                        (arrays[4].at[pl.ds(0, BLK), columns], to.at[16 + h]),
                        (arrays[4].at[pl.ds(BLK, 64), columns], to.at[18, pl.ds(h * 64, 64)]),
                    ):
                        d = copy(source, target, sem)
                        d.wait() if wait else d.start()

    arrays = arrays if extra is None else arrays + [extra]
    return call(body, [tab] + arrays, [(4, 16 if extra is None else 19, BLK, BLK)], "pack_y")[0]


def pack_z(c, tab, array, extra=None):
    def body(ins, held, sem):
        tab, array = ins[:2]
        leaf, front = tab[0], tab[1]
        z, y_lo = leaf & 3, leaf >> 2
        for wait in (False, True):
            for source in range(4):
                from_lo = source & 1
                group = from_lo * 4 + z

                @pl.when(tab[T_M + group * 16 + front] > c)
                def _():
                    def one(s, carry):
                        i = group * UB + (source >> 1) * 16 + s
                        owner = tab[T_R + i]

                        @pl.when((owner >> 2) == y_lo)
                        def _():
                            d = copy(array.at[source, s], held.at[(owner - z) & 3, from_lo, tab[T_RANK + i]], sem)
                            d.wait() if wait else d.start()

                        return carry

                    lax.fori_loop(0, 16, one, 0)

            if extra is not None:
                for k in range(4):
                    for h in range(2):
                        d = copy(ins[2].at[:, pl.ds(h * BLK, BLK)], held.at[k, h, 8], sem)
                        d.wait() if wait else d.start()

    more = [] if extra is None else [extra]
    return call(body, [tab, array] + more, [(2, 8 + len(more), BLK, BLK)] * 4, "pack_z")


def pack_panel(meta, child, front_tile):
    def body(ins, held, sem):
        meta, child, tile = ins
        leaf, front = meta[UB], meta[UB + 1]
        for wait in (False, True):
            def go(source, at):
                d = copy(source, held.at[(0,) + at], sem)
                d.wait() if wait else d.start()

            for j in range(NPAN):
                @pl.when(meta[j] < NPAN)
                def _():
                    for r in range(2):
                        go(child.at[r, :, pl.ds(j * BLK, BLK)], (meta[front * 2 + r] >> 4, r * NPAN + meta[j]))

            @pl.when((front == 0) & (meta[0] == 0) & (meta[1] == 1))
            def _():
                for t in range(8):
                    go(child.at[1, :, pl.ds(0, BLK)], (t, 4))

            @pl.when((front == 0) & (leaf == 0))
            def _():
                for t in range(8):
                    go(tile.at[pl.ds(BLK, BLK), pl.ds(0, BLK)], (t, 5))

    return call(body, [meta, child, front_tile], [(8, 6, BLK, BLK)], "pack_panel")[0]


def panel_part(flat, front_tile, arrived):
    def kernel(flat, tile, arrived, o0, o1, o2, o3, total, held, sem, tile_sem):
        leaf, front = flat[256], flat[257]
        y_hi, x, core = front >> 3, (front >> 1) & 3, front & 1
        come = copy(arrived, held, sem)
        come.start()

        def place(u):
            return (((u >> 1) & 3) - x) & 3, pl.ds(pl.multiple_of((((u & 1) ^ core) * 2 + ((u >> 3) ^ y_hi)) * BLK, BLK), BLK)

        def rows(act):
            def one(u, carry):
                act(copy(tile.at[pl.ds(pl.multiple_of(u * BLK, BLK), BLK), pl.ds(0, NPAN * BLK)], total.at[place(u)], tile_sem))
                return carry

            lax.fori_loop(0, 16, one, 0)

        @pl.when(front == 0)
        def _():
            rows(lambda d: d.start())
            rows(lambda d: d.wait())

        @pl.when(front != 0)
        def _():
            total[...] = jnp.zeros_like(total)

        come.wait()

        @pl.when(front == 0)
        def _():
            for k in range(4):
                for h in range(2):
                    total[k, pl.ds(512, 64), pl.ds(h * BLK, BLK)] = held[0, 5, pl.ds(h * 64, 64)]

            def corner(g, carry):
                @pl.when((flat[g * UB] == 0) & (flat[g * UB + 1] == 1))
                def _():
                    for k in range(4):
                        for h in range(2):
                            total[k, pl.ds(512, 64), pl.ds(h * BLK, BLK)] += held[g, 4, pl.ds(h * 64, 64)]

                return carry

            lax.fori_loop(0, 8, corner, 0)

        def add(n, carry):
            g, r = n >> 1, n & 1
            parent = flat[g * UB + front * 2 + r]

            @pl.when((parent >> 4) == leaf)
            def _():
                k, at = place(parent & 15)
                for v in range(NPAN):
                    @pl.when((flat[g * UB] == v) | (flat[g * UB + 1] == v))
                    def _():
                        total[k, at, pl.ds(v * BLK, BLK)] += held[g, r * NPAN + v]

            return carry

        lax.fori_loop(0, 16, add, 0)
        out = [copy(total.at[k], o, sem) for k, o in enumerate((o0, o1, o2, o3))]
        for o in out:
            o.start()
        for o in out:
            o.wait()

    block = (4 * BLK + 64, NPAN * BLK)
    return pl.pallas_call(
        kernel,
        out_shape=[jax.ShapeDtypeStruct(block, jnp.float32)] * 4,
        in_specs=[SMEM, HBM, HBM],
        out_specs=[HBM] * 4,
        scratch_shapes=[
            pltpu.VMEM((4,) + block, jnp.float32),
            pltpu.VMEM((8, 6, BLK, BLK), jnp.float32),
            pltpu.SemaphoreType.DMA(()),
            pltpu.SemaphoreType.DMA(()),
        ],
        compiler_params=pltpu.CompilerParams(vmem_limit_bytes=VMEM),
        cost_estimate=COST,
        name="panel_part",
    )(flat, front_tile, arrived)


def product(a, b, precision=lax.Precision.HIGHEST):
    return lax.dot_general(a, b, (((1,), (1,)), ((), ())), precision=precision, preferred_element_type=jnp.float32)


def factors(tab, block_inv, corner, sources, sides, of_rows):
    n = len(sources)
    blocks = 8

    def kernel(tab, inv, corner, *refs):
        sources, outs = refs[:n], refs[n:]
        leaf, front = tab[0], tab[1]
        below = product(corner[...], inv[0])
        for side, source in zip(sides, sources):
            for k in range(4):
                for m in range(2 if of_rows else 1):
                    if of_rows:
                        at = ((front >> 3) ^ side) * 8 + (((front >> 1) - k) & 3) * 2 + ((front & 1) ^ m)
                        raw = source[k, m]
                    else:
                        at = ((leaf >> 2) ^ side) * 4 + ((leaf - k) & 3)
                        raw = source[k]
                    first = ((leaf if of_rows else front) == 0) & (at == 0)
                    one = product(raw[:, :BLK], inv[0])
                    two = product(raw[:, BLK:] - product(one, below), inv[1])
                    two = jnp.where(first, 0.0, two)
                    rows = pl.ds(pl.multiple_of((at & 7) * BLK, BLK), BLK)
                    for h, part in enumerate((one, two)):
                        high = part.astype(jnp.bfloat16)
                        low = (part - high.astype(jnp.float32)).astype(jnp.bfloat16)
                        for t, value in enumerate((high, low, high) if of_rows else (high, high, low)):
                            outs[0][rows, pl.ds((t * 2 + h) * BLK, BLK)] = value
                        if of_rows:
                            outs[1][rows, pl.ds(h * BLK, BLK)] = part

    vmem = pl.BlockSpec(memory_space=pltpu.VMEM)
    shapes = [jax.ShapeDtypeStruct((blocks * BLK, 6 * BLK), jnp.bfloat16)]
    if of_rows:
        shapes.append(jax.ShapeDtypeStruct((blocks * BLK, 2 * BLK), jnp.float32))
    return pl.pallas_call(
        kernel,
        out_shape=shapes,
        in_specs=[SMEM] + [vmem] * (2 + n),
        out_specs=[vmem] * len(shapes),
        compiler_params=pltpu.CompilerParams(vmem_limit_bytes=VMEM),
        cost_estimate=COST,
        name="factors",
    )(tab, block_inv, corner, *sources)


def accumulate(chunks, tab, tile, arrays, panel=None):
    n_arrays = 4 * len(chunks)
    width = tile.shape[1]
    ranks = sorted({c for c, _, _ in chunks})
    steps = tile.shape[0] // (BLK * STEP)
    half = steps // 2

    def kernel(tab, tile, *refs):
        arrays, refs = refs[:n_arrays], refs[n_arrays:]
        if panel is not None:
            (near, near_plain, far, far_plain, right), refs = refs[:5], refs[5:]
        out, held, sems = refs
        i = pl.program_id(0)
        z = tab[0] & 3

        def each(step, act):
            for r in range(STEP):
                for g in range(8):
                    group = g // 4 * 4 + ((z - g) & 3)
                    p = tab[T_PROW + group * 16 + step * STEP + r]

                    @pl.when(p >= 0)
                    def _():
                        for m, c in enumerate(ranks):
                            v = tab[T_VCOL + group * 4 + c]

                            @pl.when(v >= 0)
                            def _():
                                act(r, g, p, m, c, v)

        def fetch(step, wait):
            slot = step & 1

            def act(r, g, p, m, c, v):
                for n, (cc, off, rows) in enumerate(chunks):
                    if cc == c:
                        source = arrays[n * 4 + g % 4].at[g // 4, p]
                        one = copy(source, held.at[slot, r, g, m, pl.ds(off, rows)], sems.at[slot])
                        one.wait() if wait else one.start()

            each(step, act)

        @pl.when(i == 0)
        def _():
            fetch(0, False)

        @pl.when(i + 1 < steps)
        def _():
            fetch(i + 1, False)

        if panel is None:
            out[...] = tile[...]
        else:
            mine = (i // half) == (tab[1] >> 3)
            out[...] = tile[...] - product(jnp.where(mine, near[...], far[...]), right[...], None)
        fetch(i, True)
        slot = i & 1

        def add(r, g, p, m, c, v):
            out[pl.ds(r * BLK, BLK), pl.ds(pl.multiple_of(v * BLK, BLK), BLK)] += held[slot, r, g, m]

        each(i, add)
        if panel is not None:
            @pl.when(tab[1] == 0)
            def _():
                out[:, pl.ds(0, 2 * BLK)] = jnp.where(mine, near_plain[...], far_plain[...])

    rows = BLK * STEP
    specs = [SMEM, pl.BlockSpec((rows, width), lambda i: (i, 0))] + [HBM] * n_arrays
    operands = [tab, tile] + list(arrays)
    if panel is not None:
        specs += [
            pl.BlockSpec((rows, 6 * BLK), lambda i: (i % half, 0)),
            pl.BlockSpec((rows, 2 * BLK), lambda i: (i % half, 0)),
        ] * 2 + [pl.BlockSpec((width, 6 * BLK), lambda i: (0, 0))]
        operands += list(panel)
    return pl.pallas_call(
        kernel,
        out_shape=jax.ShapeDtypeStruct(tile.shape, jnp.float32),
        grid=(steps,),
        in_specs=specs,
        out_specs=pl.BlockSpec((rows, width), lambda i: (i, 0)),
        scratch_shapes=[
            pltpu.VMEM((2, STEP, 8, len(ranks), BLK, BLK), jnp.float32),
            pltpu.SemaphoreType.DMA((2,)),
        ],
        compiler_params=pltpu.CompilerParams(vmem_limit_bytes=VMEM),
        cost_estimate=COST,
        name="accumulate" if panel is None else "final",
    )(*operands)


def shift_x(a, dx, dc):
    pairs = [
        (front_at(h, x, c), front_at(h, x + dx, c + dc)) for h in range(2) for x in range(4) for c in range(2)
    ]
    return lax.ppermute(a, "front", pairs)


def exchange_y(a):
    groups = [
        [device_at(leaf_at(y, z), front_at(y // 2, x, c)) for y in range(4)]
        for z in range(4) for x in range(4) for c in range(2)
    ]
    return lax.all_to_all(a, ("leaf", "front"), 0, 0, axis_index_groups=groups, tiled=True)


def shift_z(a, dz):
    return lax.ppermute(a, "leaf", [(leaf_at(l, z), leaf_at(l, z + dz)) for l in range(2) for z in range(4)])


def tie(values, *after):
    return list(lax.optimization_barrier(tuple(values) + after)[:len(values)])


def other_device(a, bit):
    return lax.ppermute(a, ("leaf", "front"), [(d, d ^ bit) for d in range(128)])


OTHER_CORE, OTHER_Y_HI, OTHER_Y_LO = 1, 8, 64


def tables(assembly, leaf, front):
    col_owner, row_owner = assembly >> 3, assembly >> 4
    earlier = jnp.arange(UB)[:, None] > jnp.arange(UB)[None, :]

    def rank(owner):
        same = (owner[:, :, None] == owner[:, None, :]) & earlier[None]
        return jnp.sum(same.astype(jnp.int32), axis=2)

    def pick(match, value):
        return jnp.sum(jnp.where(match, value + 1, 0), axis=1).astype(jnp.int32) - 1

    row_rank, col_rank = rank(row_owner), rank(col_owner)
    count = jnp.sum((col_owner[:, :, None] == jnp.arange(16)).astype(jnp.int32), axis=1)
    mine = row_owner == leaf
    row_u = pick(
        mine[:, :, None] & (row_rank[:, :, None] == jnp.arange(8)), (assembly & 15)[:, :, None]
    )
    row_p = pick(assembly[:, :, None] == leaf * 16 + jnp.arange(16), row_rank[:, :, None])
    col_v = pick(
        (col_owner == front)[:, :, None] & (col_rank[:, :, None] == jnp.arange(CAPF)), (assembly & 7)[:, :, None]
    )
    head = jnp.concatenate([leaf[None], front[None], jnp.zeros((T_R - 2,), jnp.int32)])
    parts = [head] + [t.reshape(-1) for t in (row_owner, row_rank, count, row_u, row_p, col_v)]
    size = sum(t.shape[0] for t in parts)
    return jnp.concatenate(parts + [jnp.zeros((T_ALL - size,), jnp.int32)])


def per_device(child_update, assembly, front_matrix, block_inv):
    leaf, front = lax.axis_index("leaf"), lax.axis_index("front")
    child = child_update.reshape(2, BLK, child_update.shape[2])
    own = lax.dynamic_index_in_dim(assembly, leaf, 0, keepdims=False)
    count = jnp.sum(((own >> 3)[:, None] == jnp.arange(16)).astype(jnp.int32), axis=0)
    meta = jnp.concatenate([own, leaf[None], front[None], jnp.zeros((COUNT - UB - 2,), jnp.int32), count])
    tab = tables(assembly, leaf, front)

    flat = jnp.concatenate([assembly.reshape(-1), leaf[None], front[None], jnp.zeros((126,), jnp.int32)])
    n = CAPF

    arrived = lax.all_to_all(pack_panel(meta, child, front_matrix), "leaf", 0, 0, tiled=True)
    first = shift_x(pack_core(0, 1, meta, child)[0], 0, 1)
    rest = shift_x(pack_core(1, n, meta, child)[0], 0, 1)

    outs = pack_x(0, 1, meta, child, first, 0, [])
    x_in = [[outs[0]] + [shift_x(outs[k], k, 0) for k in range(1, 4)]]
    outs = pack_x(1, 2, meta, child, rest, 1, x_in[0][1:])
    x_in.append([outs[0]] + [shift_x(outs[k], k, 0) for k in range(1, 4)])
    parts = panel_part(tie([flat], outs[0])[0], front_matrix, arrived)
    parts = [parts[0]] + [shift_x(a, k + 1, 0) for k, a in enumerate(tie(parts[1:], x_in[1][1], x_in[1][3]))]
    outs = pack_x(2, n, meta, child, rest, 1, x_in[1][1:] + parts[1:])
    x_in.append([outs[0]] + [shift_x(outs[k], k, 0) for k in range(1, 4)])
    *parts, x_in[1][2] = tie(parts + [x_in[1][2]])
    part = parts[0] + parts[1] + parts[2] + parts[3]
    part = jnp.concatenate([part[:256], part[512:]]) + other_device(part[256:], OTHER_CORE)
    kept = jnp.concatenate([part[:BLK], part[256:]])
    sent = part[BLK:]
    bases = (0, 1, 2, 2)
    y_in, z_out, z_in, gates = [], [], [], [[arrived], [], [], [], []]

    for s in range(n):
        packed = pack_y(s, tab, x_in[min(s, 2)], bases[s], sent if s == 1 else None)
        before = ([y_in[s - 1]] if s else []) + (z_in[s - 2][1:] if s > 1 else []) + gates[s]
        y_in.append(exchange_y(tie([packed], *before)[0]))
        if s == 1:
            got = lax.dynamic_index_in_dim(y_in[1][:, 16:], (1 - (front >> 3)) * 2 + (leaf >> 2), 0, keepdims=False)
            corner = jnp.concatenate([kept[BLK:, :BLK], kept[BLK:, BLK:]]) + got[2]
            part = kept[:BLK] + jnp.concatenate([got[0], got[1]], axis=1)
            near = jnp.stack([part, other_device(part, OTHER_CORE)])
            near = jnp.stack([near] + [shift_x(near, k, 0) for k in range(1, 4)])
            pairs = [(b, device_at(b % 8, b // 8)) for b in range(128)]
            moved = lax.ppermute(part, ("leaf", "front"), pairs)
            gates[3] += [near, moved]
        before = z_in[s - 1][1:] if s else []
        z_out.append(pack_z(s, tab, tie([y_in[s]], *before)[0] if before else y_in[s], moved if s == 2 else None))
        z_in.append([z_out[s][0]] + [shift_z(z_out[s][k], k) for k in range(1, 4)])

    columns_near = jnp.stack([jnp.concatenate([z_in[2][k][0, 8], z_in[2][k][1, 8]], axis=1) for k in range(4)])
    near_late, columns_late = tie([near, columns_near], z_out[n - 1][0])
    far = other_device(near_late, OTHER_Y_HI)
    columns_far = other_device(columns_late, OTHER_Y_LO)
    left = factors(tab, block_inv, corner, [near], [0], True)
    tile = accumulate(WHOLE[:3], tab, front_matrix, z_in[0] + z_in[1] + z_in[2])
    left = left + factors(tab, block_inv, corner, [far], [1], True)
    columns_far = tie([columns_far], left[2], tile)[0]
    right = factors(tab, block_inv, corner, [columns_near, columns_far], [0, 1], False)
    return accumulate(WHOLE[3:], tab, tile, z_in[3], left + right)


def solution(mesh):
    placed = (P("leaf", "front", None), P(), P("leaf", "front"), P())
    return jax.shard_map(
        per_device, mesh=mesh, in_specs=placed, out_specs=P("leaf", "front"), check_vma=False
    )
```

time: 1040 us -> 404 us (0.39)
  waiting for transfers between devices: 719 us -> 193 us
  matrix products: 134 us -> 0 us
  local copies, waits for them, and re-layouts: 131 us -> 11.5 us
  Pallas kernels: 0 us -> 108 us
  starting transfers between devices: 14 us -> 81.5 us
  other arithmetic: 23.3 us -> 6.18 us
  between operations: 13.5 us -> 0.81 us
    psum x4 -> x0, waiting for transfers between devices: 431 us -> none  [broadcast(): return lax.psum(jnp.where(mine, x, jnp.zeros_like(x)), axis)]
    all_to_all x2 -> x5, waiting for transfers between devices: 288 us -> 0.01 us  [the longest x4 0.01 us: exchange_y(): lax.all_to_all(a, ('leaf', 'front'), 0, 0, axis_index_groups=groups, tile...]
    ppermute x0 -> x34, waiting for transfers between devices: none -> 193 us  [the longest x17 104 us: shift_x(): return lax.ppermute(a, 'front', pairs)]
    dot_general x10 -> x0, matrix products: 134 us -> none  [the longest x1 45.1 us: per_device(): jnp.einsum('gpavb,gpu->uavb', widened, row_select, precision=highest)]
    pallas_call x0 -> x20, Pallas kernels: none -> 108 us  [the longest x14 51.7 us: call(): pl.pallas_call(kernel, out_shape=[jax.ShapeDtypeStruct(s, jnp.float32) fo...]
    reshape x4, local copies, waits for them, and re-layouts: 60.7 us -> 0.31 us  [the longest x3 0.24 us: tables(): t.reshape(-1)]
    ppermute x0 -> x34, starting transfers between devices: none -> 56.2 us  [the longest x12 27.8 us: shift_z(): lax.ppermute(a, 'leaf', [(leaf_at(l, z), leaf_at(l, z + dz)) for l in ran...]
    unnamed x11 -> x48, local copies, waits for them, and re-layouts: 31.6 us -> 6.61 us
  transfers between devices with their start and end apart: 6 -> 39, of which waited for: 6 -> 17; matrix products, arithmetic and copies ran while one was open for 1% -> 2% of each run, Pallas kernels for 0% -> 21%
where the time goes in v2:
time: 404 us; the launch traced here: 401 us
  waiting for transfers between devices  193 us (48%)
  Pallas kernels  108 us (27%)
  starting transfers between devices  81.5 us (20%)
  local copies, waits for them, and re-layouts  11.5 us (3%)
  other arithmetic  6.18 us (2%)
    ppermute x17, waiting for transfers between devices, shift_x(): return lax.ppermute(a, 'front', pairs)  104 us
    ppermute x12, waiting for transfers between devices, shift_z(): lax.ppermute(a, 'leaf', [(leaf_at(l, z), leaf_at(l, z + dz)) for l in ran...  85.9 us
    pallas_call x14, Pallas kernels, call(): pl.pallas_call(kernel, out_shape=[jax.ShapeDtypeStruct(s, jnp.float32) fo...  51.7 us
    pallas_call x2, Pallas kernels, accumulate(): pl.pallas_call(kernel, out_shape=jax.ShapeDtypeStruct(tile.shape, jnp.flo...  28.9 us
    ppermute x12, starting transfers between devices, shift_z(): lax.ppermute(a, 'leaf', [(leaf_at(l, z), leaf_at(l, z + dz)) for l in ran...  27.8 us
    ppermute x17, starting transfers between devices, shift_x(): return lax.ppermute(a, 'front', pairs)  23.6 us
    pallas_call x3, Pallas kernels, factors(): pl.pallas_call(kernel, out_shape=shapes, in_specs=[SMEM] + [vmem] * (2 +...  22 us
    all_to_all x4, starting transfers between devices, exchange_y(): lax.all_to_all(a, ('leaf', 'front'), 0, 0, axis_index_groups=groups, tile...  19.7 us
  transfers between devices with their start and end apart: 39, of which 17 were waited for; matrix products, arithmetic and copies ran while one was open for 2% of the time, Pallas kernels for 21%

profile of v2, /device:TPU:0, one launch (start us, length us, event | category | flops | bytes accessed | tf_op | source)
XLA Modules:
  0.0 401.0 jit_solution(12863401861699453837)
XLA Ops:
  1.5 3.9 pack_panel.1
  5.4 5.6 %all-to-all-start = ((f32[8,6,128,128]{3,2,1,0:T(8,128)}), f32[8,6,128,128]{3,2,1,0:T(8,128)}, u32[]{:S(2)}, u32[]{:S(2)}) async-start(f32[8,6,128,128]{3,2,1,0:T(8,128)} %pack_panel.1), calls=%async_computation | async-start | bytes 6291456 | tf_op jit(solution)/shard_map/all_to_all | solution.py:513
  30.5 8.7 %collective-permute-done.1.refs_2_.refs_3_ = f32[1,2,2,2,128,128]{5,4,3,2,1,0:T(8,128)} collective-permute-done((f32[1,2,2,2,128,128]{5,4,3,2,1,0:T(8,128)}, f32[1,2,2,2,128,128]{5,4,3,2,1,0:T(8,128)}, u32[]{:S(2)}, u32[]{:S(2)}) %collective-permute-start.1) | collective-permute-done | bytes 524320 | tf_op jit(solution)/shard_map/ppermute | solution.py:449
  39.3 12.2 %collective-permute-done.2.refs_3_.refs_4_ = f32[1,2,2,2,128,128]{5,4,3,2,1,0:T(8,128)} collective-permute-done((f32[1,2,2,2,128,128]{5,4,3,2,1,0:T(8,128)}, f32[1,2,2,2,128,128]{5,4,3,2,1,0:T(8,128)}, u32[]{:S(2)}, u32[]{:S(2)}) %collective-permute-start.2) | collective-permute-done | bytes 524320 | tf_op jit(solution)/shard_map/ppermute | solution.py:449
  51.5 4.4 %pack_y.4 = f32[4,16,128,128]{3,2,1,0:T(8,128)} custom-call(s32[1024]{0:T(1024)} %concatenate.30.refs_0_.tab, f32[1,2,2,2,128,128]{5,4,3,2,1,0:T(8,128)} %get-tuple-element.60.refs_1_, f32[1,2,2,2,128,128]{5,4,3,2,1,0:T(8,128)} %collective-permute-done.1.refs_2_.refs_3_, f32[1,2,2,2,128,128]{5,4,3,2,1,0:T(8,128)} %collective-permute-done.2.refs_3_.refs_4_, ...), custom_call_target="tpu_custom_call" | custom-call | flops 1000 | bytes 65536 | tf_op jit(solution)/shard_map/pack_y/pallas_call | solution.py:54
  55.9 4.9 %all-to-all-start.1 = ((f32[4,16,128,128]{3,2,1,0:T(8,128)}), f32[4,16,128,128]{3,2,1,0:T(8,128)}, u32[]{:S(2)}, u32[]{:S(2)}) async-start(f32[4,16,128,128]{3,2,1,0:T(8,128)} %pack_y.4), calls=%async_computation.1 | async-start | bytes 8388608 | tf_op jit(solution)/shard_map/all_to_all | solution.py:457
  70.0 5.5 %panel_part.1 = (f32[576,256]{1,0:T(8,128)}, f32[576,256]{1,0:T(8,128)}, f32[576,256]{1,0:T(8,128)}, f32[576,256]{1,0:T(8,128)}) custom-call(s32[384]{0:T(512)} %pad_add_fusion.flat, f32[2048,1024]{1,0:T(8,128)} %tile.3, f32[8,6,128,128]{3,2,1,0:T(8,128)} %all-to-all-done.arrived), custom_call_target="tpu_custom_call" | custom-call | flops 1000 | bytes 65536 | tf_op jit(solution)/shard_map/panel_part/pallas_call | solution.py:287
  75.6 5.2 %collective-permute-done.8.refs_2_.refs_3_ = f32[1,2,2,2,128,128]{5,4,3,2,1,0:T(8,128)S(1)} collective-permute-done((f32[1,2,2,2,128,128]{5,4,3,2,1,0:T(8,128)}, f32[1,2,2,2,128,128]{5,4,3,2,1,0:T(8,128)S(1)}, u32[]{:S(2)}, u32[]{:S(2)}) %collective-permute-start.8) | collective-permute-done | bytes 524320 | tf_op jit(solution)/shard_map/ppermute | solution.py:449
  87.0 34.0 %collective-permute-done.13.refs_3_.refs_4_ = f32[1,2,2,2,128,128]{5,4,3,2,1,0:T(8,128)S(1)} collective-permute-done((f32[1,2,2,2,128,128]{5,4,3,2,1,0:T(8,128)S(1)}, f32[1,2,2,2,128,128]{5,4,3,2,1,0:T(8,128)S(1)}, u32[]{:S(2)}, u32[]{:S(2)}) %collective-permute-start.13) | collective-permute-done | bytes 524320 | tf_op jit(solution)/shard_map/ppermute | solution.py:449
  125.9 4.3 %pack_y.5 = f32[4,19,128,128]{3,2,1,0:T(8,128)} custom-call(s32[1024]{0:T(1024)} %concatenate.30.refs_0_.tab, f32[1,2,2,2,128,128]{5,4,3,2,1,0:T(8,128)} %get-tuple-element.69.refs_1_, f32[1,2,2,2,128,128]{5,4,3,2,1,0:T(8,128)} %copy-done.9, f32[1,2,2,2,128,128]{5,4,3,2,1,0:T(8,128)} %copy-done.11, f32[1,2,2,2,128,128]{5,4,3,2,1,0:T(8,128)} %copy-done.10, ...), custom_call_target="tpu_custom_call" | custom-call | flops 1000 | bytes 65536 | tf_op jit(solution)/shard_map/pack_y/pallas_call | solution.py:54
  130.3 5.0 %all-to-all-start.2 = ((f32[4,19,128,128]{3,2,1,0:T(8,128)}), f32[4,19,128,128]{3,2,1,0:T(8,128)}, u32[]{:S(2)}, u32[]{:S(2)}) async-start(f32[4,19,128,128]{3,2,1,0:T(8,128)} %pack_y.5), calls=%async_computation.2 | async-start | bytes 9961472 | tf_op jit(solution)/shard_map/all_to_all | solution.py:457
  135.3 4.2 %pack_x.5 = (f32[2,2,2,2,128,128]{5,4,3,2,1,0:T(8,128)}, f32[2,2,2,2,128,128]{5,4,3,2,1,0:T(8,128)}, f32[2,2,2,2,128,128]{5,4,3,2,1,0:T(8,128)}, f32[2,2,2,2,128,128]{5,4,3,2,1,0:T(8,128)}) custom-call(s32[64]{0:T(128)} %concatenate.31.refs_0_, f32[2,128,4096]{2,1,0:T(8,128)} %bitcast.50, f32[3,8,2,128,128]{4,3,2,1,0:T(8,128)} %copy-done, ...), custom_call_target="tpu_custom_call" | custom-call | flops 1000 | bytes 65536 | tf_op jit(solution)/shard_map/pack_x/pallas_call | solution.py:54
  145.1 4.0 %pack_z.4 = (f32[2,8,128,128]{3,2,1,0:T(8,128)}, f32[2,8,128,128]{3,2,1,0:T(8,128)}, f32[2,8,128,128]{3,2,1,0:T(8,128)}, f32[2,8,128,128]{3,2,1,0:T(8,128)}) custom-call(s32[1024]{0:T(1024)} %concatenate.30.refs_0_.tab, f32[4,16,128,128]{3,2,1,0:T(8,128)} %all-to-all-done.1.refs_1_), custom_call_target="tpu_custom_call" | custom-call | flops 1000 | bytes 65536 | tf_op jit(solution)/shard_map/pack_z/pallas_call | solution.py:54
  153.8 12.5 %collective-permute-done.18.refs_2_ = f32[2,2,2,2,128,128]{5,4,3,2,1,0:T(8,128)S(1)} collective-permute-done((f32[2,2,2,2,128,128]{5,4,3,2,1,0:T(8,128)}, f32[2,2,2,2,128,128]{5,4,3,2,1,0:T(8,128)S(1)}, u32[]{:S(2)}, u32[]{:S(2)}) %collective-permute-start.18) | collective-permute-done | bytes 1048608 | tf_op jit(solution)/shard_map/ppermute | solution.py:449
  169.8 19.8 %collective-permute-done.19.refs_3_ = f32[2,2,2,2,128,128]{5,4,3,2,1,0:T(8,128)S(1)} collective-permute-done((f32[2,2,2,2,128,128]{5,4,3,2,1,0:T(8,128)}, f32[2,2,2,2,128,128]{5,4,3,2,1,0:T(8,128)S(1)}, u32[]{:S(2)}, u32[]{:S(2)}) %collective-permute-start.19) | collective-permute-done | bytes 1048608 | tf_op jit(solution)/shard_map/ppermute | solution.py:449
  193.9 5.7 %collective-permute-done.5.refs_2_ = f32[2,8,128,128]{3,2,1,0:T(8,128)} collective-permute-done((f32[2,8,128,128]{3,2,1,0:T(8,128)}, f32[2,8,128,128]{3,2,1,0:T(8,128)}, u32[]{:S(2)}, u32[]{:S(2)}) %collective-permute-start.5) | collective-permute-done | bytes 1048608 | tf_op jit(solution)/shard_map/ppermute | solution.py:461
  199.6 4.9 %all-to-all-start.3 = ((f32[4,16,128,128]{3,2,1,0:T(8,128)}), f32[4,16,128,128]{3,2,1,0:T(8,128)}, u32[]{:S(2)}, u32[]{:S(2)}) async-start(f32[4,16,128,128]{3,2,1,0:T(8,128)} %pack_y.6), calls=%async_computation.3 | async-start | bytes 8388608 | tf_op jit(solution)/shard_map/all_to_all | solution.py:457
  204.5 4.1 %pack_z.5 = (f32[2,8,128,128]{3,2,1,0:T(8,128)}, f32[2,8,128,128]{3,2,1,0:T(8,128)}, f32[2,8,128,128]{3,2,1,0:T(8,128)}, f32[2,8,128,128]{3,2,1,0:T(8,128)}) custom-call(s32[1024]{0:T(1024)} %concatenate.30.refs_0_.tab, f32[4,19,128,128]{3,2,1,0:T(8,128)} %all-to-all-done.2.refs_1_), custom_call_target="tpu_custom_call" | custom-call | flops 1000 | bytes 65536 | tf_op jit(solution)/shard_map/pack_z/pallas_call | solution.py:54
  221.1 8.8 %collective-permute-done.27 = f32[2,128,256]{2,1,0:T(8,128)S(1)} collective-permute-done((f32[2,128,256]{2,1,0:T(8,128)S(1)}, f32[2,128,256]{2,1,0:T(8,128)S(1)}, u32[]{:S(2)}, u32[]{:S(2)}) %collective-permute-start.27) | collective-permute-done | bytes 262176 | tf_op jit(solution)/shard_map/ppermute | solution.py:449
  236.8 26.0 %collective-permute-done.16.refs_6_ = f32[2,8,128,128]{3,2,1,0:T(8,128)} collective-permute-done((f32[2,8,128,128]{3,2,1,0:T(8,128)}, f32[2,8,128,128]{3,2,1,0:T(8,128)}, u32[]{:S(2)}, u32[]{:S(2)}) %collective-permute-start.16) | collective-permute-done | bytes 1048608 | tf_op jit(solution)/shard_map/ppermute | solution.py:461
  262.8 4.9 %all-to-all-start.4 = ((f32[4,16,128,128]{3,2,1,0:T(8,128)}), f32[4,16,128,128]{3,2,1,0:T(8,128)}, u32[]{:S(2)}, u32[]{:S(2)}) async-start(f32[4,16,128,128]{3,2,1,0:T(8,128)} %pack_y.7), calls=%async_computation.4 | async-start | bytes 8388608 | tf_op jit(solution)/shard_map/all_to_all | solution.py:457
  267.7 4.1 %pack_z.6 = (f32[2,9,128,128]{3,2,1,0:T(8,128)}, f32[2,9,128,128]{3,2,1,0:T(8,128)}, f32[2,9,128,128]{3,2,1,0:T(8,128)}, f32[2,9,128,128]{3,2,1,0:T(8,128)}) custom-call(s32[1024]{0:T(1024)} %concatenate.30.refs_0_.tab, f32[4,16,128,128]{3,2,1,0:T(8,128)} %all-to-all-done.3.refs_1_, f32[128,256]{1,0:T(8,128)} %copy-done.21), custom_call_target="tpu_custom_call" | custom-call | flops 1000 | bytes 65536 | tf_op jit(solution)/shard_map/pack_z/pallas_call | solution.py:54
  271.8 4.9 %collective-permute-start.22 = (f32[2,9,128,128]{3,2,1,0:T(8,128)}, f32[2,9,128,128]{3,2,1,0:T(8,128)S(1)}, u32[]{:S(2)}, u32[]{:S(2)}) collective-permute-start(f32[2,9,128,128]{3,2,1,0:T(8,128)} %get-tuple-element.99), channel_id=1, source_target_pairs={{0,16},{16,32},{32,48},{48,0},{64,80},{80,96},{96,112},{112,64},{1... | collective-permute-start | bytes 3538952 | tf_op jit(solution)/shard_map/ppermute | solution.py:461
  280.3 23.1 %collective-permute-done.22.refs_9_ = f32[2,9,128,128]{3,2,1,0:T(8,128)S(1)} collective-permute-done((f32[2,9,128,128]{3,2,1,0:T(8,128)}, f32[2,9,128,128]{3,2,1,0:T(8,128)S(1)}, u32[]{:S(2)}, u32[]{:S(2)}) %collective-permute-start.22) | collective-permute-done | bytes 1179680 | tf_op jit(solution)/shard_map/ppermute | solution.py:461
  303.5 23.2 %collective-permute-done.23.refs_10_ = f32[2,9,128,128]{3,2,1,0:T(8,128)S(1)} collective-permute-done((f32[2,9,128,128]{3,2,1,0:T(8,128)}, f32[2,9,128,128]{3,2,1,0:T(8,128)S(1)}, u32[]{:S(2)}, u32[]{:S(2)}) %collective-permute-start.23) | collective-permute-done | bytes 1179680 | tf_op jit(solution)/shard_map/ppermute | solution.py:461
  336.9 4.2 %collective-permute-start.30 = (f32[2,8,128,128]{3,2,1,0:T(8,128)}, f32[2,8,128,128]{3,2,1,0:T(8,128)}, u32[]{:S(2)}, u32[]{:S(2)}) collective-permute-start(f32[2,8,128,128]{3,2,1,0:T(8,128)} %get-tuple-element.106), channel_id=1, source_target_pairs={{0,32},{16,48},{32,0},{48,16},{64,96},{80,112},{96,64},{112,80},{1... | collective-permute-start | bytes 3145736 | tf_op jit(solution)/shard_map/ppermute | solution.py:461
  343.5 7.4 %factors.3 = (bf16[1024,768]{1,0:T(8,128)(2,1)}, f32[1024,256]{1,0:T(8,128)}) custom-call(s32[1024]{0:T(1024)} %concatenate.30.refs_0_.tab, f32[2,128,128]{2,1,0:T(8,128)} %inv.5, f32[128,128]{1,0:T(8,128)} %fusion.corner, f32[4,2,128,256]{3,2,1,0:T(8,128)} %copy-done.1), custom_call_target="tpu_custom_call" | custom-call | flops 1000 | bytes 65536 | tf_op jit(solution)/shard_map/factors/pallas_call | solution.py:342
  350.9 13.5 %accumulate.1.tile = f32[2048,1024]{1,0:T(8,128)} custom-call(s32[1024]{0:T(1024)} %concatenate.30.refs_0_.tab, f32[2048,1024]{1,0:T(8,128)} %tile.3, f32[2,8,128,128]{3,2,1,0:T(8,128)} %get-tuple-element.65.refs_0_, f32[2,8,128,128]{3,2,1,0:T(8,128)} %collective-permute-done.4.refs_1_, f32[2,8,128,128]{3,2,1,0:T(8,128)} %collective-permute-done.5.refs_2_, ...), custom_call_target="tpu_custom_call" | custom-call | flops 1000 | bytes 65536 | tf_op jit(solution)/shard_map/accumulate/pallas_call | solution.py:429
  364.4 7.5 %factors.4 = (bf16[1024,768]{1,0:T(8,128)(2,1)}, f32[1024,256]{1,0:T(8,128)}) custom-call(s32[1024]{0:T(1024)} %concatenate.30.refs_0_.tab, f32[2,128,128]{2,1,0:T(8,128)} %inv.5, f32[128,128]{1,0:T(8,128)} %fusion.corner, f32[4,2,128,256]{3,2,1,0:T(8,128)} %collective-permute-done.32.refs_0_), custom_call_target="tpu_custom_call" | custom-call | flops 1000 | bytes 65536 | tf_op jit(solution)/shard_map/factors/pallas_call | solution.py:342
  372.7 7.1 %factors.5.refs_8_ = bf16[1024,768]{1,0:T(8,128)(2,1)} custom-call(s32[1024]{0:T(1024)} %concatenate.30.refs_0_.tab, f32[2,128,128]{2,1,0:T(8,128)} %inv.5, f32[128,128]{1,0:T(8,128)} %fusion.corner, f32[4,128,256]{2,1,0:T(8,128)} %copy-done.8, f32[4,128,256]{2,1,0:T(8,128)} %copy-done.20), custom_call_target="tpu_custom_call" | custom-call | flops 1000 | bytes 65536 | tf_op jit(solution)/shard_map/factors/pallas_call | solution.py:342
  379.8 5.7 %collective-permute-done.30.refs_2_ = f32[2,8,128,128]{3,2,1,0:T(8,128)} collective-permute-done((f32[2,8,128,128]{3,2,1,0:T(8,128)}, f32[2,8,128,128]{3,2,1,0:T(8,128)}, u32[]{:S(2)}, u32[]{:S(2)}) %collective-permute-start.30) | collective-permute-done | bytes 1048608 | tf_op jit(solution)/shard_map/ppermute | solution.py:461
  385.5 15.4 %final.1 = f32[2048,1024]{1,0:T(8,128)} custom-call(s32[1024]{0:T(1024)} %concatenate.30.refs_0_.tab, f32[2048,1024]{1,0:T(8,128)} %accumulate.1.tile, f32[2,8,128,128]{3,2,1,0:T(8,128)} %get-tuple-element.104.refs_0_, f32[2,8,128,128]{3,2,1,0:T(8,128)} %copy-done.19, f32[2,8,128,128]{3,2,1,0:T(8,128)} %collective-permute-done.30.refs_2_, ...), custom_call_target="tpu_custom_call" | custom-call | flops 1000 | bytes 65536 | tf_op jit(solution)/shard_map/final/pallas_call | solution.py:429
  (163 shorter events, 95.6 us)
Async XLA Ops:
  5.4 50.5 %all-to-all-start = ((f32[8,6,128,128]{3,2,1,0:T(8,128)}), f32[8,6,128,128]{3,2,1,0:T(8,128)}, u32[]{:S(2)}, u32[]{:S(2)}) async-start(f32[8,6,128,128]{3,2,1,0:T(8,128)} %pack_panel.1), calls=%async_computation | async-start | bytes 6291456 | tf_op jit(solution)/shard_map/all_to_all | solution.py:513
  17.9 42.8 %collective-permute-start.7 = (f32[3,8,2,128,128]{4,3,2,1,0:T(8,128)}, f32[3,8,2,128,128]{4,3,2,1,0:T(8,128)S(1)}, u32[]{:S(2)}, u32[]{:S(2)}) collective-permute-start(f32[3,8,2,128,128]{4,3,2,1,0:T(8,128)} %pack_core.3), channel_id=1, source_target_pairs={{0,1},{1,0},{2,3},{3,2},{4,5},{5,4},{6,7},{7,6},{8,9},{9,8},{10,11... | collective-permute-start | bytes 9437192 | tf_op jit(solution)/shard_map/ppermute | solution.py:449
  23.7 15.5 %collective-permute-start.1 = (f32[1,2,2,2,128,128]{5,4,3,2,1,0:T(8,128)}, f32[1,2,2,2,128,128]{5,4,3,2,1,0:T(8,128)}, u32[]{:S(2)}, u32[]{:S(2)}) collective-permute-start(f32[1,2,2,2,128,128]{5,4,3,2,1,0:T(8,128)} %get-tuple-element.61), channel_id=1, source_target_pairs={{0,2},{1,3},{2,4},{3,5},{4,6},{5,7},{6,0},{7,1},{8,10},{9,11},{10,... | collective-permute-start | bytes 1572872 | tf_op jit(solution)/shard_map/ppermute | solution.py:449
  25.3 26.2 %collective-permute-start.2 = (f32[1,2,2,2,128,128]{5,4,3,2,1,0:T(8,128)}, f32[1,2,2,2,128,128]{5,4,3,2,1,0:T(8,128)}, u32[]{:S(2)}, u32[]{:S(2)}) collective-permute-start(f32[1,2,2,2,128,128]{5,4,3,2,1,0:T(8,128)} %get-tuple-element.62), channel_id=1, source_target_pairs={{0,4},{1,5},{2,6},{3,7},{4,0},{5,1},{6,2},{7,3},{8,12},{9,13},{10,... | collective-permute-start | bytes 1572872 | tf_op jit(solution)/shard_map/ppermute | solution.py:449
  28.0 23.5 %collective-permute-start.3 = (f32[1,2,2,2,128,128]{5,4,3,2,1,0:T(8,128)}, f32[1,2,2,2,128,128]{5,4,3,2,1,0:T(8,128)}, u32[]{:S(2)}, u32[]{:S(2)}) collective-permute-start(f32[1,2,2,2,128,128]{5,4,3,2,1,0:T(8,128)} %get-tuple-element.63), channel_id=1, source_target_pairs={{0,6},{1,7},{2,0},{3,1},{4,2},{5,3},{6,4},{7,5},{8,14},{9,15},{10,... | collective-permute-start | bytes 1572872 | tf_op jit(solution)/shard_map/ppermute | solution.py:449
  55.9 74.4 %all-to-all-start.1 = ((f32[4,16,128,128]{3,2,1,0:T(8,128)}), f32[4,16,128,128]{3,2,1,0:T(8,128)}, u32[]{:S(2)}, u32[]{:S(2)}) async-start(f32[4,16,128,128]{3,2,1,0:T(8,128)} %pack_y.4), calls=%async_computation.1 | async-start | bytes 8388608 | tf_op jit(solution)/shard_map/all_to_all | solution.py:457
  66.0 14.7 %collective-permute-start.8 = (f32[1,2,2,2,128,128]{5,4,3,2,1,0:T(8,128)}, f32[1,2,2,2,128,128]{5,4,3,2,1,0:T(8,128)S(1)}, u32[]{:S(2)}, u32[]{:S(2)}) collective-permute-start(f32[1,2,2,2,128,128]{5,4,3,2,1,0:T(8,128)} %get-tuple-element.70), channel_id=1, source_target_pairs={{0,2},{1,3},{2,4},{3,5},{4,6},{5,7},{6,0},{7,1},{8,10},{9,11},{10,... | collective-permute-start | bytes 1572872 | tf_op jit(solution)/shard_map/ppermute | solution.py:449
  80.8 40.2 %collective-permute-start.10 = (f32[576,256]{1,0:T(8,128)}, f32[576,256]{1,0:T(8,128)S(1)}, u32[]{:S(2)}, u32[]{:S(2)}) collective-permute-start(f32[576,256]{1,0:T(8,128)} %get-tuple-element.77), channel_id=1, source_target_pairs={{0,2},{1,3},{2,4},{3,5},{4,6},{5,7},{6,0},{7,1},{8,10},{9,11},{10,... | collective-permute-start | bytes 1769480 | tf_op jit(solution)/shard_map/ppermute | solution.py:449
  81.9 39.1 %collective-permute-start.11 = (f32[576,256]{1,0:T(8,128)}, f32[576,256]{1,0:T(8,128)S(1)}, u32[]{:S(2)}, u32[]{:S(2)}) collective-permute-start(f32[576,256]{1,0:T(8,128)} %get-tuple-element.78), channel_id=1, source_target_pairs={{0,4},{1,5},{2,6},{3,7},{4,0},{5,1},{6,2},{7,3},{8,12},{9,13},{10,... | collective-permute-start | bytes 1769480 | tf_op jit(solution)/shard_map/ppermute | solution.py:449
  85.3 35.7 %collective-permute-start.12 = (f32[576,256]{1,0:T(8,128)}, f32[576,256]{1,0:T(8,128)S(1)}, u32[]{:S(2)}, u32[]{:S(2)}) collective-permute-start(f32[576,256]{1,0:T(8,128)} %get-tuple-element.79), channel_id=1, source_target_pairs={{0,6},{1,7},{2,0},{3,1},{4,2},{5,3},{6,4},{7,5},{8,14},{9,15},{10,... | collective-permute-start | bytes 1769480 | tf_op jit(solution)/shard_map/ppermute | solution.py:449
  86.3 34.6 %collective-permute-start.13 = (f32[1,2,2,2,128,128]{5,4,3,2,1,0:T(8,128)S(1)}, f32[1,2,2,2,128,128]{5,4,3,2,1,0:T(8,128)S(1)}, u32[]{:S(2)}, u32[]{:S(2)}) collective-permute-start(f32[1,2,2,2,128,128]{5,4,3,2,1,0:T(8,128)S(1)} %copy-done.23), channel_id=1, source_target_pairs={{0,4},{1,5},{2,6},{3,7},{4,0},{5,1},{6,2},{7,3},{8,12},{9,13},{10,... | collective-permute-start | bytes 1572872 | tf_op jit(solution)/shard_map/ppermute | solution.py:449
  130.3 69.3 %all-to-all-start.2 = ((f32[4,19,128,128]{3,2,1,0:T(8,128)}), f32[4,19,128,128]{3,2,1,0:T(8,128)}, u32[]{:S(2)}, u32[]{:S(2)}) async-start(f32[4,19,128,128]{3,2,1,0:T(8,128)} %pack_y.5), calls=%async_computation.2 | async-start | bytes 9961472 | tf_op jit(solution)/shard_map/all_to_all | solution.py:457
  139.5 26.7 %collective-permute-start.18 = (f32[2,2,2,2,128,128]{5,4,3,2,1,0:T(8,128)}, f32[2,2,2,2,128,128]{5,4,3,2,1,0:T(8,128)S(1)}, u32[]{:S(2)}, u32[]{:S(2)}) collective-permute-start(f32[2,2,2,2,128,128]{5,4,3,2,1,0:T(8,128)} %get-tuple-element.93), channel_id=1, source_target_pairs={{0,2},{1,3},{2,4},{3,5},{4,6},{5,7},{6,0},{7,1},{8,10},{9,11},{10,... | collective-permute-start | bytes 3145736 | tf_op jit(solution)/shard_map/ppermute | solution.py:449
  142.3 47.3 %collective-permute-start.19 = (f32[2,2,2,2,128,128]{5,4,3,2,1,0:T(8,128)}, f32[2,2,2,2,128,128]{5,4,3,2,1,0:T(8,128)S(1)}, u32[]{:S(2)}, u32[]{:S(2)}) collective-permute-start(f32[2,2,2,2,128,128]{5,4,3,2,1,0:T(8,128)} %get-tuple-element.94), channel_id=1, source_target_pairs={{0,4},{1,5},{2,6},{3,7},{4,0},{5,1},{6,2},{7,3},{8,12},{9,13},{10,... | collective-permute-start | bytes 3145736 | tf_op jit(solution)/shard_map/ppermute | solution.py:449
  143.4 46.2 %collective-permute-start.20 = (f32[2,2,2,2,128,128]{5,4,3,2,1,0:T(8,128)}, f32[2,2,2,2,128,128]{5,4,3,2,1,0:T(8,128)S(1)}, u32[]{:S(2)}, u32[]{:S(2)}) collective-permute-start(f32[2,2,2,2,128,128]{5,4,3,2,1,0:T(8,128)} %get-tuple-element.95), channel_id=1, source_target_pairs={{0,6},{1,7},{2,0},{3,1},{4,2},{5,3},{6,4},{7,5},{8,14},{9,15},{10,... | collective-permute-start | bytes 3145736 | tf_op jit(solution)/shard_map/ppermute | solution.py:449
  149.1 44.8 %collective-permute-start.4 = (f32[2,8,128,128]{3,2,1,0:T(8,128)}, f32[2,8,128,128]{3,2,1,0:T(8,128)}, u32[]{:S(2)}, u32[]{:S(2)}) collective-permute-start(f32[2,8,128,128]{3,2,1,0:T(8,128)} %get-tuple-element.66), channel_id=1, source_target_pairs={{0,16},{16,32},{32,48},{48,0},{64,80},{80,96},{96,112},{112,64},{1... | collective-permute-start | bytes 3145736 | tf_op jit(solution)/shard_map/ppermute | solution.py:461
  151.6 48.0 %collective-permute-start.5 = (f32[2,8,128,128]{3,2,1,0:T(8,128)}, f32[2,8,128,128]{3,2,1,0:T(8,128)}, u32[]{:S(2)}, u32[]{:S(2)}) collective-permute-start(f32[2,8,128,128]{3,2,1,0:T(8,128)} %get-tuple-element.67), channel_id=1, source_target_pairs={{0,32},{16,48},{32,0},{48,16},{64,96},{80,112},{96,64},{112,80},{1... | collective-permute-start | bytes 3145736 | tf_op jit(solution)/shard_map/ppermute | solution.py:461
  166.3 33.3 %collective-permute-start.6 = (f32[2,8,128,128]{3,2,1,0:T(8,128)}, f32[2,8,128,128]{3,2,1,0:T(8,128)}, u32[]{:S(2)}, u32[]{:S(2)}) collective-permute-start(f32[2,8,128,128]{3,2,1,0:T(8,128)} %get-tuple-element.68), channel_id=1, source_target_pairs={{0,48},{16,0},{32,16},{48,32},{64,112},{80,64},{96,80},{112,96},{1... | collective-permute-start | bytes 3145736 | tf_op jit(solution)/shard_map/ppermute | solution.py:461
  199.6 63.2 %all-to-all-start.3 = ((f32[4,16,128,128]{3,2,1,0:T(8,128)}), f32[4,16,128,128]{3,2,1,0:T(8,128)}, u32[]{:S(2)}, u32[]{:S(2)}) async-start(f32[4,16,128,128]{3,2,1,0:T(8,128)} %pack_y.6), calls=%async_computation.3 | async-start | bytes 8388608 | tf_op jit(solution)/shard_map/all_to_all | solution.py:457
  208.6 28.1 %collective-permute-start.15 = (f32[2,8,128,128]{3,2,1,0:T(8,128)}, f32[2,8,128,128]{3,2,1,0:T(8,128)S(1)}, u32[]{:S(2)}, u32[]{:S(2)}) collective-permute-start(f32[2,8,128,128]{3,2,1,0:T(8,128)} %get-tuple-element.89), channel_id=1, source_target_pairs={{0,16},{16,32},{32,48},{48,0},{64,80},{80,96},{96,112},{112,64},{1... | collective-permute-start | bytes 3145736 | tf_op jit(solution)/shard_map/ppermute | solution.py:461
  212.2 50.5 %collective-permute-start.16 = (f32[2,8,128,128]{3,2,1,0:T(8,128)}, f32[2,8,128,128]{3,2,1,0:T(8,128)}, u32[]{:S(2)}, u32[]{:S(2)}) collective-permute-start(f32[2,8,128,128]{3,2,1,0:T(8,128)} %get-tuple-element.90), channel_id=1, source_target_pairs={{0,32},{16,48},{32,0},{48,16},{64,96},{80,112},{96,64},{112,80},{1... | collective-permute-start | bytes 3145736 | tf_op jit(solution)/shard_map/ppermute | solution.py:461
  213.0 49.8 %collective-permute-start.17 = (f32[2,8,128,128]{3,2,1,0:T(8,128)}, f32[2,8,128,128]{3,2,1,0:T(8,128)}, u32[]{:S(2)}, u32[]{:S(2)}) collective-permute-start(f32[2,8,128,128]{3,2,1,0:T(8,128)} %get-tuple-element.91), channel_id=1, source_target_pairs={{0,48},{16,0},{32,16},{48,32},{64,112},{80,64},{96,80},{112,96},{1... | collective-permute-start | bytes 3145736 | tf_op jit(solution)/shard_map/ppermute | solution.py:461
  219.5 15.0 %collective-permute-start.26 = (f32[2,128,256]{2,1,0:T(8,128)S(1)}, f32[2,128,256]{2,1,0:T(8,128)S(1)}, u32[]{:S(2)}, u32[]{:S(2)}) collective-permute-start(f32[2,128,256]{2,1,0:T(8,128)S(1)} %get-tuple-element.132), channel_id=1, source_target_pairs={{0,2},{1,3},{2,4},{3,5},{4,6},{5,7},{6,0},{7,1},{8,10},{9,11},{10,... | collective-permute-start | bytes 786440 | tf_op jit(solution)/shard_map/ppermute | solution.py:449
  262.8 67.2 %all-to-all-start.4 = ((f32[4,16,128,128]{3,2,1,0:T(8,128)}), f32[4,16,128,128]{3,2,1,0:T(8,128)}, u32[]{:S(2)}, u32[]{:S(2)}) async-start(f32[4,16,128,128]{3,2,1,0:T(8,128)} %pack_y.7), calls=%async_computation.4 | async-start | bytes 8388608 | tf_op jit(solution)/shard_map/all_to_all | solution.py:457
  271.8 31.6 %collective-permute-start.22 = (f32[2,9,128,128]{3,2,1,0:T(8,128)}, f32[2,9,128,128]{3,2,1,0:T(8,128)S(1)}, u32[]{:S(2)}, u32[]{:S(2)}) collective-permute-start(f32[2,9,128,128]{3,2,1,0:T(8,128)} %get-tuple-element.99), channel_id=1, source_target_pairs={{0,16},{16,32},{32,48},{48,0},{64,80},{80,96},{96,112},{112,64},{1... | collective-permute-start | bytes 3538952 | tf_op jit(solution)/shard_map/ppermute | solution.py:461
  276.7 49.9 %collective-permute-start.23 = (f32[2,9,128,128]{3,2,1,0:T(8,128)}, f32[2,9,128,128]{3,2,1,0:T(8,128)S(1)}, u32[]{:S(2)}, u32[]{:S(2)}) collective-permute-start(f32[2,9,128,128]{3,2,1,0:T(8,128)} %get-tuple-element.100), channel_id=1, source_target_pairs={{0,32},{16,48},{32,0},{48,16},{64,96},{80,112},{96,64},{112,80},{1... | collective-permute-start | bytes 3538952 | tf_op jit(solution)/shard_map/ppermute | solution.py:461
  276.7 52.2 %collective-permute-start.24 = (f32[2,9,128,128]{3,2,1,0:T(8,128)}, f32[2,9,128,128]{3,2,1,0:T(8,128)S(1)}, u32[]{:S(2)}, u32[]{:S(2)}) collective-permute-start(f32[2,9,128,128]{3,2,1,0:T(8,128)} %get-tuple-element.101), channel_id=1, source_target_pairs={{0,48},{16,0},{32,16},{48,32},{64,112},{80,64},{96,80},{112,96},{1... | collective-permute-start | bytes 3538952 | tf_op jit(solution)/shard_map/ppermute | solution.py:461
  332.8 31.5 %collective-permute-start.32 = (f32[4,2,128,256]{3,2,1,0:T(8,128)S(1)}, f32[4,2,128,256]{3,2,1,0:T(8,128)}, u32[]{:S(2)}, u32[]{:S(2)}) collective-permute-start(f32[4,2,128,256]{3,2,1,0:T(8,128)S(1)} %pad_maximum_fusion.refs_0_), channel_id=1, source_target_pairs={{0,8},{1,9},{2,10},{3,11},{4,12},{5,13},{6,14},{7,15},{8,0},{9,1},... | collective-permute-start | bytes 3145736 | tf_op jit(solution)/shard_map/ppermute | solution.py:469
  335.9 43.8 %collective-permute-start.29 = (f32[2,8,128,128]{3,2,1,0:T(8,128)}, f32[2,8,128,128]{3,2,1,0:T(8,128)S(1)}, u32[]{:S(2)}, u32[]{:S(2)}) collective-permute-start(f32[2,8,128,128]{3,2,1,0:T(8,128)} %get-tuple-element.105), channel_id=1, source_target_pairs={{0,16},{16,32},{32,48},{48,0},{64,80},{80,96},{96,112},{112,64},{1... | collective-permute-start | bytes 3145736 | tf_op jit(solution)/shard_map/ppermute | solution.py:461
  336.9 48.6 %collective-permute-start.30 = (f32[2,8,128,128]{3,2,1,0:T(8,128)}, f32[2,8,128,128]{3,2,1,0:T(8,128)}, u32[]{:S(2)}, u32[]{:S(2)}) collective-permute-start(f32[2,8,128,128]{3,2,1,0:T(8,128)} %get-tuple-element.106), channel_id=1, source_target_pairs={{0,32},{16,48},{32,0},{48,16},{64,96},{80,112},{96,64},{112,80},{1... | collective-permute-start | bytes 3145736 | tf_op jit(solution)/shard_map/ppermute | solution.py:461
  341.0 44.4 %collective-permute-start.31 = (f32[2,8,128,128]{3,2,1,0:T(8,128)}, f32[2,8,128,128]{3,2,1,0:T(8,128)}, u32[]{:S(2)}, u32[]{:S(2)}) collective-permute-start(f32[2,8,128,128]{3,2,1,0:T(8,128)} %get-tuple-element.107), channel_id=1, source_target_pairs={{0,48},{16,0},{32,16},{48,32},{64,112},{80,64},{96,80},{112,96},{1... | collective-permute-start | bytes 3145736 | tf_op jit(solution)/shard_map/ppermute | solution.py:461
  341.0 30.8 %collective-permute-start.33 = (f32[4,128,256]{2,1,0:T(8,128)S(1)}, f32[4,128,256]{2,1,0:T(8,128)S(1)}, u32[]{:S(2)}, u32[]{:S(2)}) collective-permute-start(f32[4,128,256]{2,1,0:T(8,128)S(1)} %pad_maximum_fusion.1.refs_0_), channel_id=1, source_target_pairs={{0,64},{1,65},{2,66},{3,67},{4,68},{5,69},{6,70},{7,71},{8,72},{9,... | collective-permute-start | bytes 1572872 | tf_op jit(solution)/shard_map/ppermute | solution.py:469
  (31 other events, 449.8 us)

commit v3 on v2

--- a/solution.py
+++ b/solution.py
@@ -218,14 +218,14 @@
 
 
 def panel_part(flat, front_tile, arrived):
-    def kernel(flat, tile, arrived, o0, o1, o2, o3, total, held, sem, tile_sem):
+    def kernel(flat, tile, arrived, o0, o1, total, held, sem, tile_sem):
         leaf, front = flat[256], flat[257]
         y_hi, x, core = front >> 3, (front >> 1) & 3, front & 1
         come = copy(arrived, held, sem)
         come.start()
 
         def place(u):
-            return (((u >> 1) & 3) - x) & 3, pl.ds(pl.multiple_of((((u & 1) ^ core) * 2 + ((u >> 3) ^ y_hi)) * BLK, BLK), BLK)
+            return (u & 1) ^ core, (((u >> 1) & 3) - x) & 3, pl.ds(pl.multiple_of(((u >> 3) ^ y_hi) * BLK, BLK), BLK)
 
         def rows(act):
             def one(u, carry):
@@ -247,16 +247,16 @@
 
         @pl.when(front == 0)
         def _():
-            for k in range(4):
+            for k in range(8):
                 for h in range(2):
-                    total[k, pl.ds(512, 64), pl.ds(h * BLK, BLK)] = held[0, 5, pl.ds(h * 64, 64)]
+                    total[k // 4, k % 4, pl.ds(256, 64), pl.ds(h * BLK, BLK)] = held[0, 5, pl.ds(h * 64, 64)]
 
             def corner(g, carry):
                 @pl.when((flat[g * UB] == 0) & (flat[g * UB + 1] == 1))
                 def _():
-                    for k in range(4):
+                    for k in range(8):
                         for h in range(2):
-                            total[k, pl.ds(512, 64), pl.ds(h * BLK, BLK)] += held[g, 4, pl.ds(h * 64, 64)]
+                            total[k // 4, k % 4, pl.ds(256, 64), pl.ds(h * BLK, BLK)] += held[g, 4, pl.ds(h * 64, 64)]
 
                 return carry
 
@@ -268,29 +268,29 @@
 
             @pl.when((parent >> 4) == leaf)
             def _():
-                k, at = place(parent & 15)
+                other, k, at = place(parent & 15)
                 for v in range(NPAN):
                     @pl.when((flat[g * UB] == v) | (flat[g * UB + 1] == v))
                     def _():
-                        total[k, at, pl.ds(v * BLK, BLK)] += held[g, r * NPAN + v]
+                        total[other, k, at, pl.ds(v * BLK, BLK)] += held[g, r * NPAN + v]
 
             return carry
 
         lax.fori_loop(0, 16, add, 0)
-        out = [copy(total.at[k], o, sem) for k, o in enumerate((o0, o1, o2, o3))]
+        out = [copy(total.at[k], o, sem) for k, o in enumerate((o0, o1))]
         for o in out:
             o.start()
         for o in out:
             o.wait()
 
-    block = (4 * BLK + 64, NPAN * BLK)
+    block = (4, 2 * BLK + 64, NPAN * BLK)
     return pl.pallas_call(
         kernel,
-        out_shape=[jax.ShapeDtypeStruct(block, jnp.float32)] * 4,
+        out_shape=[jax.ShapeDtypeStruct(block, jnp.float32)] * 2,
         in_specs=[SMEM, HBM, HBM],
-        out_specs=[HBM] * 4,
+        out_specs=[HBM] * 2,
         scratch_shapes=[
-            pltpu.VMEM((4,) + block, jnp.float32),
+            pltpu.VMEM((2,) + block, jnp.float32),
             pltpu.VMEM((8, 6, BLK, BLK), jnp.float32),
             pltpu.SemaphoreType.DMA(()),
             pltpu.SemaphoreType.DMA(()),
@@ -518,19 +518,22 @@
     x_in = [[outs[0]] + [shift_x(outs[k], k, 0) for k in range(1, 4)]]
     outs = pack_x(1, 2, meta, child, rest, 1, x_in[0][1:])
     x_in.append([outs[0]] + [shift_x(outs[k], k, 0) for k in range(1, 4)])
-    parts = panel_part(tie([flat], outs[0])[0], front_matrix, arrived)
+    mine, others = panel_part(tie([flat], outs[0])[0], front_matrix, arrived)
+    mine = mine + other_device(others, OTHER_CORE)
+    parts = [mine[k] for k in range(4)]
     parts = [parts[0]] + [shift_x(a, k + 1, 0) for k, a in enumerate(tie(parts[1:], x_in[1][1], x_in[1][3]))]
+    *parts, x_in[1][2] = tie(parts + [x_in[1][2]])
     outs = pack_x(2, n, meta, child, rest, 1, x_in[1][1:] + parts[1:])
     x_in.append([outs[0]] + [shift_x(outs[k], k, 0) for k in range(1, 4)])
-    *parts, x_in[1][2] = tie(parts + [x_in[1][2]])
     part = parts[0] + parts[1] + parts[2] + parts[3]
-    part = jnp.concatenate([part[:256], part[512:]]) + other_device(part[256:], OTHER_CORE)
     kept = jnp.concatenate([part[:BLK], part[256:]])
     sent = part[BLK:]
     bases = (0, 1, 2, 2)
     y_in, z_out, z_in, gates = [], [], [], [[arrived], [], [], [], []]
 
     for s in range(n):
+        if s == 1:
+            sent = tie([sent], z_out[0][0])[0]
         packed = pack_y(s, tab, x_in[min(s, 2)], bases[s], sent if s == 1 else None)
         before = ([y_in[s - 1]] if s else []) + (z_in[s - 2][1:] if s > 1 else []) + gates[s]
         y_in.append(exchange_y(tie([packed], *before)[0]))

time: 404 us -> 399 us (0.988)
  waiting for transfers between devices: 193 us -> 188 us
    ppermute x12, waiting for transfers between devices: 85.9 us -> 78.2 us  [shift_z(): lax.ppermute(a, 'leaf', [(leaf_at(l, z), leaf_at(l, z + dz)) for l in ran...]
  transfers between devices with their start and end apart: 39 -> 39, of which waited for: 17 -> 21; matrix products, arithmetic and copies ran while one was open for 2% -> 3% of each run, Pallas kernels for 21% -> 20%
where the time goes in v3:
time: 399 us; the launch traced here: 396 us
  waiting for transfers between devices  188 us (47%)
  Pallas kernels  109 us (27%)
  starting transfers between devices  78.3 us (20%)
  local copies, waits for them, and re-layouts  11.8 us (3%)
  other arithmetic  7.2 us (2%)
    ppermute x17, waiting for transfers between devices, shift_x(): return lax.ppermute(a, 'front', pairs)  108 us
    ppermute x12, waiting for transfers between devices, shift_z(): lax.ppermute(a, 'leaf', [(leaf_at(l, z), leaf_at(l, z + dz)) for l in ran...  78.2 us
    pallas_call x14, Pallas kernels, call(): pl.pallas_call(kernel, out_shape=[jax.ShapeDtypeStruct(s, jnp.float32) fo...  53.2 us
    pallas_call x2, Pallas kernels, accumulate(): pl.pallas_call(kernel, out_shape=jax.ShapeDtypeStruct(tile.shape, jnp.flo...  28.6 us
    ppermute x12, starting transfers between devices, shift_z(): lax.ppermute(a, 'leaf', [(leaf_at(l, z), leaf_at(l, z + dz)) for l in ran...  25.3 us
    pallas_call x3, Pallas kernels, factors(): pl.pallas_call(kernel, out_shape=shapes, in_specs=[SMEM] + [vmem] * (2 +...  22 us
    ppermute x17, starting transfers between devices, shift_x(): return lax.ppermute(a, 'front', pairs)  21.2 us
    all_to_all x4, starting transfers between devices, exchange_y(): lax.all_to_all(a, ('leaf', 'front'), 0, 0, axis_index_groups=groups, tile...  20.8 us
  transfers between devices with their start and end apart: 39, of which 21 were waited for; matrix products, arithmetic and copies ran while one was open for 3% of the time, Pallas kernels for 20%

profile of v3, /device:TPU:0, one launch (start us, length us, event | category | flops | bytes accessed | tf_op | source)
XLA Modules:
  0.0 395.7 jit_solution(12995837255508347082)
XLA Ops:
  1.5 3.9 pack_panel.1
  5.4 5.7 %all-to-all-start = ((f32[8,6,128,128]{3,2,1,0:T(8,128)}), f32[8,6,128,128]{3,2,1,0:T(8,128)}, u32[]{:S(2)}, u32[]{:S(2)}) async-start(f32[8,6,128,128]{3,2,1,0:T(8,128)} %pack_panel.1), calls=%async_computation | async-start | bytes 6291456 | tf_op jit(solution)/shard_map/all_to_all | solution.py:513
  11.1 3.8 pack_core.3
  33.0 8.7 %collective-permute-done.1.refs_2_.refs_3_ = f32[1,2,2,2,128,128]{5,4,3,2,1,0:T(8,128)} collective-permute-done((f32[1,2,2,2,128,128]{5,4,3,2,1,0:T(8,128)}, f32[1,2,2,2,128,128]{5,4,3,2,1,0:T(8,128)}, u32[]{:S(2)}, u32[]{:S(2)}) %collective-permute-start.1) | collective-permute-done | bytes 524320 | tf_op jit(solution)/shard_map/ppermute | solution.py:449
  41.7 12.2 %collective-permute-done.2.refs_3_.refs_4_ = f32[1,2,2,2,128,128]{5,4,3,2,1,0:T(8,128)} collective-permute-done((f32[1,2,2,2,128,128]{5,4,3,2,1,0:T(8,128)}, f32[1,2,2,2,128,128]{5,4,3,2,1,0:T(8,128)}, u32[]{:S(2)}, u32[]{:S(2)}) %collective-permute-start.2) | collective-permute-done | bytes 524320 | tf_op jit(solution)/shard_map/ppermute | solution.py:449
  54.0 4.4 %pack_y.4 = f32[4,16,128,128]{3,2,1,0:T(8,128)} custom-call(s32[1024]{0:T(1024)} %concatenate.27.refs_0_.tab, f32[1,2,2,2,128,128]{5,4,3,2,1,0:T(8,128)} %get-tuple-element.59.refs_1_, f32[1,2,2,2,128,128]{5,4,3,2,1,0:T(8,128)} %collective-permute-done.1.refs_2_.refs_3_, f32[1,2,2,2,128,128]{5,4,3,2,1,0:T(8,128)} %collective-permute-done.2.refs_3_.refs_4_, ...), custom_call_target="tpu_custom_call" | custom-call | flops 1000 | bytes 65536 | tf_op jit(solution)/shard_map/pack_y/pallas_call | solution.py:54
  58.3 4.9 %all-to-all-start.1 = ((f32[4,16,128,128]{3,2,1,0:T(8,128)}), f32[4,16,128,128]{3,2,1,0:T(8,128)}, u32[]{:S(2)}, u32[]{:S(2)}) async-start(f32[4,16,128,128]{3,2,1,0:T(8,128)} %pack_y.4), calls=%async_computation.1 | async-start | bytes 8388608 | tf_op jit(solution)/shard_map/all_to_all | solution.py:457
  69.3 5.7 %panel_part.1 = (f32[4,320,256]{2,1,0:T(8,128)}, f32[4,320,256]{2,1,0:T(8,128)}) custom-call(s32[384]{0:T(512)} %pad_add_fusion.flat, f32[2048,1024]{1,0:T(8,128)} %tile.3, f32[8,6,128,128]{3,2,1,0:T(8,128)} %all-to-all-done.arrived), custom_call_target="tpu_custom_call" | custom-call | flops 1000 | bytes 65536 | tf_op jit(solution)/shard_map/panel_part/pallas_call | solution.py:287
  80.0 21.9 %collective-permute-done.8.refs_2_.refs_3_ = f32[1,2,2,2,128,128]{5,4,3,2,1,0:T(8,128)S(1)} collective-permute-done((f32[1,2,2,2,128,128]{5,4,3,2,1,0:T(8,128)S(1)}, f32[1,2,2,2,128,128]{5,4,3,2,1,0:T(8,128)S(1)}, u32[]{:S(2)}, u32[]{:S(2)}) %collective-permute-start.8) | collective-permute-done | bytes 524320 | tf_op jit(solution)/shard_map/ppermute | solution.py:449
  101.9 4.3 %collective-permute-start.12 = (f32[320,256]{1,0:T(8,128)S(1)}, f32[320,256]{1,0:T(8,128)S(1)}, u32[]{:S(2)}, u32[]{:S(2)}) collective-permute-start(f32[320,256]{1,0:T(8,128)S(1)} %get-tuple-element.75), channel_id=1, source_target_pairs={{0,4},{1,5},{2,6},{3,7},{4,0},{5,1},{6,2},{7,3},{8,12},{9,13},{10,... | collective-permute-start | bytes 983048 | tf_op jit(solution)/shard_map/ppermute | solution.py:449
  106.3 7.0 %collective-permute-done.11.refs_6_ = f32[320,256]{1,0:T(8,128)S(1)} collective-permute-done((f32[320,256]{1,0:T(8,128)S(1)}, f32[320,256]{1,0:T(8,128)S(1)}, u32[]{:S(2)}, u32[]{:S(2)}) %collective-permute-start.11) | collective-permute-done | bytes 327712 | tf_op jit(solution)/shard_map/ppermute | solution.py:449
  113.3 7.0 %collective-permute-done.12.refs_7_ = f32[320,256]{1,0:T(8,128)S(1)} collective-permute-done((f32[320,256]{1,0:T(8,128)S(1)}, f32[320,256]{1,0:T(8,128)S(1)}, u32[]{:S(2)}, u32[]{:S(2)}) %collective-permute-start.12) | collective-permute-done | bytes 327712 | tf_op jit(solution)/shard_map/ppermute | solution.py:449
  121.2 4.7 %pack_z.4 = (f32[2,8,128,128]{3,2,1,0:T(8,128)}, f32[2,8,128,128]{3,2,1,0:T(8,128)}, f32[2,8,128,128]{3,2,1,0:T(8,128)}, f32[2,8,128,128]{3,2,1,0:T(8,128)}) custom-call(s32[1024]{0:T(1024)} %concatenate.27.refs_0_.tab, f32[4,16,128,128]{3,2,1,0:T(8,128)} %all-to-all-done.1.refs_1_), custom_call_target="tpu_custom_call" | custom-call | flops 1000 | bytes 65536 | tf_op jit(solution)/shard_map/pack_z/pallas_call | solution.py:54
  125.9 4.3 %pack_y.5 = f32[4,19,128,128]{3,2,1,0:T(8,128)} custom-call(s32[1024]{0:T(1024)} %concatenate.27.refs_0_.tab, f32[1,2,2,2,128,128]{5,4,3,2,1,0:T(8,128)} %get-tuple-element.68.refs_1_, f32[1,2,2,2,128,128]{5,4,3,2,1,0:T(8,128)} %copy-done.5, f32[1,2,2,2,128,128]{5,4,3,2,1,0:T(8,128)} %copy-done.7, f32[1,2,2,2,128,128]{5,4,3,2,1,0:T(8,128)} %copy-done.6, ...), custom_call_target="tpu_custom_call" | custom-call | flops 1000 | bytes 65536 | tf_op jit(solution)/shard_map/pack_y/pallas_call | solution.py:54
  130.3 5.0 %all-to-all-start.2 = ((f32[4,19,128,128]{3,2,1,0:T(8,128)}), f32[4,19,128,128]{3,2,1,0:T(8,128)}, u32[]{:S(2)}, u32[]{:S(2)}) async-start(f32[4,19,128,128]{3,2,1,0:T(8,128)} %pack_y.5), calls=%async_computation.2 | async-start | bytes 9961472 | tf_op jit(solution)/shard_map/all_to_all | solution.py:457
  135.3 4.1 %pack_x.5 = (f32[2,2,2,2,128,128]{5,4,3,2,1,0:T(8,128)}, f32[2,2,2,2,128,128]{5,4,3,2,1,0:T(8,128)}, f32[2,2,2,2,128,128]{5,4,3,2,1,0:T(8,128)}, f32[2,2,2,2,128,128]{5,4,3,2,1,0:T(8,128)}) custom-call(s32[64]{0:T(128)} %concatenate.28.refs_0_, f32[2,128,4096]{2,1,0:T(8,128)} %bitcast.58, f32[3,8,2,128,128]{4,3,2,1,0:T(8,128)} %copy-done, ...), custom_call_target="tpu_custom_call" | custom-call | flops 1000 | bytes 65536 | tf_op jit(solution)/shard_map/pack_x/pallas_call | solution.py:54
  147.7 18.4 %collective-permute-done.18.refs_2_ = f32[2,2,2,2,128,128]{5,4,3,2,1,0:T(8,128)S(1)} collective-permute-done((f32[2,2,2,2,128,128]{5,4,3,2,1,0:T(8,128)}, f32[2,2,2,2,128,128]{5,4,3,2,1,0:T(8,128)S(1)}, u32[]{:S(2)}, u32[]{:S(2)}) %collective-permute-start.18) | collective-permute-done | bytes 1048608 | tf_op jit(solution)/shard_map/ppermute | solution.py:449
  168.3 19.9 %collective-permute-done.19.refs_3_ = f32[2,2,2,2,128,128]{5,4,3,2,1,0:T(8,128)S(1)} collective-permute-done((f32[2,2,2,2,128,128]{5,4,3,2,1,0:T(8,128)}, f32[2,2,2,2,128,128]{5,4,3,2,1,0:T(8,128)S(1)}, u32[]{:S(2)}, u32[]{:S(2)}) %collective-permute-start.19) | collective-permute-done | bytes 1048608 | tf_op jit(solution)/shard_map/ppermute | solution.py:449
  193.0 4.9 %all-to-all-start.3 = ((f32[4,16,128,128]{3,2,1,0:T(8,128)}), f32[4,16,128,128]{3,2,1,0:T(8,128)}, u32[]{:S(2)}, u32[]{:S(2)}) async-start(f32[4,16,128,128]{3,2,1,0:T(8,128)} %pack_y.6), calls=%async_computation.3 | async-start | bytes 8388608 | tf_op jit(solution)/shard_map/all_to_all | solution.py:457
  197.9 4.6 %pack_z.5 = (f32[2,8,128,128]{3,2,1,0:T(8,128)}, f32[2,8,128,128]{3,2,1,0:T(8,128)}, f32[2,8,128,128]{3,2,1,0:T(8,128)}, f32[2,8,128,128]{3,2,1,0:T(8,128)}) custom-call(s32[1024]{0:T(1024)} %concatenate.27.refs_0_.tab, f32[4,19,128,128]{3,2,1,0:T(8,128)} %all-to-all-done.2.refs_1_), custom_call_target="tpu_custom_call" | custom-call | flops 1000 | bytes 65536 | tf_op jit(solution)/shard_map/pack_z/pallas_call | solution.py:54
  203.7 4.2 %collective-permute-start.16 = (f32[2,8,128,128]{3,2,1,0:T(8,128)}, f32[2,8,128,128]{3,2,1,0:T(8,128)S(1)}, u32[]{:S(2)}, u32[]{:S(2)}) collective-permute-start(f32[2,8,128,128]{3,2,1,0:T(8,128)} %get-tuple-element.88), channel_id=1, source_target_pairs={{0,32},{16,48},{32,0},{48,16},{64,96},{80,112},{96,64},{112,80},{1... | collective-permute-start | bytes 3145736 | tf_op jit(solution)/shard_map/ppermute | solution.py:461
  216.0 8.2 %collective-permute-done.27 = f32[2,128,256]{2,1,0:T(8,128)S(1)} collective-permute-done((f32[2,128,256]{2,1,0:T(8,128)S(1)}, f32[2,128,256]{2,1,0:T(8,128)S(1)}, u32[]{:S(2)}, u32[]{:S(2)}) %collective-permute-start.27) | collective-permute-done | bytes 262176 | tf_op jit(solution)/shard_map/ppermute | solution.py:449
  232.9 21.2 %collective-permute-done.16.refs_6_ = f32[2,8,128,128]{3,2,1,0:T(8,128)S(1)} collective-permute-done((f32[2,8,128,128]{3,2,1,0:T(8,128)}, f32[2,8,128,128]{3,2,1,0:T(8,128)S(1)}, u32[]{:S(2)}, u32[]{:S(2)}) %collective-permute-start.16) | collective-permute-done | bytes 1048608 | tf_op jit(solution)/shard_map/ppermute | solution.py:461
  255.1 6.1 %all-to-all-start.4 = ((f32[4,16,128,128]{3,2,1,0:T(8,128)}), f32[4,16,128,128]{3,2,1,0:T(8,128)}, u32[]{:S(2)}, u32[]{:S(2)}) async-start(f32[4,16,128,128]{3,2,1,0:T(8,128)} %pack_y.7), calls=%async_computation.4 | async-start | bytes 8388608 | tf_op jit(solution)/shard_map/all_to_all | solution.py:457
  261.2 4.6 %pack_z.6 = (f32[2,9,128,128]{3,2,1,0:T(8,128)}, f32[2,9,128,128]{3,2,1,0:T(8,128)}, f32[2,9,128,128]{3,2,1,0:T(8,128)}, f32[2,9,128,128]{3,2,1,0:T(8,128)}) custom-call(s32[1024]{0:T(1024)} %concatenate.27.refs_0_.tab, f32[4,16,128,128]{3,2,1,0:T(8,128)} %all-to-all-done.3.refs_1_, f32[128,256]{1,0:T(8,128)} %copy-done.23), custom_call_target="tpu_custom_call" | custom-call | flops 1000 | bytes 65536 | tf_op jit(solution)/shard_map/pack_z/pallas_call | solution.py:54
  273.3 48.2 %collective-permute-done.22.refs_9_ = f32[2,9,128,128]{3,2,1,0:T(8,128)S(1)} collective-permute-done((f32[2,9,128,128]{3,2,1,0:T(8,128)}, f32[2,9,128,128]{3,2,1,0:T(8,128)S(1)}, u32[]{:S(2)}, u32[]{:S(2)}) %collective-permute-start.22) | collective-permute-done | bytes 1179680 | tf_op jit(solution)/shard_map/ppermute | solution.py:461
  336.8 7.4 %factors.3 = (bf16[1024,768]{1,0:T(8,128)(2,1)}, f32[1024,256]{1,0:T(8,128)}) custom-call(s32[1024]{0:T(1024)} %concatenate.27.refs_0_.tab, f32[2,128,128]{2,1,0:T(8,128)} %inv.5, f32[128,128]{1,0:T(8,128)} %fusion.corner, f32[4,2,128,256]{3,2,1,0:T(8,128)} %copy-done.1), custom_call_target="tpu_custom_call" | custom-call | flops 1000 | bytes 65536 | tf_op jit(solution)/shard_map/factors/pallas_call | solution.py:342
  344.2 13.2 %accumulate.1.tile = f32[2048,1024]{1,0:T(8,128)} custom-call(s32[1024]{0:T(1024)} %concatenate.27.refs_0_.tab, f32[2048,1024]{1,0:T(8,128)} %tile.3, f32[2,8,128,128]{3,2,1,0:T(8,128)} %get-tuple-element.64.refs_0_, f32[2,8,128,128]{3,2,1,0:T(8,128)} %collective-permute-done.4.refs_1_, f32[2,8,128,128]{3,2,1,0:T(8,128)} %collective-permute-done.5.refs_2_, ...), custom_call_target="tpu_custom_call" | custom-call | flops 1000 | bytes 65536 | tf_op jit(solution)/shard_map/accumulate/pallas_call | solution.py:429
  357.4 7.5 %factors.4 = (bf16[1024,768]{1,0:T(8,128)(2,1)}, f32[1024,256]{1,0:T(8,128)}) custom-call(s32[1024]{0:T(1024)} %concatenate.27.refs_0_.tab, f32[2,128,128]{2,1,0:T(8,128)} %inv.5, f32[128,128]{1,0:T(8,128)} %fusion.corner, f32[4,2,128,256]{3,2,1,0:T(8,128)} %collective-permute-done.32.refs_0_), custom_call_target="tpu_custom_call" | custom-call | flops 1000 | bytes 65536 | tf_op jit(solution)/shard_map/factors/pallas_call | solution.py:342
  366.0 7.1 %factors.5.refs_8_ = bf16[1024,768]{1,0:T(8,128)(2,1)} custom-call(s32[1024]{0:T(1024)} %concatenate.27.refs_0_.tab, f32[2,128,128]{2,1,0:T(8,128)} %inv.5, f32[128,128]{1,0:T(8,128)} %fusion.corner, f32[4,128,256]{2,1,0:T(8,128)} %copy-done.8, f32[4,128,256]{2,1,0:T(8,128)} %copy-done.19), custom_call_target="tpu_custom_call" | custom-call | flops 1000 | bytes 65536 | tf_op jit(solution)/shard_map/factors/pallas_call | solution.py:342
  373.1 6.0 %collective-permute-done.29.refs_1_ = f32[2,8,128,128]{3,2,1,0:T(8,128)S(1)} collective-permute-done((f32[2,8,128,128]{3,2,1,0:T(8,128)}, f32[2,8,128,128]{3,2,1,0:T(8,128)S(1)}, u32[]{:S(2)}, u32[]{:S(2)}) %collective-permute-start.29) | collective-permute-done | bytes 1048608 | tf_op jit(solution)/shard_map/ppermute | solution.py:461
  380.1 15.4 %final.1 = f32[2048,1024]{1,0:T(8,128)} custom-call(s32[1024]{0:T(1024)} %concatenate.27.refs_0_.tab, f32[2048,1024]{1,0:T(8,128)} %accumulate.1.tile, f32[2,8,128,128]{3,2,1,0:T(8,128)} %get-tuple-element.102.refs_0_, f32[2,8,128,128]{3,2,1,0:T(8,128)} %copy-done.18, f32[2,8,128,128]{3,2,1,0:T(8,128)} %collective-permute-done.30.refs_2_, ...), custom_call_target="tpu_custom_call" | custom-call | flops 1000 | bytes 65536 | tf_op jit(solution)/shard_map/final/pallas_call | solution.py:429
  (169 shorter events, 90.2 us)
Async XLA Ops:
  5.4 53.0 %all-to-all-start = ((f32[8,6,128,128]{3,2,1,0:T(8,128)}), f32[8,6,128,128]{3,2,1,0:T(8,128)}, u32[]{:S(2)}, u32[]{:S(2)}) async-start(f32[8,6,128,128]{3,2,1,0:T(8,128)} %pack_panel.1), calls=%async_computation | async-start | bytes 6291456 | tf_op jit(solution)/shard_map/all_to_all | solution.py:513
  14.9 49.1 %collective-permute-start.7 = (f32[3,8,2,128,128]{4,3,2,1,0:T(8,128)}, f32[3,8,2,128,128]{4,3,2,1,0:T(8,128)S(1)}, u32[]{:S(2)}, u32[]{:S(2)}) collective-permute-start(f32[3,8,2,128,128]{4,3,2,1,0:T(8,128)} %pack_core.3), channel_id=1, source_target_pairs={{0,1},{1,0},{2,3},{3,2},{4,5},{5,4},{6,7},{7,6},{8,9},{9,8},{10,11... | collective-permute-start | bytes 9437192 | tf_op jit(solution)/shard_map/ppermute | solution.py:449
  26.2 15.5 %collective-permute-start.1 = (f32[1,2,2,2,128,128]{5,4,3,2,1,0:T(8,128)}, f32[1,2,2,2,128,128]{5,4,3,2,1,0:T(8,128)}, u32[]{:S(2)}, u32[]{:S(2)}) collective-permute-start(f32[1,2,2,2,128,128]{5,4,3,2,1,0:T(8,128)} %get-tuple-element.60), channel_id=1, source_target_pairs={{0,2},{1,3},{2,4},{3,5},{4,6},{5,7},{6,0},{7,1},{8,10},{9,11},{10,... | collective-permute-start | bytes 1572872 | tf_op jit(solution)/shard_map/ppermute | solution.py:449
  27.8 26.2 %collective-permute-start.2 = (f32[1,2,2,2,128,128]{5,4,3,2,1,0:T(8,128)}, f32[1,2,2,2,128,128]{5,4,3,2,1,0:T(8,128)}, u32[]{:S(2)}, u32[]{:S(2)}) collective-permute-start(f32[1,2,2,2,128,128]{5,4,3,2,1,0:T(8,128)} %get-tuple-element.61), channel_id=1, source_target_pairs={{0,4},{1,5},{2,6},{3,7},{4,0},{5,1},{6,2},{7,3},{8,12},{9,13},{10,... | collective-permute-start | bytes 1572872 | tf_op jit(solution)/shard_map/ppermute | solution.py:449
  30.5 23.4 %collective-permute-start.3 = (f32[1,2,2,2,128,128]{5,4,3,2,1,0:T(8,128)}, f32[1,2,2,2,128,128]{5,4,3,2,1,0:T(8,128)}, u32[]{:S(2)}, u32[]{:S(2)}) collective-permute-start(f32[1,2,2,2,128,128]{5,4,3,2,1,0:T(8,128)} %get-tuple-element.62), channel_id=1, source_target_pairs={{0,6},{1,7},{2,0},{3,1},{4,2},{5,3},{6,4},{7,5},{8,14},{9,15},{10,... | collective-permute-start | bytes 1572872 | tf_op jit(solution)/shard_map/ppermute | solution.py:449
  58.3 62.8 %all-to-all-start.1 = ((f32[4,16,128,128]{3,2,1,0:T(8,128)}), f32[4,16,128,128]{3,2,1,0:T(8,128)}, u32[]{:S(2)}, u32[]{:S(2)}) async-start(f32[4,16,128,128]{3,2,1,0:T(8,128)} %pack_y.4), calls=%async_computation.1 | async-start | bytes 8388608 | tf_op jit(solution)/shard_map/all_to_all | solution.py:457
  75.1 26.8 %collective-permute-start.8 = (f32[1,2,2,2,128,128]{5,4,3,2,1,0:T(8,128)S(1)}, f32[1,2,2,2,128,128]{5,4,3,2,1,0:T(8,128)S(1)}, u32[]{:S(2)}, u32[]{:S(2)}) collective-permute-start(f32[1,2,2,2,128,128]{5,4,3,2,1,0:T(8,128)S(1)} %copy-done.27), channel_id=1, source_target_pairs={{0,2},{1,3},{2,4},{3,5},{4,6},{5,7},{6,0},{7,1},{8,10},{9,11},{10,... | collective-permute-start | bytes 1572872 | tf_op jit(solution)/shard_map/ppermute | solution.py:449
  75.3 26.6 %collective-permute-start.10 = (f32[1,2,2,2,128,128]{5,4,3,2,1,0:T(8,128)S(1)}, f32[1,2,2,2,128,128]{5,4,3,2,1,0:T(8,128)S(1)}, u32[]{:S(2)}, u32[]{:S(2)}) collective-permute-start(f32[1,2,2,2,128,128]{5,4,3,2,1,0:T(8,128)S(1)} %copy-done.26), channel_id=1, source_target_pairs={{0,6},{1,7},{2,0},{3,1},{4,2},{5,3},{6,4},{7,5},{8,14},{9,15},{10,... | collective-permute-start | bytes 1572872 | tf_op jit(solution)/shard_map/ppermute | solution.py:449
  78.4 27.9 %collective-permute-start.14 = (f32[1,2,2,2,128,128]{5,4,3,2,1,0:T(8,128)S(1)}, f32[1,2,2,2,128,128]{5,4,3,2,1,0:T(8,128)S(1)}, u32[]{:S(2)}, u32[]{:S(2)}) collective-permute-start(f32[1,2,2,2,128,128]{5,4,3,2,1,0:T(8,128)S(1)} %copy-done.25), channel_id=1, source_target_pairs={{0,4},{1,5},{2,6},{3,7},{4,0},{5,1},{6,2},{7,3},{8,12},{9,13},{10,... | collective-permute-start | bytes 1572872 | tf_op jit(solution)/shard_map/ppermute | solution.py:449
  101.9 18.4 %collective-permute-start.12 = (f32[320,256]{1,0:T(8,128)S(1)}, f32[320,256]{1,0:T(8,128)S(1)}, u32[]{:S(2)}, u32[]{:S(2)}) collective-permute-start(f32[320,256]{1,0:T(8,128)S(1)} %get-tuple-element.75), channel_id=1, source_target_pairs={{0,4},{1,5},{2,6},{3,7},{4,0},{5,1},{6,2},{7,3},{8,12},{9,13},{10,... | collective-permute-start | bytes 983048 | tf_op jit(solution)/shard_map/ppermute | solution.py:449
  106.3 14.0 %collective-permute-start.13 = (f32[320,256]{1,0:T(8,128)S(1)}, f32[320,256]{1,0:T(8,128)S(1)}, u32[]{:S(2)}, u32[]{:S(2)}) collective-permute-start(f32[320,256]{1,0:T(8,128)S(1)} %get-tuple-element.76), channel_id=1, source_target_pairs={{0,6},{1,7},{2,0},{3,1},{4,2},{5,3},{6,4},{7,5},{8,14},{9,15},{10,... | collective-permute-start | bytes 983048 | tf_op jit(solution)/shard_map/ppermute | solution.py:449
  130.3 62.7 %all-to-all-start.2 = ((f32[4,19,128,128]{3,2,1,0:T(8,128)}), f32[4,19,128,128]{3,2,1,0:T(8,128)}, u32[]{:S(2)}, u32[]{:S(2)}) async-start(f32[4,19,128,128]{3,2,1,0:T(8,128)} %pack_y.5), calls=%async_computation.2 | async-start | bytes 9961472 | tf_op jit(solution)/shard_map/all_to_all | solution.py:457
  139.5 26.6 %collective-permute-start.18 = (f32[2,2,2,2,128,128]{5,4,3,2,1,0:T(8,128)}, f32[2,2,2,2,128,128]{5,4,3,2,1,0:T(8,128)S(1)}, u32[]{:S(2)}, u32[]{:S(2)}) collective-permute-start(f32[2,2,2,2,128,128]{5,4,3,2,1,0:T(8,128)} %get-tuple-element.91), channel_id=1, source_target_pairs={{0,2},{1,3},{2,4},{3,5},{4,6},{5,7},{6,0},{7,1},{8,10},{9,11},{10,... | collective-permute-start | bytes 3145736 | tf_op jit(solution)/shard_map/ppermute | solution.py:449
  139.8 48.4 %collective-permute-start.19 = (f32[2,2,2,2,128,128]{5,4,3,2,1,0:T(8,128)}, f32[2,2,2,2,128,128]{5,4,3,2,1,0:T(8,128)S(1)}, u32[]{:S(2)}, u32[]{:S(2)}) collective-permute-start(f32[2,2,2,2,128,128]{5,4,3,2,1,0:T(8,128)} %get-tuple-element.92), channel_id=1, source_target_pairs={{0,4},{1,5},{2,6},{3,7},{4,0},{5,1},{6,2},{7,3},{8,12},{9,13},{10,... | collective-permute-start | bytes 3145736 | tf_op jit(solution)/shard_map/ppermute | solution.py:449
  142.9 45.4 %collective-permute-start.20 = (f32[2,2,2,2,128,128]{5,4,3,2,1,0:T(8,128)}, f32[2,2,2,2,128,128]{5,4,3,2,1,0:T(8,128)S(1)}, u32[]{:S(2)}, u32[]{:S(2)}) collective-permute-start(f32[2,2,2,2,128,128]{5,4,3,2,1,0:T(8,128)} %get-tuple-element.93), channel_id=1, source_target_pairs={{0,6},{1,7},{2,0},{3,1},{4,2},{5,3},{6,4},{7,5},{8,14},{9,15},{10,... | collective-permute-start | bytes 3145736 | tf_op jit(solution)/shard_map/ppermute | solution.py:449
  143.1 49.4 %collective-permute-start.4 = (f32[2,8,128,128]{3,2,1,0:T(8,128)}, f32[2,8,128,128]{3,2,1,0:T(8,128)}, u32[]{:S(2)}, u32[]{:S(2)}) collective-permute-start(f32[2,8,128,128]{3,2,1,0:T(8,128)} %get-tuple-element.65), channel_id=1, source_target_pairs={{0,16},{16,32},{32,48},{48,0},{64,80},{80,96},{96,112},{112,64},{1... | collective-permute-start | bytes 3145736 | tf_op jit(solution)/shard_map/ppermute | solution.py:461
  144.4 48.6 %collective-permute-start.5 = (f32[2,8,128,128]{3,2,1,0:T(8,128)}, f32[2,8,128,128]{3,2,1,0:T(8,128)}, u32[]{:S(2)}, u32[]{:S(2)}) collective-permute-start(f32[2,8,128,128]{3,2,1,0:T(8,128)} %get-tuple-element.66), channel_id=1, source_target_pairs={{0,32},{16,48},{32,0},{48,16},{64,96},{80,112},{96,64},{112,80},{1... | collective-permute-start | bytes 3145736 | tf_op jit(solution)/shard_map/ppermute | solution.py:461
  166.1 26.9 %collective-permute-start.6 = (f32[2,8,128,128]{3,2,1,0:T(8,128)}, f32[2,8,128,128]{3,2,1,0:T(8,128)}, u32[]{:S(2)}, u32[]{:S(2)}) collective-permute-start(f32[2,8,128,128]{3,2,1,0:T(8,128)} %get-tuple-element.67), channel_id=1, source_target_pairs={{0,48},{16,0},{32,16},{48,32},{64,112},{80,64},{96,80},{112,96},{1... | collective-permute-start | bytes 3145736 | tf_op jit(solution)/shard_map/ppermute | solution.py:461
  193.0 61.9 %all-to-all-start.3 = ((f32[4,16,128,128]{3,2,1,0:T(8,128)}), f32[4,16,128,128]{3,2,1,0:T(8,128)}, u32[]{:S(2)}, u32[]{:S(2)}) async-start(f32[4,16,128,128]{3,2,1,0:T(8,128)} %pack_y.6), calls=%async_computation.3 | async-start | bytes 8388608 | tf_op jit(solution)/shard_map/all_to_all | solution.py:457
  202.5 30.4 %collective-permute-start.15 = (f32[2,8,128,128]{3,2,1,0:T(8,128)}, f32[2,8,128,128]{3,2,1,0:T(8,128)S(1)}, u32[]{:S(2)}, u32[]{:S(2)}) collective-permute-start(f32[2,8,128,128]{3,2,1,0:T(8,128)} %get-tuple-element.87), channel_id=1, source_target_pairs={{0,16},{16,32},{32,48},{48,0},{64,80},{80,96},{96,112},{112,64},{1... | collective-permute-start | bytes 3145736 | tf_op jit(solution)/shard_map/ppermute | solution.py:461
  203.7 50.4 %collective-permute-start.16 = (f32[2,8,128,128]{3,2,1,0:T(8,128)}, f32[2,8,128,128]{3,2,1,0:T(8,128)S(1)}, u32[]{:S(2)}, u32[]{:S(2)}) collective-permute-start(f32[2,8,128,128]{3,2,1,0:T(8,128)} %get-tuple-element.88), channel_id=1, source_target_pairs={{0,32},{16,48},{32,0},{48,16},{64,96},{80,112},{96,64},{112,80},{1... | collective-permute-start | bytes 3145736 | tf_op jit(solution)/shard_map/ppermute | solution.py:461
  208.0 46.9 %collective-permute-start.17 = (f32[2,8,128,128]{3,2,1,0:T(8,128)}, f32[2,8,128,128]{3,2,1,0:T(8,128)}, u32[]{:S(2)}, u32[]{:S(2)}) collective-permute-start(f32[2,8,128,128]{3,2,1,0:T(8,128)} %get-tuple-element.89), channel_id=1, source_target_pairs={{0,48},{16,0},{32,16},{48,32},{64,112},{80,64},{96,80},{112,96},{1... | collective-permute-start | bytes 3145736 | tf_op jit(solution)/shard_map/ppermute | solution.py:461
  213.5 15.3 %collective-permute-start.26 = (f32[2,128,256]{2,1,0:T(8,128)S(1)}, f32[2,128,256]{2,1,0:T(8,128)S(1)}, u32[]{:S(2)}, u32[]{:S(2)}) collective-permute-start(f32[2,128,256]{2,1,0:T(8,128)S(1)} %get-tuple-element.134), channel_id=1, source_target_pairs={{0,2},{1,3},{2,4},{3,5},{4,6},{5,7},{6,0},{7,1},{8,10},{9,11},{10,... | collective-permute-start | bytes 786440 | tf_op jit(solution)/shard_map/ppermute | solution.py:449
  255.1 68.2 %all-to-all-start.4 = ((f32[4,16,128,128]{3,2,1,0:T(8,128)}), f32[4,16,128,128]{3,2,1,0:T(8,128)}, u32[]{:S(2)}, u32[]{:S(2)}) async-start(f32[4,16,128,128]{3,2,1,0:T(8,128)} %pack_y.7), calls=%async_computation.4 | async-start | bytes 8388608 | tf_op jit(solution)/shard_map/all_to_all | solution.py:457
  265.9 55.6 %collective-permute-start.22 = (f32[2,9,128,128]{3,2,1,0:T(8,128)}, f32[2,9,128,128]{3,2,1,0:T(8,128)S(1)}, u32[]{:S(2)}, u32[]{:S(2)}) collective-permute-start(f32[2,9,128,128]{3,2,1,0:T(8,128)} %get-tuple-element.97), channel_id=1, source_target_pairs={{0,16},{16,32},{32,48},{48,0},{64,80},{80,96},{96,112},{112,64},{1... | collective-permute-start | bytes 3538952 | tf_op jit(solution)/shard_map/ppermute | solution.py:461
  268.8 52.7 %collective-permute-start.23 = (f32[2,9,128,128]{3,2,1,0:T(8,128)}, f32[2,9,128,128]{3,2,1,0:T(8,128)S(1)}, u32[]{:S(2)}, u32[]{:S(2)}) collective-permute-start(f32[2,9,128,128]{3,2,1,0:T(8,128)} %get-tuple-element.98), channel_id=1, source_target_pairs={{0,32},{16,48},{32,0},{48,16},{64,96},{80,112},{96,64},{112,80},{1... | collective-permute-start | bytes 3538952 | tf_op jit(solution)/shard_map/ppermute | solution.py:461
  269.9 52.2 %collective-permute-start.24 = (f32[2,9,128,128]{3,2,1,0:T(8,128)}, f32[2,9,128,128]{3,2,1,0:T(8,128)S(1)}, u32[]{:S(2)}, u32[]{:S(2)}) collective-permute-start(f32[2,9,128,128]{3,2,1,0:T(8,128)} %get-tuple-element.99), channel_id=1, source_target_pairs={{0,48},{16,0},{32,16},{48,32},{64,112},{80,64},{96,80},{112,96},{1... | collective-permute-start | bytes 3538952 | tf_op jit(solution)/shard_map/ppermute | solution.py:461
  326.1 31.2 %collective-permute-start.32 = (f32[4,2,128,256]{3,2,1,0:T(8,128)S(1)}, f32[4,2,128,256]{3,2,1,0:T(8,128)}, u32[]{:S(2)}, u32[]{:S(2)}) collective-permute-start(f32[4,2,128,256]{3,2,1,0:T(8,128)S(1)} %pad_maximum_fusion.refs_0_), channel_id=1, source_target_pairs={{0,8},{1,9},{2,10},{3,11},{4,12},{5,13},{6,14},{7,15},{8,0},{9,1},... | collective-permute-start | bytes 3145736 | tf_op jit(solution)/shard_map/ppermute | solution.py:469
  329.3 49.8 %collective-permute-start.29 = (f32[2,8,128,128]{3,2,1,0:T(8,128)}, f32[2,8,128,128]{3,2,1,0:T(8,128)S(1)}, u32[]{:S(2)}, u32[]{:S(2)}) collective-permute-start(f32[2,8,128,128]{3,2,1,0:T(8,128)} %get-tuple-element.103), channel_id=1, source_target_pairs={{0,16},{16,32},{32,48},{48,0},{64,80},{80,96},{96,112},{112,64},{1... | collective-permute-start | bytes 3145736 | tf_op jit(solution)/shard_map/ppermute | solution.py:461
  331.3 47.8 %collective-permute-start.30 = (f32[2,8,128,128]{3,2,1,0:T(8,128)}, f32[2,8,128,128]{3,2,1,0:T(8,128)}, u32[]{:S(2)}, u32[]{:S(2)}) collective-permute-start(f32[2,8,128,128]{3,2,1,0:T(8,128)} %get-tuple-element.104), channel_id=1, source_target_pairs={{0,32},{16,48},{32,0},{48,16},{64,96},{80,112},{96,64},{112,80},{1... | collective-permute-start | bytes 3145736 | tf_op jit(solution)/shard_map/ppermute | solution.py:461
  333.4 46.7 %collective-permute-start.31 = (f32[2,8,128,128]{3,2,1,0:T(8,128)}, f32[2,8,128,128]{3,2,1,0:T(8,128)}, u32[]{:S(2)}, u32[]{:S(2)}) collective-permute-start(f32[2,8,128,128]{3,2,1,0:T(8,128)} %get-tuple-element.105), channel_id=1, source_target_pairs={{0,48},{16,0},{32,16},{48,32},{64,112},{80,64},{96,80},{112,96},{1... | collective-permute-start | bytes 3145736 | tf_op jit(solution)/shard_map/ppermute | solution.py:461
  334.0 31.2 %collective-permute-start.33 = (f32[4,128,256]{2,1,0:T(8,128)S(1)}, f32[4,128,256]{2,1,0:T(8,128)S(1)}, u32[]{:S(2)}, u32[]{:S(2)}) collective-permute-start(f32[4,128,256]{2,1,0:T(8,128)S(1)} %pad_maximum_fusion.1.refs_0_), channel_id=1, source_target_pairs={{0,64},{1,65},{2,66},{3,67},{4,68},{5,69},{6,70},{7,71},{8,72},{9,... | collective-permute-start | bytes 1572872 | tf_op jit(solution)/shard_map/ppermute | solution.py:469
  (35 other events, 349.2 us)

commit v4 on v3

--- a/solution.py
+++ b/solution.py
@@ -20,7 +20,7 @@
 SMEM = pl.BlockSpec(memory_space=pltpu.SMEM)
 COST = pl.CostEstimate(flops=1000, bytes_accessed=1 << 16, transcendentals=0)
 VMEM = 60 << 20
-STEP = 2
+STEP = 4
 
 
 def leaf_at(y_lo, z):

time: 399 us -> 399 us (level)
  Pallas kernels: 109 us -> 104 us
  transfers between devices with their start and end apart: 39 -> 39, of which waited for: 21 -> 17; matrix products, arithmetic and copies ran while one was open for 3% -> 3% of each run, Pallas kernels for 20% -> 19%
where the time goes in v4:
time: 399 us; the launch traced here: 392 us
  waiting for transfers between devices  188 us (47%)
  Pallas kernels  104 us (26%)
  starting transfers between devices  79.9 us (20%)
  local copies, waits for them, and re-layouts  12.6 us (3%)
  other arithmetic  7.2 us (2%)
    ppermute x17, waiting for transfers between devices, shift_x(): return lax.ppermute(a, 'front', pairs)  107 us
    ppermute x12, waiting for transfers between devices, shift_z(): lax.ppermute(a, 'leaf', [(leaf_at(l, z), leaf_at(l, z + dz)) for l in ran...  79.2 us
    pallas_call x14, Pallas kernels, call(): pl.pallas_call(kernel, out_shape=[jax.ShapeDtypeStruct(s, jnp.float32) fo...  50.8 us
    pallas_call x2, Pallas kernels, accumulate(): pl.pallas_call(kernel, out_shape=jax.ShapeDtypeStruct(tile.shape, jnp.flo...  25.3 us
    ppermute x12, starting transfers between devices, shift_z(): lax.ppermute(a, 'leaf', [(leaf_at(l, z), leaf_at(l, z + dz)) for l in ran...  24.8 us
    ppermute x17, starting transfers between devices, shift_x(): return lax.ppermute(a, 'front', pairs)  23.5 us
    pallas_call x3, Pallas kernels, factors(): pl.pallas_call(kernel, out_shape=shapes, in_specs=[SMEM] + [vmem] * (2 +...  22 us
    all_to_all x4, starting transfers between devices, exchange_y(): lax.all_to_all(a, ('leaf', 'front'), 0, 0, axis_index_groups=groups, tile...  20.5 us
  transfers between devices with their start and end apart: 39, of which 17 were waited for; matrix products, arithmetic and copies ran while one was open for 3% of the time, Pallas kernels for 19%

profile of v4, /device:TPU:0, one launch (start us, length us, event | category | flops | bytes accessed | tf_op | source)
XLA Modules:
  0.0 392.2 jit_solution(13649470918588574205)
XLA Ops:
  1.5 3.8 pack_panel.1
  5.3 4.9 %all-to-all-start = ((f32[8,6,128,128]{3,2,1,0:T(8,128)}), f32[8,6,128,128]{3,2,1,0:T(8,128)}, u32[]{:S(2)}, u32[]{:S(2)}) async-start(f32[8,6,128,128]{3,2,1,0:T(8,128)} %pack_panel.1), calls=%async_computation | async-start | bytes 6291456 | tf_op jit(solution)/shard_map/all_to_all | solution.py:513
  10.3 3.8 pack_core.3
  32.1 8.8 %collective-permute-done.1.refs_2_.refs_3_ = f32[1,2,2,2,128,128]{5,4,3,2,1,0:T(8,128)} collective-permute-done((f32[1,2,2,2,128,128]{5,4,3,2,1,0:T(8,128)}, f32[1,2,2,2,128,128]{5,4,3,2,1,0:T(8,128)}, u32[]{:S(2)}, u32[]{:S(2)}) %collective-permute-start.1) | collective-permute-done | bytes 524320 | tf_op jit(solution)/shard_map/ppermute | solution.py:449
  40.9 12.2 %collective-permute-done.2.refs_3_.refs_4_ = f32[1,2,2,2,128,128]{5,4,3,2,1,0:T(8,128)} collective-permute-done((f32[1,2,2,2,128,128]{5,4,3,2,1,0:T(8,128)}, f32[1,2,2,2,128,128]{5,4,3,2,1,0:T(8,128)}, u32[]{:S(2)}, u32[]{:S(2)}) %collective-permute-start.2) | collective-permute-done | bytes 524320 | tf_op jit(solution)/shard_map/ppermute | solution.py:449
  53.1 4.4 %pack_y.4 = f32[4,16,128,128]{3,2,1,0:T(8,128)} custom-call(s32[1024]{0:T(1024)} %concatenate.27.refs_0_.tab, f32[1,2,2,2,128,128]{5,4,3,2,1,0:T(8,128)} %get-tuple-element.59.refs_1_, f32[1,2,2,2,128,128]{5,4,3,2,1,0:T(8,128)} %collective-permute-done.1.refs_2_.refs_3_, f32[1,2,2,2,128,128]{5,4,3,2,1,0:T(8,128)} %collective-permute-done.2.refs_3_.refs_4_, ...), custom_call_target="tpu_custom_call" | custom-call | flops 1000 | bytes 65536 | tf_op jit(solution)/shard_map/pack_y/pallas_call | solution.py:54
  57.5 4.9 %all-to-all-start.1 = ((f32[4,16,128,128]{3,2,1,0:T(8,128)}), f32[4,16,128,128]{3,2,1,0:T(8,128)}, u32[]{:S(2)}, u32[]{:S(2)}) async-start(f32[4,16,128,128]{3,2,1,0:T(8,128)} %pack_y.4), calls=%async_computation.1 | async-start | bytes 8388608 | tf_op jit(solution)/shard_map/all_to_all | solution.py:457
  68.5 5.5 %panel_part.1 = (f32[4,320,256]{2,1,0:T(8,128)}, f32[4,320,256]{2,1,0:T(8,128)}) custom-call(s32[384]{0:T(512)} %pad_add_fusion.flat, f32[2048,1024]{1,0:T(8,128)} %tile.3, f32[8,6,128,128]{3,2,1,0:T(8,128)} %all-to-all-done.arrived), custom_call_target="tpu_custom_call" | custom-call | flops 1000 | bytes 65536 | tf_op jit(solution)/shard_map/panel_part/pallas_call | solution.py:287
  79.2 21.7 %collective-permute-done.8.refs_2_.refs_3_ = f32[1,2,2,2,128,128]{5,4,3,2,1,0:T(8,128)S(1)} collective-permute-done((f32[1,2,2,2,128,128]{5,4,3,2,1,0:T(8,128)S(1)}, f32[1,2,2,2,128,128]{5,4,3,2,1,0:T(8,128)S(1)}, u32[]{:S(2)}, u32[]{:S(2)}) %collective-permute-start.8) | collective-permute-done | bytes 524320 | tf_op jit(solution)/shard_map/ppermute | solution.py:449
  101.0 4.3 %collective-permute-start.12 = (f32[320,256]{1,0:T(8,128)S(1)}, f32[320,256]{1,0:T(8,128)S(1)}, u32[]{:S(2)}, u32[]{:S(2)}) collective-permute-start(f32[320,256]{1,0:T(8,128)S(1)} %get-tuple-element.75), channel_id=1, source_target_pairs={{0,4},{1,5},{2,6},{3,7},{4,0},{5,1},{6,2},{7,3},{8,12},{9,13},{10,... | collective-permute-start | bytes 983048 | tf_op jit(solution)/shard_map/ppermute | solution.py:449
  105.3 7.0 %collective-permute-done.11.refs_6_ = f32[320,256]{1,0:T(8,128)S(1)} collective-permute-done((f32[320,256]{1,0:T(8,128)S(1)}, f32[320,256]{1,0:T(8,128)S(1)}, u32[]{:S(2)}, u32[]{:S(2)}) %collective-permute-start.11) | collective-permute-done | bytes 327712 | tf_op jit(solution)/shard_map/ppermute | solution.py:449
  112.4 7.0 %collective-permute-done.12.refs_7_ = f32[320,256]{1,0:T(8,128)S(1)} collective-permute-done((f32[320,256]{1,0:T(8,128)S(1)}, f32[320,256]{1,0:T(8,128)S(1)}, u32[]{:S(2)}, u32[]{:S(2)}) %collective-permute-start.12) | collective-permute-done | bytes 327712 | tf_op jit(solution)/shard_map/ppermute | solution.py:449
  120.3 4.6 %pack_z.4 = (f32[2,8,128,128]{3,2,1,0:T(8,128)}, f32[2,8,128,128]{3,2,1,0:T(8,128)}, f32[2,8,128,128]{3,2,1,0:T(8,128)}, f32[2,8,128,128]{3,2,1,0:T(8,128)}) custom-call(s32[1024]{0:T(1024)} %concatenate.27.refs_0_.tab, f32[4,16,128,128]{3,2,1,0:T(8,128)} %all-to-all-done.1.refs_1_), custom_call_target="tpu_custom_call" | custom-call | flops 1000 | bytes 65536 | tf_op jit(solution)/shard_map/pack_z/pallas_call | solution.py:54
  124.9 4.4 %pack_y.5 = f32[4,19,128,128]{3,2,1,0:T(8,128)} custom-call(s32[1024]{0:T(1024)} %concatenate.27.refs_0_.tab, f32[1,2,2,2,128,128]{5,4,3,2,1,0:T(8,128)} %get-tuple-element.68.refs_1_, f32[1,2,2,2,128,128]{5,4,3,2,1,0:T(8,128)} %copy-done.5, f32[1,2,2,2,128,128]{5,4,3,2,1,0:T(8,128)} %copy-done.7, f32[1,2,2,2,128,128]{5,4,3,2,1,0:T(8,128)} %copy-done.6, ...), custom_call_target="tpu_custom_call" | custom-call | flops 1000 | bytes 65536 | tf_op jit(solution)/shard_map/pack_y/pallas_call | solution.py:54
  129.3 5.0 %all-to-all-start.2 = ((f32[4,19,128,128]{3,2,1,0:T(8,128)}), f32[4,19,128,128]{3,2,1,0:T(8,128)}, u32[]{:S(2)}, u32[]{:S(2)}) async-start(f32[4,19,128,128]{3,2,1,0:T(8,128)} %pack_y.5), calls=%async_computation.2 | async-start | bytes 9961472 | tf_op jit(solution)/shard_map/all_to_all | solution.py:457
  134.3 4.2 %pack_x.5 = (f32[2,2,2,2,128,128]{5,4,3,2,1,0:T(8,128)}, f32[2,2,2,2,128,128]{5,4,3,2,1,0:T(8,128)}, f32[2,2,2,2,128,128]{5,4,3,2,1,0:T(8,128)}, f32[2,2,2,2,128,128]{5,4,3,2,1,0:T(8,128)}) custom-call(s32[64]{0:T(128)} %concatenate.28.refs_0_, f32[2,128,4096]{2,1,0:T(8,128)} %bitcast.58, f32[3,8,2,128,128]{4,3,2,1,0:T(8,128)} %copy-done, ...), custom_call_target="tpu_custom_call" | custom-call | flops 1000 | bytes 65536 | tf_op jit(solution)/shard_map/pack_x/pallas_call | solution.py:54
  138.6 3.8 collective-permute-start.19
  146.8 18.1 %collective-permute-done.18.refs_2_ = f32[2,2,2,2,128,128]{5,4,3,2,1,0:T(8,128)S(1)} collective-permute-done((f32[2,2,2,2,128,128]{5,4,3,2,1,0:T(8,128)}, f32[2,2,2,2,128,128]{5,4,3,2,1,0:T(8,128)S(1)}, u32[]{:S(2)}, u32[]{:S(2)}) %collective-permute-start.18) | collective-permute-done | bytes 1048608 | tf_op jit(solution)/shard_map/ppermute | solution.py:449
  167.3 21.3 %collective-permute-done.19.refs_3_ = f32[2,2,2,2,128,128]{5,4,3,2,1,0:T(8,128)S(1)} collective-permute-done((f32[2,2,2,2,128,128]{5,4,3,2,1,0:T(8,128)}, f32[2,2,2,2,128,128]{5,4,3,2,1,0:T(8,128)S(1)}, u32[]{:S(2)}, u32[]{:S(2)}) %collective-permute-start.19) | collective-permute-done | bytes 1048608 | tf_op jit(solution)/shard_map/ppermute | solution.py:449
  192.8 5.5 %all-to-all-start.3 = ((f32[4,16,128,128]{3,2,1,0:T(8,128)}), f32[4,16,128,128]{3,2,1,0:T(8,128)}, u32[]{:S(2)}, u32[]{:S(2)}) async-start(f32[4,16,128,128]{3,2,1,0:T(8,128)} %pack_y.6), calls=%async_computation.3 | async-start | bytes 8388608 | tf_op jit(solution)/shard_map/all_to_all | solution.py:457
  215.5 7.1 %collective-permute-done.27 = f32[2,128,256]{2,1,0:T(8,128)S(1)} collective-permute-done((f32[2,128,256]{2,1,0:T(8,128)S(1)}, f32[2,128,256]{2,1,0:T(8,128)S(1)}, u32[]{:S(2)}, u32[]{:S(2)}) %collective-permute-start.27) | collective-permute-done | bytes 262176 | tf_op jit(solution)/shard_map/ppermute | solution.py:449
  231.5 22.3 %collective-permute-done.16.refs_6_ = f32[2,8,128,128]{3,2,1,0:T(8,128)S(1)} collective-permute-done((f32[2,8,128,128]{3,2,1,0:T(8,128)}, f32[2,8,128,128]{3,2,1,0:T(8,128)S(1)}, u32[]{:S(2)}, u32[]{:S(2)}) %collective-permute-start.16) | collective-permute-done | bytes 1048608 | tf_op jit(solution)/shard_map/ppermute | solution.py:461
  254.8 5.1 %all-to-all-start.4 = ((f32[4,16,128,128]{3,2,1,0:T(8,128)}), f32[4,16,128,128]{3,2,1,0:T(8,128)}, u32[]{:S(2)}, u32[]{:S(2)}) async-start(f32[4,16,128,128]{3,2,1,0:T(8,128)} %pack_y.7), calls=%async_computation.4 | async-start | bytes 8388608 | tf_op jit(solution)/shard_map/all_to_all | solution.py:457
  260.0 4.2 %pack_z.6 = (f32[2,9,128,128]{3,2,1,0:T(8,128)}, f32[2,9,128,128]{3,2,1,0:T(8,128)}, f32[2,9,128,128]{3,2,1,0:T(8,128)}, f32[2,9,128,128]{3,2,1,0:T(8,128)}) custom-call(s32[1024]{0:T(1024)} %concatenate.27.refs_0_.tab, f32[4,16,128,128]{3,2,1,0:T(8,128)} %all-to-all-done.3.refs_1_, f32[128,256]{1,0:T(8,128)} %copy-done.23), custom_call_target="tpu_custom_call" | custom-call | flops 1000 | bytes 65536 | tf_op jit(solution)/shard_map/pack_z/pallas_call | solution.py:54
  272.0 47.3 %collective-permute-done.22.refs_9_ = f32[2,9,128,128]{3,2,1,0:T(8,128)S(1)} collective-permute-done((f32[2,9,128,128]{3,2,1,0:T(8,128)}, f32[2,9,128,128]{3,2,1,0:T(8,128)S(1)}, u32[]{:S(2)}, u32[]{:S(2)}) %collective-permute-start.22) | collective-permute-done | bytes 1179680 | tf_op jit(solution)/shard_map/ppermute | solution.py:461
  324.1 4.4 %collective-permute-start.32 = (f32[4,2,128,256]{3,2,1,0:T(8,128)S(1)}, f32[4,2,128,256]{3,2,1,0:T(8,128)}, u32[]{:S(2)}, u32[]{:S(2)}) collective-permute-start(f32[4,2,128,256]{3,2,1,0:T(8,128)S(1)} %pad_maximum_fusion.refs_0_), channel_id=1, source_target_pairs={{0,8},{1,9},{2,10},{3,11},{4,12},{5,13},{6,14},{7,15},{8,0},{9,1},... | collective-permute-start | bytes 3145736 | tf_op jit(solution)/shard_map/ppermute | solution.py:469
  334.8 7.4 %factors.3 = (bf16[1024,768]{1,0:T(8,128)(2,1)}, f32[1024,256]{1,0:T(8,128)}) custom-call(s32[1024]{0:T(1024)} %concatenate.27.refs_0_.tab, f32[2,128,128]{2,1,0:T(8,128)} %inv.5, f32[128,128]{1,0:T(8,128)} %fusion.corner, f32[4,2,128,256]{3,2,1,0:T(8,128)} %copy-done.1), custom_call_target="tpu_custom_call" | custom-call | flops 1000 | bytes 65536 | tf_op jit(solution)/shard_map/factors/pallas_call | solution.py:342
  342.2 11.2 %accumulate.1.tile = f32[2048,1024]{1,0:T(8,128)} custom-call(s32[1024]{0:T(1024)} %concatenate.27.refs_0_.tab, f32[2048,1024]{1,0:T(8,128)} %tile.3, f32[2,8,128,128]{3,2,1,0:T(8,128)} %get-tuple-element.64.refs_0_, f32[2,8,128,128]{3,2,1,0:T(8,128)} %collective-permute-done.4.refs_1_, f32[2,8,128,128]{3,2,1,0:T(8,128)} %collective-permute-done.5.refs_2_, ...), custom_call_target="tpu_custom_call" | custom-call | flops 1000 | bytes 65536 | tf_op jit(solution)/shard_map/accumulate/pallas_call | solution.py:429
  353.4 7.5 %factors.4 = (bf16[1024,768]{1,0:T(8,128)(2,1)}, f32[1024,256]{1,0:T(8,128)}) custom-call(s32[1024]{0:T(1024)} %concatenate.27.refs_0_.tab, f32[2,128,128]{2,1,0:T(8,128)} %inv.5, f32[128,128]{1,0:T(8,128)} %fusion.corner, f32[4,2,128,256]{3,2,1,0:T(8,128)} %collective-permute-done.32.refs_0_), custom_call_target="tpu_custom_call" | custom-call | flops 1000 | bytes 65536 | tf_op jit(solution)/shard_map/factors/pallas_call | solution.py:342
  361.9 7.1 %factors.5.refs_8_ = bf16[1024,768]{1,0:T(8,128)(2,1)} custom-call(s32[1024]{0:T(1024)} %concatenate.27.refs_0_.tab, f32[2,128,128]{2,1,0:T(8,128)} %inv.5, f32[128,128]{1,0:T(8,128)} %fusion.corner, f32[4,128,256]{2,1,0:T(8,128)} %copy-done.8, f32[4,128,256]{2,1,0:T(8,128)} %copy-done.19), custom_call_target="tpu_custom_call" | custom-call | flops 1000 | bytes 65536 | tf_op jit(solution)/shard_map/factors/pallas_call | solution.py:342
  368.9 9.0 %collective-permute-done.30.refs_2_ = f32[2,8,128,128]{3,2,1,0:T(8,128)} collective-permute-done((f32[2,8,128,128]{3,2,1,0:T(8,128)}, f32[2,8,128,128]{3,2,1,0:T(8,128)}, u32[]{:S(2)}, u32[]{:S(2)}) %collective-permute-start.30) | collective-permute-done | bytes 1048608 | tf_op jit(solution)/shard_map/ppermute | solution.py:461
  377.9 14.0 %final.1 = f32[2048,1024]{1,0:T(8,128)} custom-call(s32[1024]{0:T(1024)} %concatenate.27.refs_0_.tab, f32[2048,1024]{1,0:T(8,128)} %accumulate.1.tile, f32[2,8,128,128]{3,2,1,0:T(8,128)} %get-tuple-element.102.refs_0_, f32[2,8,128,128]{3,2,1,0:T(8,128)} %copy-done.18, f32[2,8,128,128]{3,2,1,0:T(8,128)} %collective-permute-done.30.refs_2_, ...), custom_call_target="tpu_custom_call" | custom-call | flops 1000 | bytes 65536 | tf_op jit(solution)/shard_map/final/pallas_call | solution.py:429
  (169 shorter events, 89.2 us)
Async XLA Ops:
  5.3 52.2 %all-to-all-start = ((f32[8,6,128,128]{3,2,1,0:T(8,128)}), f32[8,6,128,128]{3,2,1,0:T(8,128)}, u32[]{:S(2)}, u32[]{:S(2)}) async-start(f32[8,6,128,128]{3,2,1,0:T(8,128)} %pack_panel.1), calls=%async_computation | async-start | bytes 6291456 | tf_op jit(solution)/shard_map/all_to_all | solution.py:513
  14.0 49.1 %collective-permute-start.7 = (f32[3,8,2,128,128]{4,3,2,1,0:T(8,128)}, f32[3,8,2,128,128]{4,3,2,1,0:T(8,128)S(1)}, u32[]{:S(2)}, u32[]{:S(2)}) collective-permute-start(f32[3,8,2,128,128]{4,3,2,1,0:T(8,128)} %pack_core.3), channel_id=1, source_target_pairs={{0,1},{1,0},{2,3},{3,2},{4,5},{5,4},{6,7},{7,6},{8,9},{9,8},{10,11... | collective-permute-start | bytes 9437192 | tf_op jit(solution)/shard_map/ppermute | solution.py:449
  25.3 15.6 %collective-permute-start.1 = (f32[1,2,2,2,128,128]{5,4,3,2,1,0:T(8,128)}, f32[1,2,2,2,128,128]{5,4,3,2,1,0:T(8,128)}, u32[]{:S(2)}, u32[]{:S(2)}) collective-permute-start(f32[1,2,2,2,128,128]{5,4,3,2,1,0:T(8,128)} %get-tuple-element.60), channel_id=1, source_target_pairs={{0,2},{1,3},{2,4},{3,5},{4,6},{5,7},{6,0},{7,1},{8,10},{9,11},{10,... | collective-permute-start | bytes 1572872 | tf_op jit(solution)/shard_map/ppermute | solution.py:449
  26.8 26.3 %collective-permute-start.2 = (f32[1,2,2,2,128,128]{5,4,3,2,1,0:T(8,128)}, f32[1,2,2,2,128,128]{5,4,3,2,1,0:T(8,128)}, u32[]{:S(2)}, u32[]{:S(2)}) collective-permute-start(f32[1,2,2,2,128,128]{5,4,3,2,1,0:T(8,128)} %get-tuple-element.61), channel_id=1, source_target_pairs={{0,4},{1,5},{2,6},{3,7},{4,0},{5,1},{6,2},{7,3},{8,12},{9,13},{10,... | collective-permute-start | bytes 1572872 | tf_op jit(solution)/shard_map/ppermute | solution.py:449
  29.6 23.6 %collective-permute-start.3 = (f32[1,2,2,2,128,128]{5,4,3,2,1,0:T(8,128)}, f32[1,2,2,2,128,128]{5,4,3,2,1,0:T(8,128)}, u32[]{:S(2)}, u32[]{:S(2)}) collective-permute-start(f32[1,2,2,2,128,128]{5,4,3,2,1,0:T(8,128)} %get-tuple-element.62), channel_id=1, source_target_pairs={{0,6},{1,7},{2,0},{3,1},{4,2},{5,3},{6,4},{7,5},{8,14},{9,15},{10,... | collective-permute-start | bytes 1572872 | tf_op jit(solution)/shard_map/ppermute | solution.py:449
  57.5 62.7 %all-to-all-start.1 = ((f32[4,16,128,128]{3,2,1,0:T(8,128)}), f32[4,16,128,128]{3,2,1,0:T(8,128)}, u32[]{:S(2)}, u32[]{:S(2)}) async-start(f32[4,16,128,128]{3,2,1,0:T(8,128)} %pack_y.4), calls=%async_computation.1 | async-start | bytes 8388608 | tf_op jit(solution)/shard_map/all_to_all | solution.py:457
  74.1 26.8 %collective-permute-start.8 = (f32[1,2,2,2,128,128]{5,4,3,2,1,0:T(8,128)S(1)}, f32[1,2,2,2,128,128]{5,4,3,2,1,0:T(8,128)S(1)}, u32[]{:S(2)}, u32[]{:S(2)}) collective-permute-start(f32[1,2,2,2,128,128]{5,4,3,2,1,0:T(8,128)S(1)} %copy-done.27), channel_id=1, source_target_pairs={{0,2},{1,3},{2,4},{3,5},{4,6},{5,7},{6,0},{7,1},{8,10},{9,11},{10,... | collective-permute-start | bytes 1572872 | tf_op jit(solution)/shard_map/ppermute | solution.py:449
  74.2 26.7 %collective-permute-start.10 = (f32[1,2,2,2,128,128]{5,4,3,2,1,0:T(8,128)S(1)}, f32[1,2,2,2,128,128]{5,4,3,2,1,0:T(8,128)S(1)}, u32[]{:S(2)}, u32[]{:S(2)}) collective-permute-start(f32[1,2,2,2,128,128]{5,4,3,2,1,0:T(8,128)S(1)} %copy-done.26), channel_id=1, source_target_pairs={{0,6},{1,7},{2,0},{3,1},{4,2},{5,3},{6,4},{7,5},{8,14},{9,15},{10,... | collective-permute-start | bytes 1572872 | tf_op jit(solution)/shard_map/ppermute | solution.py:449
  77.4 27.9 %collective-permute-start.14 = (f32[1,2,2,2,128,128]{5,4,3,2,1,0:T(8,128)S(1)}, f32[1,2,2,2,128,128]{5,4,3,2,1,0:T(8,128)S(1)}, u32[]{:S(2)}, u32[]{:S(2)}) collective-permute-start(f32[1,2,2,2,128,128]{5,4,3,2,1,0:T(8,128)S(1)} %copy-done.25), channel_id=1, source_target_pairs={{0,4},{1,5},{2,6},{3,7},{4,0},{5,1},{6,2},{7,3},{8,12},{9,13},{10,... | collective-permute-start | bytes 1572872 | tf_op jit(solution)/shard_map/ppermute | solution.py:449
  101.0 18.4 %collective-permute-start.12 = (f32[320,256]{1,0:T(8,128)S(1)}, f32[320,256]{1,0:T(8,128)S(1)}, u32[]{:S(2)}, u32[]{:S(2)}) collective-permute-start(f32[320,256]{1,0:T(8,128)S(1)} %get-tuple-element.75), channel_id=1, source_target_pairs={{0,4},{1,5},{2,6},{3,7},{4,0},{5,1},{6,2},{7,3},{8,12},{9,13},{10,... | collective-permute-start | bytes 983048 | tf_op jit(solution)/shard_map/ppermute | solution.py:449
  105.3 14.0 %collective-permute-start.13 = (f32[320,256]{1,0:T(8,128)S(1)}, f32[320,256]{1,0:T(8,128)S(1)}, u32[]{:S(2)}, u32[]{:S(2)}) collective-permute-start(f32[320,256]{1,0:T(8,128)S(1)} %get-tuple-element.76), channel_id=1, source_target_pairs={{0,6},{1,7},{2,0},{3,1},{4,2},{5,3},{6,4},{7,5},{8,14},{9,15},{10,... | collective-permute-start | bytes 983048 | tf_op jit(solution)/shard_map/ppermute | solution.py:449
  129.3 63.6 %all-to-all-start.2 = ((f32[4,19,128,128]{3,2,1,0:T(8,128)}), f32[4,19,128,128]{3,2,1,0:T(8,128)}, u32[]{:S(2)}, u32[]{:S(2)}) async-start(f32[4,19,128,128]{3,2,1,0:T(8,128)} %pack_y.5), calls=%async_computation.2 | async-start | bytes 9961472 | tf_op jit(solution)/shard_map/all_to_all | solution.py:457
  138.5 26.4 %collective-permute-start.18 = (f32[2,2,2,2,128,128]{5,4,3,2,1,0:T(8,128)}, f32[2,2,2,2,128,128]{5,4,3,2,1,0:T(8,128)S(1)}, u32[]{:S(2)}, u32[]{:S(2)}) collective-permute-start(f32[2,2,2,2,128,128]{5,4,3,2,1,0:T(8,128)} %get-tuple-element.91), channel_id=1, source_target_pairs={{0,2},{1,3},{2,4},{3,5},{4,6},{5,7},{6,0},{7,1},{8,10},{9,11},{10,... | collective-permute-start | bytes 3145736 | tf_op jit(solution)/shard_map/ppermute | solution.py:449
  138.6 50.0 %collective-permute-start.19 = (f32[2,2,2,2,128,128]{5,4,3,2,1,0:T(8,128)}, f32[2,2,2,2,128,128]{5,4,3,2,1,0:T(8,128)S(1)}, u32[]{:S(2)}, u32[]{:S(2)}) collective-permute-start(f32[2,2,2,2,128,128]{5,4,3,2,1,0:T(8,128)} %get-tuple-element.92), channel_id=1, source_target_pairs={{0,4},{1,5},{2,6},{3,7},{4,0},{5,1},{6,2},{7,3},{8,12},{9,13},{10,... | collective-permute-start | bytes 3145736 | tf_op jit(solution)/shard_map/ppermute | solution.py:449
  142.4 46.2 %collective-permute-start.20 = (f32[2,2,2,2,128,128]{5,4,3,2,1,0:T(8,128)}, f32[2,2,2,2,128,128]{5,4,3,2,1,0:T(8,128)S(1)}, u32[]{:S(2)}, u32[]{:S(2)}) collective-permute-start(f32[2,2,2,2,128,128]{5,4,3,2,1,0:T(8,128)} %get-tuple-element.93), channel_id=1, source_target_pairs={{0,6},{1,7},{2,0},{3,1},{4,2},{5,3},{6,4},{7,5},{8,14},{9,15},{10,... | collective-permute-start | bytes 3145736 | tf_op jit(solution)/shard_map/ppermute | solution.py:449
  142.4 50.4 %collective-permute-start.4 = (f32[2,8,128,128]{3,2,1,0:T(8,128)}, f32[2,8,128,128]{3,2,1,0:T(8,128)}, u32[]{:S(2)}, u32[]{:S(2)}) collective-permute-start(f32[2,8,128,128]{3,2,1,0:T(8,128)} %get-tuple-element.65), channel_id=1, source_target_pairs={{0,16},{16,32},{32,48},{48,0},{64,80},{80,96},{96,112},{112,64},{1... | collective-permute-start | bytes 3145736 | tf_op jit(solution)/shard_map/ppermute | solution.py:461
  144.1 48.7 %collective-permute-start.5 = (f32[2,8,128,128]{3,2,1,0:T(8,128)}, f32[2,8,128,128]{3,2,1,0:T(8,128)}, u32[]{:S(2)}, u32[]{:S(2)}) collective-permute-start(f32[2,8,128,128]{3,2,1,0:T(8,128)} %get-tuple-element.66), channel_id=1, source_target_pairs={{0,32},{16,48},{32,0},{48,16},{64,96},{80,112},{96,64},{112,80},{1... | collective-permute-start | bytes 3145736 | tf_op jit(solution)/shard_map/ppermute | solution.py:461
  164.9 27.9 %collective-permute-start.6 = (f32[2,8,128,128]{3,2,1,0:T(8,128)}, f32[2,8,128,128]{3,2,1,0:T(8,128)}, u32[]{:S(2)}, u32[]{:S(2)}) collective-permute-start(f32[2,8,128,128]{3,2,1,0:T(8,128)} %get-tuple-element.67), channel_id=1, source_target_pairs={{0,48},{16,0},{32,16},{48,32},{64,112},{80,64},{96,80},{112,96},{1... | collective-permute-start | bytes 3145736 | tf_op jit(solution)/shard_map/ppermute | solution.py:461
  192.8 61.0 %all-to-all-start.3 = ((f32[4,16,128,128]{3,2,1,0:T(8,128)}), f32[4,16,128,128]{3,2,1,0:T(8,128)}, u32[]{:S(2)}, u32[]{:S(2)}) async-start(f32[4,16,128,128]{3,2,1,0:T(8,128)} %pack_y.6), calls=%async_computation.3 | async-start | bytes 8388608 | tf_op jit(solution)/shard_map/all_to_all | solution.py:457
  201.1 30.4 %collective-permute-start.15 = (f32[2,8,128,128]{3,2,1,0:T(8,128)}, f32[2,8,128,128]{3,2,1,0:T(8,128)S(1)}, u32[]{:S(2)}, u32[]{:S(2)}) collective-permute-start(f32[2,8,128,128]{3,2,1,0:T(8,128)} %get-tuple-element.87), channel_id=1, source_target_pairs={{0,16},{16,32},{32,48},{48,0},{64,80},{80,96},{96,112},{112,64},{1... | collective-permute-start | bytes 3145736 | tf_op jit(solution)/shard_map/ppermute | solution.py:461
  203.3 50.6 %collective-permute-start.16 = (f32[2,8,128,128]{3,2,1,0:T(8,128)}, f32[2,8,128,128]{3,2,1,0:T(8,128)S(1)}, u32[]{:S(2)}, u32[]{:S(2)}) collective-permute-start(f32[2,8,128,128]{3,2,1,0:T(8,128)} %get-tuple-element.88), channel_id=1, source_target_pairs={{0,32},{16,48},{32,0},{48,16},{64,96},{80,112},{96,64},{112,80},{1... | collective-permute-start | bytes 3145736 | tf_op jit(solution)/shard_map/ppermute | solution.py:461
  205.7 48.1 %collective-permute-start.17 = (f32[2,8,128,128]{3,2,1,0:T(8,128)}, f32[2,8,128,128]{3,2,1,0:T(8,128)}, u32[]{:S(2)}, u32[]{:S(2)}) collective-permute-start(f32[2,8,128,128]{3,2,1,0:T(8,128)} %get-tuple-element.89), channel_id=1, source_target_pairs={{0,48},{16,0},{32,16},{48,32},{64,112},{80,64},{96,80},{112,96},{1... | collective-permute-start | bytes 3145736 | tf_op jit(solution)/shard_map/ppermute | solution.py:461
  212.5 14.9 %collective-permute-start.26 = (f32[2,128,256]{2,1,0:T(8,128)S(1)}, f32[2,128,256]{2,1,0:T(8,128)S(1)}, u32[]{:S(2)}, u32[]{:S(2)}) collective-permute-start(f32[2,128,256]{2,1,0:T(8,128)S(1)} %get-tuple-element.134), channel_id=1, source_target_pairs={{0,2},{1,3},{2,4},{3,5},{4,6},{5,7},{6,0},{7,1},{8,10},{9,11},{10,... | collective-permute-start | bytes 786440 | tf_op jit(solution)/shard_map/ppermute | solution.py:449
  254.8 66.4 %all-to-all-start.4 = ((f32[4,16,128,128]{3,2,1,0:T(8,128)}), f32[4,16,128,128]{3,2,1,0:T(8,128)}, u32[]{:S(2)}, u32[]{:S(2)}) async-start(f32[4,16,128,128]{3,2,1,0:T(8,128)} %pack_y.7), calls=%async_computation.4 | async-start | bytes 8388608 | tf_op jit(solution)/shard_map/all_to_all | solution.py:457
  264.1 55.2 %collective-permute-start.22 = (f32[2,9,128,128]{3,2,1,0:T(8,128)}, f32[2,9,128,128]{3,2,1,0:T(8,128)S(1)}, u32[]{:S(2)}, u32[]{:S(2)}) collective-permute-start(f32[2,9,128,128]{3,2,1,0:T(8,128)} %get-tuple-element.97), channel_id=1, source_target_pairs={{0,16},{16,32},{32,48},{48,0},{64,80},{80,96},{96,112},{112,64},{1... | collective-permute-start | bytes 3538952 | tf_op jit(solution)/shard_map/ppermute | solution.py:461
  267.1 52.3 %collective-permute-start.23 = (f32[2,9,128,128]{3,2,1,0:T(8,128)}, f32[2,9,128,128]{3,2,1,0:T(8,128)S(1)}, u32[]{:S(2)}, u32[]{:S(2)}) collective-permute-start(f32[2,9,128,128]{3,2,1,0:T(8,128)} %get-tuple-element.98), channel_id=1, source_target_pairs={{0,32},{16,48},{32,0},{48,16},{64,96},{80,112},{96,64},{112,80},{1... | collective-permute-start | bytes 3538952 | tf_op jit(solution)/shard_map/ppermute | solution.py:461
  268.6 51.4 %collective-permute-start.24 = (f32[2,9,128,128]{3,2,1,0:T(8,128)}, f32[2,9,128,128]{3,2,1,0:T(8,128)S(1)}, u32[]{:S(2)}, u32[]{:S(2)}) collective-permute-start(f32[2,9,128,128]{3,2,1,0:T(8,128)} %get-tuple-element.99), channel_id=1, source_target_pairs={{0,48},{16,0},{32,16},{48,32},{64,112},{80,64},{96,80},{112,96},{1... | collective-permute-start | bytes 3538952 | tf_op jit(solution)/shard_map/ppermute | solution.py:461
  324.1 29.4 %collective-permute-start.32 = (f32[4,2,128,256]{3,2,1,0:T(8,128)S(1)}, f32[4,2,128,256]{3,2,1,0:T(8,128)}, u32[]{:S(2)}, u32[]{:S(2)}) collective-permute-start(f32[4,2,128,256]{3,2,1,0:T(8,128)S(1)} %pad_maximum_fusion.refs_0_), channel_id=1, source_target_pairs={{0,8},{1,9},{2,10},{3,11},{4,12},{5,13},{6,14},{7,15},{8,0},{9,1},... | collective-permute-start | bytes 3145736 | tf_op jit(solution)/shard_map/ppermute | solution.py:469
  328.4 40.5 %collective-permute-start.29 = (f32[2,8,128,128]{3,2,1,0:T(8,128)}, f32[2,8,128,128]{3,2,1,0:T(8,128)S(1)}, u32[]{:S(2)}, u32[]{:S(2)}) collective-permute-start(f32[2,8,128,128]{3,2,1,0:T(8,128)} %get-tuple-element.103), channel_id=1, source_target_pairs={{0,16},{16,32},{32,48},{48,0},{64,80},{80,96},{96,112},{112,64},{1... | collective-permute-start | bytes 3145736 | tf_op jit(solution)/shard_map/ppermute | solution.py:461
  328.7 49.2 %collective-permute-start.30 = (f32[2,8,128,128]{3,2,1,0:T(8,128)}, f32[2,8,128,128]{3,2,1,0:T(8,128)}, u32[]{:S(2)}, u32[]{:S(2)}) collective-permute-start(f32[2,8,128,128]{3,2,1,0:T(8,128)} %get-tuple-element.104), channel_id=1, source_target_pairs={{0,32},{16,48},{32,0},{48,16},{64,96},{80,112},{96,64},{112,80},{1... | collective-permute-start | bytes 3145736 | tf_op jit(solution)/shard_map/ppermute | solution.py:461
  332.4 45.6 %collective-permute-start.31 = (f32[2,8,128,128]{3,2,1,0:T(8,128)}, f32[2,8,128,128]{3,2,1,0:T(8,128)}, u32[]{:S(2)}, u32[]{:S(2)}) collective-permute-start(f32[2,8,128,128]{3,2,1,0:T(8,128)} %get-tuple-element.105), channel_id=1, source_target_pairs={{0,48},{16,0},{32,16},{48,32},{64,112},{80,64},{96,80},{112,96},{1... | collective-permute-start | bytes 3145736 | tf_op jit(solution)/shard_map/ppermute | solution.py:461
  332.4 28.7 %collective-permute-start.33 = (f32[4,128,256]{2,1,0:T(8,128)S(1)}, f32[4,128,256]{2,1,0:T(8,128)S(1)}, u32[]{:S(2)}, u32[]{:S(2)}) collective-permute-start(f32[4,128,256]{2,1,0:T(8,128)S(1)} %pad_maximum_fusion.1.refs_0_), channel_id=1, source_target_pairs={{0,64},{1,65},{2,66},{3,67},{4,68},{5,69},{6,70},{7,71},{8,72},{9,... | collective-permute-start | bytes 1572872 | tf_op jit(solution)/shard_map/ppermute | solution.py:469
  (35 other events, 359.9 us)
